TPU v7x, 256 devices: a whole 4x4x8 slice. The times are simulated.
256 devices in a mesh: su: 16 (over z, core), sv: 8 (over x, y_lo), nrm: 2 (over y_hi).
Axes of the slice: x: 4, y: 4 (y_hi: 2, y_lo: 2; y = y_hi * 2 + y_lo), z: 8, core: 2. Of those that a mesh axis runs over, the one named last changes fastest.
Arguments:
- primitive: float32 [5, 256, 320, 256], P(None, 'su', 'sv', 'nrm'), may hold values from -4 to 4, as said below
- adjoint_state: float32 [5, 256, 320, 256], P(None, 'su', 'sv', 'nrm'), may hold values from -0.6 to 0.6
- objective_grad: float32 [5, 256, 320, 256], P(None, 'su', 'sv', 'nrm'), may hold values from -6 to 6
- front_height: float32 [256, 320], P('su', 'sv'), may hold values from 0.8 to 1.25
- shock_state: float32 [5, 256, 320], P(None, 'su', 'sv'), may hold values from -4 to 4, as said below
- state_by_height: float32 [5, 256, 320], P(None, 'su', 'sv'), may hold values from -18 to 18
- state_by_slope: float32 [5, 256, 320], P(None, 'su', 'sv'), may hold values from -6 to 6
- fitted_flags: int32 [256, 320], P('su', 'sv'), may hold values 0 or 1
Outputs:
- adjoint_residual: float32 [5, 256, 320, 256], P(None, 'su', 'sv', 'nrm')
- slope_sensitivity: float32 [256, 320], P('su', 'sv')
Inputs may be any that keep to these rules, and one draw needn't show every extreme that they name: `primitive`: variables 0 (density) and 4 (pressure) lie in 0.5 to 2; variables 1 to 3 are velocity components. `shock_state`: variables 0 (density) and 4 (pressure) lie in 0.5 to 2; variables 1 to 3 are velocity components.
All inputs are finite; a program needn't handle non-finite values. No bound on the sum of `fitted_flags` on one device may be relied on, other than what follows from the above.
Results may differ from a plain program's by a relative error of at most 0.0003.
Values sent between devices are 32-bit elements; how exact they have to be, the bound alone decides.
No kernel may reach another device: no remote copies, remote signals or barrier semaphores. Data moves between devices by JAX's collectives and lax.ppermute only.
A program may use at most 128 MiB of HBM per device.

v0:
```python
import jax
import jax.numpy as jnp
from jax import lax
from jax.sharding import PartitionSpec as P

gamma_ratio = 1.4
damping_coef = 0.0625
stretch_rate = 2.2


def prefix(part, axis, combine, identity):
    count = lax.axis_size(axis)
    place = lax.axis_index(axis)
    ahead = count - 1 - place
    gathered = lax.all_gather(part, axis)
    state = jnp.zeros_like(part) + jnp.asarray(identity, part.dtype)

    def one(lap, state):
        source = count - 1 - lap
        return combine(state, lax.dynamic_index_in_dim(gathered, source, 0, False))

    return lax.fori_loop(0, ahead, one, state)


def extended(block, sides, width):
    for axis, dim in sides:
        count = lax.axis_size(axis)
        forward = [(i, i + 1) for i in range(count - 1)]
        backward = [(target, source) for source, target in forward]
        low = lax.ppermute(
            lax.slice_in_dim(block, block.shape[dim] - width, None, axis=dim), axis, forward
        )
        high = lax.ppermute(lax.slice_in_dim(block, 0, width, axis=dim), axis, backward)
        block = jnp.concatenate([low, block, high], axis=dim)
    return block


def spread(block, axis, source):
    block = jnp.where(lax.axis_index(axis) == source, block, jnp.zeros_like(block))
    return lax.psum(block, axis)


def thermo(state):
    speed_square = state[1] * state[1] + state[2] * state[2] + state[3] * state[3]
    kinetic = 0.5 * (gamma_ratio - 1.0) * speed_square
    enthalpy = gamma_ratio * state[4] / ((gamma_ratio - 1.0) * state[0]) + 0.5 * speed_square
    return (kinetic, enthalpy)


def line_flux(state, enthalpy):
    mass_flow = state[0] * state[3]
    return jnp.stack(
        [
            mass_flow,
            mass_flow * state[1],
            mass_flow * state[2],
            mass_flow * state[3] + state[4],
            mass_flow * enthalpy,
        ],
        0,
    )


def flux_transpose(state, kinetic, enthalpy, adjoint, direction):
    normal_speed = state[direction]
    projected = adjoint[direction]
    dotted = state[1] * adjoint[1] + state[2] * adjoint[2] + state[3] * adjoint[3]
    energy_term = adjoint[4]
    mass_row = (
        kinetic * projected
        - normal_speed * dotted
        + normal_speed * (kinetic - enthalpy) * energy_term
    )
    common = adjoint[0] + dotted + enthalpy * energy_term
    shared = projected + normal_speed * energy_term
    pieces = [mass_row]
    for component in (1, 2, 3):
        entry = normal_speed * adjoint[component] - (gamma_ratio - 1.0) * state[component] * shared
        if component == direction:
            entry = entry + common
        pieces.append(entry)
    pieces.append((gamma_ratio - 1.0) * projected + gamma_ratio * normal_speed * energy_term)
    return jnp.stack(pieces, 0)


def tangent_parts(padded_adjoint, padded_radius, along_axis, length):

    def window(source, offset):
        return lax.slice_in_dim(source, offset, offset + length, axis=along_axis)

    gradient = (
        8.0 * (window(padded_adjoint, 1) - window(padded_adjoint, 3))
        - (window(padded_adjoint, 0) - window(padded_adjoint, 4))
    ) / 12.0
    weighted = padded_radius[None] * padded_adjoint
    fourth = (
        window(weighted, 0)
        - 4.0 * window(weighted, 1)
        + 6.0 * window(weighted, 2)
        - 4.0 * window(weighted, 3)
        + window(weighted, 4)
    )
    return (gradient, fourth)


def add_totals(earlier, later):
    return earlier + later


def upstream_sum(column_totals):
    return prefix(column_totals, "su", add_totals, jnp.zeros_like(column_totals))


def local(
    primitive,
    adjoint_state,
    objective_grad,
    front_height,
    shock_state,
    state_by_height,
    state_by_slope,
    fitted_flags,
):
    row_count = adjoint_state.shape[1]
    column_count = adjoint_state.shape[2]
    line_depth = adjoint_state.shape[3]
    line_count = lax.axis_size("nrm")
    line_index = lax.axis_index("nrm")
    total_depth = line_depth * line_count
    position = (line_index * line_depth + jnp.arange(line_depth, dtype=jnp.int32)).astype(
        jnp.float32
    ) + 0.5
    fraction = position / total_depth
    stretch = jnp.exp(stretch_rate * (fraction - 1.0))
    kinetic, enthalpy = thermo(primitive)
    sound_speed = jnp.sqrt(gamma_ratio * primitive[4] / primitive[0])
    radius_first = jnp.abs(primitive[1]) + sound_speed
    radius_second = jnp.abs(primitive[2]) + sound_speed
    stacked = jnp.concatenate([adjoint_state, radius_first[None], radius_second[None]], 0)
    padded = extended(stacked, (("su", 1), ("sv", 2)), 2)
    first_pad = padded[:, :, 2 : column_count + 2]
    second_pad = padded[:, 2 : row_count + 2]
    first_grad, first_fourth = tangent_parts(first_pad[:5], first_pad[5], 1, row_count)
    second_grad, second_fourth = tangent_parts(second_pad[:5], second_pad[6], 2, column_count)
    scaled = adjoint_state / (2.0 * front_height[None, :, :, None] * stretch[None, None, None, :])
    fluxes = line_flux(primitive, enthalpy)
    line_pad = extended(jnp.concatenate([scaled, fluxes], 0), (("nrm", 3),), 1)
    on_front = line_index == line_count - 1
    shock_kinetic, shock_enthalpy = thermo(shock_state)
    shock_flux = line_flux(shock_state, shock_enthalpy)
    top_flux = jnp.where(on_front, shock_flux, line_pad[5:, :, :, line_depth + 1])
    flux_above = jnp.concatenate([line_pad[5:, :, :, 2 : line_depth + 1], top_flux[..., None]], -1)
    flux_below = line_pad[5:, :, :, 0:line_depth]
    metric_part = -jnp.sum(scaled * (flux_above - flux_below), axis=(0, 3)) / front_height
    normal_term = flux_transpose(
        primitive,
        kinetic,
        enthalpy,
        line_pad[:5, :, :, 0:line_depth] - line_pad[:5, :, :, 2 : line_depth + 2],
        3,
    )
    top_scaled = scaled[..., line_depth - 1]
    metric = lax.psum(metric_part, "nrm")
    shock_adjoint = flux_transpose(shock_state, shock_kinetic, shock_enthalpy, top_scaled, 3)
    fitted = fitted_flags.astype(jnp.float32)
    height_term = metric + fitted * jnp.sum(shock_adjoint * state_by_height, 0)
    local_total = lax.cumsum(height_term, axis=0, reverse=True)
    upstream = upstream_sum(local_total[0])
    surface_count = row_count * lax.axis_size("su")
    slope_sens = (local_total + upstream[None, :]) / surface_count + fitted * jnp.sum(
        shock_adjoint * state_by_slope, 0
    )
    slope_sens = spread(slope_sens, "nrm", line_count - 1)
    result = (
        objective_grad
        + flux_transpose(primitive, kinetic, enthalpy, first_grad, 1)
        + flux_transpose(primitive, kinetic, enthalpy, second_grad, 2)
        + damping_coef * (first_fourth + second_fourth)
        + normal_term
        + fraction[None, None, None, :] * slope_sens[None, :, :, None] * fluxes
    )
    return (result, slope_sens)


def solution(mesh):
    placed = (
        P(None, "su", "sv", "nrm"),
        P(None, "su", "sv", "nrm"),
        P(None, "su", "sv", "nrm"),
        P("su", "sv"),
        P(None, "su", "sv"),
        P(None, "su", "sv"),
        P(None, "su", "sv"),
        P("su", "sv"),
    )
    return jax.shard_map(
        local,
        mesh=mesh,
        in_specs=placed,
        out_specs=(P(None, "su", "sv", "nrm"), P("su", "sv")),
        check_vma=False,
    )
```

profile of v0, /device:TPU:22, one launch (start us, length us, event | category | flops | bytes accessed | tf_op | source)
XLA Modules:
  0.0 119.2 jit_solution(15050058700215018982)
XLA Ops:
  1.5 1.1 constant_dynamic-update-slice_fusion.4
  3.1 1.6 %copy-done.1 = f32[5,16,40,128]{3,2,1,0:T(8,128)S(1)} copy-done((f32[5,16,40,128]{3,2,1,0:T(8,128)S(1)}, f32[5,16,40,128]{3,2,1,0:T(8,128)}, u32[]{:S(2)}) %copy-start.1) | copy-done | bytes 1638424
  5.0 0.8 pad_maximum_fusion.25
  5.8 2.6 %collective-permute-start = (f32[7,2,40,128]{3,2,1,0:T(8,128)}, f32[7,2,40,128]{3,2,1,0:T(8,128)}, u32[]{:S(2)}, u32[]{:S(2)}) collective-permute-start(f32[7,2,40,128]{3,2,1,0:T(8,128)} %get-tuple-element.114), channel_id=1, source_target_pairs={{0,16},{16,32},{32,48},{48,64},{64,80},{80,96},{96,112},{112,128},... | collective-permute-start | bytes 860168 | tf_op jit(solution)/shard_map/ppermute | solution.py:30
  8.4 1.3 %collective-permute-start.1 = (f32[7,2,40,128]{3,2,1,0:T(8,128)}, f32[7,2,40,128]{3,2,1,0:T(8,128)}, u32[]{:S(2)}, u32[]{:S(2)}) collective-permute-start(f32[7,2,40,128]{3,2,1,0:T(8,128)} %get-tuple-element.115), channel_id=1, source_target_pairs={{16,0},{32,16},{48,32},{64,48},{80,64},{96,80},{112,96},{128,112},... | collective-permute-start | bytes 860168 | tf_op jit(solution)/shard_map/ppermute | solution.py:33
  10.4 0.9 slice_reduce_fusion
  12.2 1.1 collective-permute-done.1
  13.2 1.8 %maximum_maximum_fusion = (f32[7,18,40,128]{3,2,1,0:T(8,128)S(1)}, f32[7,18,40,128]{3,2,1,0:T(8,128)S(1)}) fusion(f32[1,16,40,128]{3,2,1,0:T(8,128)} %copy-done.6, f32[1,16,40,128]{3,2,1,0:T(8,128)} %copy-done.9, f32[5,16,40,128]{3,2,1,0:T(8,128)S(1)} %copy-done, f32[7,2,40,128]{3,2,1,0:T(8,128)} %collective-permute-done, ...), kind=kLoop, calls=%fused_computation.1 | loop fusion | flops 3870720 | bytes 8028160 | tf_op jit(solution)/shard_map/concatenate | solution.py:34
  15.4 2.2 %copy-done.4 = f32[10,16,40,128]{3,2,1,0:T(8,128)S(1)} copy-done((f32[10,16,40,128]{3,2,1,0:T(8,128)S(1)}, f32[10,16,40,128]{3,2,1,0:T(8,128)}, u32[]{:S(2)}) %copy-start.4) | copy-done | bytes 3276824
  17.6 1.2 %constant_dynamic-update-slice_fusion.3 = (f32[5,16,40,128]{3,2,1,0:T(8,128)}, f32[10,16,40,128]{3,2,1,0:T(8,128)S(1)}, f32[5,16,40,128]{3,2,1,0:T(8,128)}, f32[...) fusion(f32[5,16,40,128]{3,2,1,0:T(8,128)} %copy-done.20, ...), kind=kLoop, calls=%fused_computation.125 | loop fusion | flops 2129919 | bytes 5242880
  19.7 3.9 %fusion.44 = (f32[10,16,40,1]{3,2,1,0:T(8,128)}, f32[10,16,40,1]{3,2,1,0:T(8,128)}) fusion(f32[10,16,40,128]{3,2,1,0:T(8,128)S(1)} %get-tuple-element.130), kind=kLoop, calls=%fused_computation.172 | loop fusion | bytes 102400 | tf_op jit(solution)/shard_map/slice | solution.py:31
  23.6 3.3 %copy.401 = f32[10,16,40,1]{2,1,3,0:T(8,128)} copy(f32[10,16,40,1]{3,2,1,0:T(8,128)} %get-tuple-element.106) | data formatting | bytes 51200 | tf_op jit(solution)/shard_map/slice | solution.py:31
  26.9 1.3 %collective-permute-start.4 = (f32[10,16,40,1]{2,1,3,0:T(8,128)}, f32[10,16,40,1]{2,1,3,0:T(8,128)}, u32[]{:S(2)}, u32[]{:S(2)}) collective-permute-start(f32[10,16,40,1]{2,1,3,0:T(8,128)} %copy.401), channel_id=1, source_target_pairs={{0,1},{2,3},{4,5},{6,7},{8,9},{10,11},{12,13},{14,15},{16,17},{18,... | collective-permute-start | bytes 76808 | tf_op jit(solution)/shard_map/ppermute | solution.py:30
  28.2 3.3 %copy.403 = f32[10,16,40,1]{2,1,3,0:T(8,128)} copy(f32[10,16,40,1]{3,2,1,0:T(8,128)} %get-tuple-element.107) | data formatting | bytes 51200 | tf_op jit(solution)/shard_map/slice | solution.py:33
  31.5 6.8 %collective-permute-start.5 = (f32[10,16,40,1]{2,1,3,0:T(8,128)}, f32[10,16,40,1]{2,1,3,0:T(8,128)S(1)}, u32[]{:S(2)}, u32[]{:S(2)}) collective-permute-start(f32[10,16,40,1]{2,1,3,0:T(8,128)} %copy.403), channel_id=1, source_target_pairs={{1,0},{3,2},{5,4},{7,6},{9,8},{11,10},{13,12},{15,14},{17,16},{19,... | collective-permute-start | bytes 76808 | tf_op jit(solution)/shard_map/ppermute | solution.py:33
  38.3 1.9 %pad_maximum_fusion.27 = (f32[7,20,2,128]{3,2,1,0:T(2,128)}, f32[7,20,2,128]{3,2,1,0:T(2,128)}) fusion(f32[7,2,40,128]{3,2,1,0:T(8,128)} %collective-permute-done.1, f32[7,2,40,128]{3,2,1,0:T(8,128)} %collective-permute-done, f32[1,16,40,128]{3,2,1,0:T(8,128)} %copy-done.6, f32[1,16,40,128]{3,2,1,0:T(8,128)} %copy-done.9, f32[5,16,40,128]{3,2,1,0:T(8,128)S(1)} %copy-done), kind=kLoop, calls=%fused_computation.121 | loop fusion | flops 286720 | bytes 3153920 | tf_op jit(solution)/shard_map/slice | solution.py:31
  40.2 3.2 %collective-permute-start.2 = (f32[7,20,2,128]{3,2,1,0:T(2,128)}, f32[7,20,2,128]{3,2,1,0:T(2,128)S(1)}, u32[]{:S(2)}, u32[]{:S(2)}) collective-permute-start(f32[7,20,2,128]{3,2,1,0:T(2,128)} %get-tuple-element.108), channel_id=1, source_target_pairs={{0,2},{2,4},{4,6},{6,8},{8,10},{10,12},{12,14},{1,3},{3,5},{5,7},{... | collective-permute-start | bytes 430088 | tf_op jit(solution)/shard_map/ppermute | solution.py:30
  43.3 3.6 %collective-permute-start.3 = (f32[7,20,2,128]{3,2,1,0:T(2,128)}, f32[7,20,2,128]{3,2,1,0:T(2,128)}, u32[]{:S(2)}, u32[]{:S(2)}) collective-permute-start(f32[7,20,2,128]{3,2,1,0:T(2,128)} %get-tuple-element.109), channel_id=1, source_target_pairs={{2,0},{4,2},{6,4},{8,6},{10,8},{12,10},{14,12},{3,1},{5,3},{7,5},{... | collective-permute-start | bytes 430088 | tf_op jit(solution)/shard_map/ppermute | solution.py:33
  46.9 0.8 maximum_bitcast_fusion
  47.8 2.6 %fusion = f32[5,20,40,128]{3,2,1,0:T(8,128)} fusion(f32[7,2,40,128]{3,2,1,0:T(8,128)} %collective-permute-done.1, f32[7,2,40,128]{3,2,1,0:T(8,128)} %collective-permute-done, f32[1,16,40,128]{3,2,1,0:T(8,128)S(1)} %copy-done.7, f32[1,16,40,128]{3,2,1,0:T(8,128)S(1)} %copy-done.10, f32[5,16,40,128]{3,2,1,0:T(8,128)S(1)} %copy-done, ...), kind=kLoop, calls=%fused_computation.4 | loop fusion | flops 2560000 | bytes 5324800 | tf_op jit(solution)/shard_map/mul | solution.py:95
  50.4 1.7 %slice.386 = f32[5,16,40,127]{3,2,1,0:T(8,128)} slice(f32[5,16,40,128]{3,2,1,0:T(8,128)S(1)} %copy-done.21), slice={[0:5], [0:16], [0:40], [1:128]} | slice | bytes 3251200 | tf_op jit(solution)/shard_map/slice | solution.py:152
  52.1 1.8 %copy.406 = f32[5,16,40,1]{3,2,1,0:T(8,128)} copy(f32[5,16,40,1]{2,1,3,0:T(8,128)S(1)} %slice_select_fusion) | data formatting | bytes 25600 | tf_op jit(solution)/shard_map/jit(_where)/select_n | solution.py:151
  53.9 2.5 %copy.404 = f32[10,16,40,1]{3,2,1,0:T(8,128)} copy(f32[10,16,40,1]{2,1,3,0:T(8,128)S(1)} %collective-permute-done.5) | data formatting | bytes 51200 | tf_op jit(solution)/shard_map/ppermute | solution.py:33
  56.3 3.3 %copy.402 = f32[10,16,40,1]{3,2,1,0:T(8,128)} copy(f32[10,16,40,1]{2,1,3,0:T(8,128)} %collective-permute-done.4) | data formatting | bytes 51200 | tf_op jit(solution)/shard_map/ppermute | solution.py:30
  59.6 8.6 %fusion.4 = (f32[16,40]{1,0:T(8,128)S(1)}, f32[5,16,40,128]{3,2,1,0:T(8,128)}) fusion(f32[5,16,40,128]{3,2,1,0:T(8,128)} %copy-done.17, f32[10,16,40,128]{3,2,1,0:T(8,128)} %copy-done.5, f32[10,16,40,1]{3,2,1,0:T(8,128)} %copy.402, f32[5,16,40,1]{3,2,1,0:T(8,128)} %copy.406, f32[5,16,40,127]{3,2,1,0:T(8,128)} %slice.386, f32[10,16,40,1]{3,2,1,0:T(8,128)} %copy.404), kind=kLoop, calls=%fused_computation.18 | loop fusion | flops 3276160 | bytes 8245760 | tf_op jit(solution)/shard_map/reduce_sum | solution.py:154
  68.3 6.5 %psum.14 = f32[16,40]{1,0:T(8,128)S(1)} all-reduce(f32[16,40]{1,0:T(8,128)S(1)} %negate_divide_fusion), channel_id=1, replica_groups=mesh['su'=16,'sv'=8,'nrm'=2] {'nrm'}, use_global_device_ids=true, to_apply=%region_1.2 | all-reduce | flops 640 | bytes 5120 | tf_op jit(solution)/shard_map/psum | solution.py:163
  74.9 22.6 %all-gather = f32[16,1,40]{2,1,0:T(1,128)S(1)} all-gather(f32[1,1,40]{2,1,0:T(1,128)S(1)} %slice_bitcast_fusion), channel_id=1, replica_groups=mesh['su'=16,'sv'=8,'nrm'=2] {'su'}, dimensions={0}, use_global_device_ids=true | all-gather | bytes 2720 | tf_op jit(solution)/shard_map/all_gather | solution.py:15
  98.2 6.5 %psum.15 = f32[16,40]{1,0:T(8,128)S(1)} all-reduce(f32[16,40]{1,0:T(8,128)S(1)} %add_select_fusion), channel_id=1, replica_groups=mesh['su'=16,'sv'=8,'nrm'=2] {'nrm'}, use_global_device_ids=true, to_apply=%region_7.8 | all-reduce | flops 640 | bytes 5120 | tf_op jit(solution)/shard_map/psum | solution.py:40
  104.9 3.9 %fusion.19 = f32[5,16,40,128]{3,2,1,0:T(8,128)S(1)} fusion(f32[7,20,2,128]{3,2,1,0:T(2,128)} %collective-permute-done.3, f32[7,2,40,128]{3,2,1,0:T(8,128)} %collective-permute-done.1, f32[7,2,40,128]{3,2,1,0:T(8,128)} %collective-permute-done, f32[1,16,40,128]{3,2,1,0:T(8,128)} %copy-done.6, f32[1,16,40,128]{3,2,1,0:T(8,128)} %copy-done.9, ...), kind=kLoop, calls=%fused_computation.43 | loop fusion | flops 10240000 | bytes 4792320 | tf_op jit(solution)/shard_map/div | solution.py:91
  109.4 1.2 %copy-done.14 = f32[5,16,40,128]{3,2,1,0:T(8,128)S(1)} copy-done((f32[5,16,40,128]{3,2,1,0:T(8,128)S(1)}, f32[5,16,40,128]{3,2,1,0:T(8,128)}, u32[]{:S(2)}) %copy-start.14) | copy-done | bytes 1638424
  113.9 1.3 %fusion.1 = f32[5,16,44,128]{3,2,1,0:T(8,128)S(1)} fusion(f32[7,20,2,128]{3,2,1,0:T(2,128)} %collective-permute-done.3, f32[7,20,2,128]{3,2,1,0:T(2,128)S(1)} %collective-permute-done.2, f32[7,2,40,128]{3,2,1,0:T(8,128)} %collective-permute-done.1, f32[7,2,40,128]{3,2,1,0:T(8,128)} %collective-permute-done, f32[1,16,40,128]{3,2,1,0:T(8,128)S(1)} %copy-done.8, ...), kind=kLoop, calls=%fused_computation.9 | loop fusion | flops 3153920 | bytes 5316608 | tf_op jit(solution)/shard_map/mul | solution.py:95
  116.4 2.7 %fusion.10 = f32[5,16,40,128]{3,2,1,0:T(8,128)} fusion(f32[5,16,40,128]{3,2,1,0:T(8,128)S(1)} %get-tuple-element.121, f32[5,16,44,128]{3,2,1,0:T(8,128)S(1)} %fusion.1, f32[5,20,40,128]{3,2,1,0:T(8,128)S(1)} %copy-done.2, f32[5,16,40,128]{3,2,1,0:T(8,128)S(1)} %copy-done.22, f32[5,16,40,128]{3,2,1,0:T(8,128)S(1)} %add_dynamic-update-slice_fusion.2, ...), kind=kLoop, calls=%fused_computation.26 | loop fusion | flops 9011200 | bytes 26542080 | tf_op jit(solution)/shard_map/add | solution.py:175
  (131 shorter events, 10.2 us)
Async XLA Ops:
  0.6 2.1 %copy-start = (f32[5,16,40,128]{3,2,1,0:T(8,128)S(1)}, f32[5,16,40,128]{3,2,1,0:T(8,128)}, u32[]{:S(2)}) copy-start(f32[5,16,40,128]{3,2,1,0:T(8,128)} %param.11) | copy-start | bytes 4915204
  2.6 2.2 %copy-start.15 = (f32[1,16,40,128]{3,2,1,0:T(8,128)}, f32[1,16,40,128]{3,2,1,0:T(8,128)S(1)}, u32[]{:S(2)}) copy-start(f32[1,16,40,128]{3,2,1,0:T(8,128)S(1)} %get-tuple-element.97) | copy-start | bytes 983044
  3.1 7.4 %copy-start.17 = (f32[5,16,40,128]{3,2,1,0:T(8,128)}, f32[5,16,40,128]{3,2,1,0:T(8,128)S(1)}, u32[]{:S(2)}) copy-start(f32[5,16,40,128]{3,2,1,0:T(8,128)S(1)} %get-tuple-element.103) | copy-start | bytes 4915204
  4.9 6.4 %copy-start.3 = (f32[10,16,40,128]{3,2,1,0:T(8,128)}, f32[10,16,40,128]{3,2,1,0:T(8,128)S(1)}, u32[]{:S(2)}) copy-start(f32[10,16,40,128]{3,2,1,0:T(8,128)S(1)} %get-tuple-element.131) | copy-start | bytes 9830404
  5.0 6.4 %copy-start.6 = (f32[1,16,40,128]{3,2,1,0:T(8,128)}, f32[1,16,40,128]{3,2,1,0:T(8,128)S(1)}, u32[]{:S(2)}) copy-start(f32[1,16,40,128]{3,2,1,0:T(8,128)S(1)} %get-tuple-element.127) | copy-start | bytes 983044
  5.0 6.4 %copy-start.9 = (f32[1,16,40,128]{3,2,1,0:T(8,128)}, f32[1,16,40,128]{3,2,1,0:T(8,128)S(1)}, u32[]{:S(2)}) copy-start(f32[1,16,40,128]{3,2,1,0:T(8,128)S(1)} %get-tuple-element.128) | copy-start | bytes 983044
  5.0 6.4 %copy-start.20 = (f32[5,16,40,128]{3,2,1,0:T(8,128)}, f32[5,16,40,128]{3,2,1,0:T(8,128)S(1)}, u32[]{:S(2)}) copy-start(f32[5,16,40,128]{3,2,1,0:T(8,128)S(1)} %get-tuple-element.126) | copy-start | bytes 4915204
  5.0 4.8 %copy-start.27 = (f32[5,16,40]{2,1,0:T(8,128)S(1)}, f32[5,16,40]{2,1,0:T(8,128)}, u32[]{:S(2)}) copy-start(f32[5,16,40]{2,1,0:T(8,128)} %param.14) | copy-start | bytes 38404
  5.8 5.7 %copy-start.30 = (f32[5,16,40]{2,1,0:T(8,128)S(1)}, f32[5,16,40]{2,1,0:T(8,128)}, u32[]{:S(2)}) copy-start(f32[5,16,40]{2,1,0:T(8,128)} %param.15) | copy-start | bytes 38404
  5.8 5.7 %copy-start.31 = (f32[5,16,40]{2,1,0:T(8,128)S(1)}, f32[5,16,40]{2,1,0:T(8,128)}, u32[]{:S(2)}) copy-start(f32[5,16,40]{2,1,0:T(8,128)} %param.16) | copy-start | bytes 38404
  5.8 6.3 %collective-permute-start = (f32[7,2,40,128]{3,2,1,0:T(8,128)}, f32[7,2,40,128]{3,2,1,0:T(8,128)}, u32[]{:S(2)}, u32[]{:S(2)}) collective-permute-start(f32[7,2,40,128]{3,2,1,0:T(8,128)} %get-tuple-element.114), channel_id=1, source_target_pairs={{0,16},{16,32},{32,48},{48,64},{64,80},{80,96},{96,112},{112,128},... | collective-permute-start | bytes 860168 | tf_op jit(solution)/shard_map/ppermute | solution.py:30
  8.4 4.8 %collective-permute-start.1 = (f32[7,2,40,128]{3,2,1,0:T(8,128)}, f32[7,2,40,128]{3,2,1,0:T(8,128)}, u32[]{:S(2)}, u32[]{:S(2)}) collective-permute-start(f32[7,2,40,128]{3,2,1,0:T(8,128)} %get-tuple-element.115), channel_id=1, source_target_pairs={{16,0},{32,16},{48,32},{64,48},{80,64},{96,80},{112,96},{128,112},... | collective-permute-start | bytes 860168 | tf_op jit(solution)/shard_map/ppermute | solution.py:33
  15.0 2.5 %copy-start.4 = (f32[10,16,40,128]{3,2,1,0:T(8,128)S(1)}, f32[10,16,40,128]{3,2,1,0:T(8,128)}, u32[]{:S(2)}) copy-start(f32[10,16,40,128]{3,2,1,0:T(8,128)} %copy-done.3) | copy-start | bytes 9830404
  15.0 2.5 %copy-start.16 = (f32[1,16,40,128]{3,2,1,0:T(8,128)S(1)}, f32[1,16,40,128]{3,2,1,0:T(8,128)}, u32[]{:S(2)}) copy-start(f32[1,16,40,128]{3,2,1,0:T(8,128)} %copy-done.15) | copy-start | bytes 983044
  15.3 3.5 %copy-start.13 = (f32[5,16,40,128]{3,2,1,0:T(8,128)}, f32[5,16,40,128]{3,2,1,0:T(8,128)S(1)}, u32[]{:S(2)}) copy-start(f32[5,16,40,128]{3,2,1,0:T(8,128)S(1)} %fusion.22) | copy-start | bytes 4915204
  19.7 3.9 %copy-start.5 = (f32[10,16,40,128]{3,2,1,0:T(8,128)}, f32[10,16,40,128]{3,2,1,0:T(8,128)S(1)}, u32[]{:S(2)}) copy-start(f32[10,16,40,128]{3,2,1,0:T(8,128)S(1)} %get-tuple-element.130) | copy-start | bytes 9830404
  26.9 29.5 %collective-permute-start.4 = (f32[10,16,40,1]{2,1,3,0:T(8,128)}, f32[10,16,40,1]{2,1,3,0:T(8,128)}, u32[]{:S(2)}, u32[]{:S(2)}) collective-permute-start(f32[10,16,40,1]{2,1,3,0:T(8,128)} %copy.401), channel_id=1, source_target_pairs={{0,1},{2,3},{4,5},{6,7},{8,9},{10,11},{12,13},{14,15},{16,17},{18,... | collective-permute-start | bytes 76808 | tf_op jit(solution)/shard_map/ppermute | solution.py:30
  31.4 15.5 %copy-start.7 = (f32[1,16,40,128]{3,2,1,0:T(8,128)S(1)}, f32[1,16,40,128]{3,2,1,0:T(8,128)}, u32[]{:S(2)}) copy-start(f32[1,16,40,128]{3,2,1,0:T(8,128)} %copy-done.6) | copy-start | bytes 983044
  31.5 15.5 %copy-start.10 = (f32[1,16,40,128]{3,2,1,0:T(8,128)S(1)}, f32[1,16,40,128]{3,2,1,0:T(8,128)}, u32[]{:S(2)}) copy-start(f32[1,16,40,128]{3,2,1,0:T(8,128)} %copy-done.9) | copy-start | bytes 983044
  31.5 20.6 %collective-permute-start.5 = (f32[10,16,40,1]{2,1,3,0:T(8,128)}, f32[10,16,40,1]{2,1,3,0:T(8,128)S(1)}, u32[]{:S(2)}, u32[]{:S(2)}) collective-permute-start(f32[10,16,40,1]{2,1,3,0:T(8,128)} %copy.403), channel_id=1, source_target_pairs={{1,0},{3,2},{5,4},{7,6},{9,8},{11,10},{13,12},{15,14},{17,16},{19,... | collective-permute-start | bytes 76808 | tf_op jit(solution)/shard_map/ppermute | solution.py:33
  40.2 64.7 %collective-permute-start.2 = (f32[7,20,2,128]{3,2,1,0:T(2,128)}, f32[7,20,2,128]{3,2,1,0:T(2,128)S(1)}, u32[]{:S(2)}, u32[]{:S(2)}) collective-permute-start(f32[7,20,2,128]{3,2,1,0:T(2,128)} %get-tuple-element.108), channel_id=1, source_target_pairs={{0,2},{2,4},{4,6},{6,8},{8,10},{10,12},{12,14},{1,3},{3,5},{5,7},{... | collective-permute-start | bytes 430088 | tf_op jit(solution)/shard_map/ppermute | solution.py:30
  43.3 61.5 %collective-permute-start.3 = (f32[7,20,2,128]{3,2,1,0:T(2,128)}, f32[7,20,2,128]{3,2,1,0:T(2,128)}, u32[]{:S(2)}, u32[]{:S(2)}) collective-permute-start(f32[7,20,2,128]{3,2,1,0:T(2,128)} %get-tuple-element.109), channel_id=1, source_target_pairs={{2,0},{4,2},{6,4},{8,6},{10,8},{12,10},{14,12},{3,1},{5,3},{7,5},{... | collective-permute-start | bytes 430088 | tf_op jit(solution)/shard_map/ppermute | solution.py:33
  47.8 2.6 %copy-start.21 = (f32[5,16,40,128]{3,2,1,0:T(8,128)S(1)}, f32[5,16,40,128]{3,2,1,0:T(8,128)}, u32[]{:S(2)}) copy-start(f32[5,16,40,128]{3,2,1,0:T(8,128)} %get-tuple-element.129) | copy-start | bytes 4915204
  59.6 8.7 %copy-start.32 = (f32[16,40]{1,0:T(8,128)S(1)}, f32[16,40]{1,0:T(8,128)}, u32[]{:S(2)}) copy-start(f32[16,40]{1,0:T(8,128)} %param.13) | copy-start | bytes 7684
  59.6 15.2 %copy-start.33 = (f32[16,40]{1,0:T(8,128)S(1)}, f32[16,40]{1,0:T(8,128)}, u32[]{:S(2)}) copy-start(f32[16,40]{1,0:T(8,128)} %get-tuple-element.70) | copy-start | bytes 7684
  59.6 15.2 %copy-start.34 = (s32[16,40]{1,0:T(8,128)S(1)}, s32[16,40]{1,0:T(8,128)}, u32[]{:S(2)}) copy-start(s32[16,40]{1,0:T(8,128)} %param.17) | copy-start | bytes 7684
  104.7 4.1 %copy-start.35 = (f32[16,40]{1,0:T(8,128)}, f32[16,40]{1,0:T(8,128)S(1)}, u32[]{:S(2)}) copy-start(f32[16,40]{1,0:T(8,128)S(1)} %psum.15) | copy-start | bytes 7684
  104.8 4.0 %copy-start.12 = (f32[5,16,40,128]{3,2,1,0:T(8,128)S(1)}, f32[5,16,40,128]{3,2,1,0:T(8,128)}, u32[]{:S(2)}) copy-start(f32[5,16,40,128]{3,2,1,0:T(8,128)} %get-tuple-element.105) | copy-start | bytes 4915204
  104.8 4.0 %copy-start.19 = (f32[1,16,40,128]{3,2,1,0:T(8,128)S(1)}, f32[1,16,40,128]{3,2,1,0:T(8,128)}, u32[]{:S(2)}) copy-start(f32[1,16,40,128]{3,2,1,0:T(8,128)} %copy-done.18) | copy-start | bytes 983044
  104.9 4.0 %copy-start.26 = (f32[1,16,40,128]{3,2,1,0:T(8,128)S(1)}, f32[1,16,40,128]{3,2,1,0:T(8,128)}, u32[]{:S(2)}) copy-start(f32[1,16,40,128]{3,2,1,0:T(8,128)} %get-tuple-element.125) | copy-start | bytes 983044
  113.9 2.1 %copy-start.22 = (f32[5,16,40,128]{3,2,1,0:T(8,128)S(1)}, f32[5,16,40,128]{3,2,1,0:T(8,128)}, u32[]{:S(2)}) copy-start(f32[5,16,40,128]{3,2,1,0:T(8,128)} %get-tuple-element.129) | copy-start | bytes 4915204
  113.9 2.6 %copy-start.24 = (f32[5,16,40,128]{3,2,1,0:T(8,128)S(1)}, f32[5,16,40,128]{3,2,1,0:T(8,128)}, u32[]{:S(2)}) copy-start(f32[5,16,40,128]{3,2,1,0:T(8,128)} %param.12) | copy-start | bytes 4915204
  (10 other events, 14.0 us)
where the time goes:
time: 120 us; the launch traced here: 119 us
  blocking collectives  35.7 us (30%)
  other arithmetic  33 us (28%)
  local copies, waits for them, and re-layouts  29 us (24%)
  starting transfers between devices  18.7 us (16%)
  between operations  1.28 us (1%)
    all_gather x1, blocking collectives, prefix(): gathered = lax.all_gather(part, axis)  22.6 us
    ppermute x3, starting transfers between devices, extended(): lax.ppermute(lax.slice_in_dim(block, 0, width, axis=dim), axis, backward)  11.6 us
    reduce_sum x1, other arithmetic, local(): jnp.sum(scaled * (flux_above - flux_below), axis=(0, 3))  8.65 us
    unnamed x73, local copies, waits for them, and re-layouts  8.41 us
    slice x2, local copies, waits for them, and re-layouts, extended(): lax.slice_in_dim(block, block.shape[dim] - width, None, axis=dim)  7.2 us
    ppermute x3, starting transfers between devices, extended(): lax.ppermute(lax.slice_in_dim(block, block.shape[dim] - width, None, axis...  7.06 us
    psum x1, blocking collectives, spread(): return lax.psum(block, axis)  6.53 us
    psum x1, blocking collectives, local(): metric = lax.psum(metric_part, 'nrm')  6.53 us
  transfers between devices with their start and end apart: 6, of which 1 were waited for; matrix products, arithmetic and copies ran while one was open for 24% of the time, Pallas kernels for 0%

commit v1 on v0

v1 whole, which is shorter than its diff:
```python
import functools

import jax
import jax.numpy as jnp
from jax import lax
from jax.experimental import pallas as pl
from jax.experimental.pallas import tpu as pltpu
from jax.sharding import PartitionSpec as P

gamma_ratio = 1.4
damping_coef = 0.0625
stretch_rate = 2.2
gm = gamma_ratio - 1.0
f32 = jnp.float32
VMEM = pltpu.VMEM


def lanes(shape=(8, 128)):
    return lax.broadcasted_iota(jnp.int32, shape, 1)


def spread_lane(tile, lane):
    return jnp.broadcast_to(tile[:, lane : lane + 1], tile.shape)


def edges_kernel(rows, tiles, prim, psi, ends, su_low, su_high, sv_low, sv_high):
    nrm = lax.axis_index("nrm")
    lane = lanes()
    extra = jnp.where(nrm == 0, 1, 0)
    for t in range(tiles):
        packed = jnp.zeros((8, 128), f32)
        for q in range(5):
            for i in range(rows):
                spot = rows * q + i
                moved = pltpu.roll(psi[q, i, 8 * t : 8 * t + 8, :], spot + extra, 1)
                packed = jnp.where(lane == spot, moved, packed)
        ends[8 * t : 8 * t + 8, :] = packed

    def radius(which, i, low, high):
        sound = jnp.sqrt(gamma_ratio * prim[4, i, low:high, :] / prim[0, i, low:high, :])
        return jnp.abs(prim[which, i, low:high, :]) + sound

    columns = 8 * tiles
    for r in range(2):
        for q in range(5):
            su_low[q, r] = psi[q, r]
            su_high[q, r] = psi[q, rows - 2 + r]
        su_low[5, r] = radius(1, r, 0, columns)
        su_high[5, r] = radius(1, rows - 2 + r, 0, columns)
    for i in range(rows):
        for q in range(5):
            sv_low[q, 2 * i : 2 * i + 2, :] = psi[q, i, 0:2, :]
            sv_high[q, 2 * i : 2 * i + 2, :] = psi[q, i, columns - 2 : columns, :]
        sv_low[5, 2 * i : 2 * i + 2, :] = radius(2, i, 0, 8)[0:2]
        sv_high[5, 2 * i : 2 * i + 2, :] = radius(2, i, columns - 8, columns)[6:8]


def flux_of(rho, u1, u2, u3, p, enthalpy):
    mass = rho * u3
    return (mass, mass * u1, mass * u2, mass * u3 + p, mass * enthalpy)


def thermo(rho, u1, u2, u3, p):
    half = 0.5 * (u1 * u1 + u2 * u2 + u3 * u3)
    return gm * half, (gamma_ratio / gm) * (p / rho) + half


def lines_kernel(
    rows, tiles, depth, total_depth, surface, fan,
    prim, psi, arrived, height, shock, by_height, by_slope, flags,
    chunk, normal,
    turn, facts,
):
    nrm = lax.axis_index("nrm")
    first = nrm == 0
    lane = lanes()
    lane_row = lanes((1, 128))
    depth_index = (lane_row + nrm * depth).astype(f32)
    inv_stretch = 1.0 / jnp.exp(stretch_rate * ((depth_index + 0.5) / total_depth - 1.0))
    partner = jnp.where(first, depth, depth - 1).astype(f32)
    partner_row = jnp.zeros((1, 128), f32) + partner
    partner_inv = 1.0 / jnp.exp(stretch_rate * ((partner_row + 0.5) / total_depth - 1.0))
    top_inv = 1.0 / jnp.exp(
        stretch_rate * ((jnp.zeros((1, 128), f32) + (total_depth - 0.5)) / total_depth - 1.0)
    )
    weight = 0.5 * inv_stretch
    lower = jnp.broadcast_to(jnp.where(lane_row == depth - 1, 0.0, weight), (8, 128))
    upper = jnp.broadcast_to(jnp.where(lane_row == 0, 0.0, weight), (8, 128))
    entry = jnp.where(first, depth - 1, 0)
    sign = jnp.where(first, -0.5, 0.5)
    edge = jnp.broadcast_to(jnp.where(lane_row == entry, sign * partner_inv, 0.0), (8, 128))

    turn[...] = jnp.zeros_like(turn)
    columns = 8 * tiles
    for place, array in enumerate(
        [height[...]]
        + [shock[q] for q in range(5)]
        + [flags[...].astype(f32)]
    ):
        turn[0, rows * place : rows * place + rows, 0:columns] = array
    for q in range(5):
        turn[1, rows * q : rows * q + rows, 0:columns] = by_height[q]
        turn[2, rows * q : rows * q + rows, 0:columns] = by_slope[q]
    for n in range(3):
        facts[n] = turn[n].T

    out = jnp.zeros((8, 128), f32)
    for t in range(tiles):
        span = slice(8 * t, 8 * t + 8)
        surf = facts[0, span, :]
        inv_height = jnp.where(lane < rows, 1.0 / jnp.where(lane < rows, surf, 1.0), 0.0)
        came = arrived[span, :]
        gathered = jnp.zeros((8, 128), f32)
        tops = jnp.zeros((8, 128), f32)
        for i in range(rows):
            rho, u1, u2, u3, p = (prim[q, i, span, :] for q in range(5))
            _, enthalpy = thermo(rho, u1, u2, u3, p)
            fluxes = flux_of(rho, u1, u2, u3, p, enthalpy)
            inv = spread_lane(inv_height, i)
            low, high, end = lower * inv, upper * inv, edge * inv
            work = None
            for q in range(5):
                value = psi[q, i, span, :]
                spot = rows * q + i
                step = (
                    pltpu.roll(value * low, 1, 1)
                    - pltpu.roll(value * high, 127, 1)
                    + end * spread_lane(came, spot)
                )
                normal[q, i, span, :] = step
                work = fluxes[q] * step if work is None else work + fluxes[q] * step
                tops = jnp.where(lane == spot, pltpu.roll(value, (spot + 1) % 128, 1), tops)
            summed = jnp.broadcast_to(jnp.sum(work, axis=1, keepdims=True), (8, 128))
            gathered = jnp.where(lane == i, summed, gathered)

        def part(array, q):
            return pltpu.roll(array, (128 - rows * q) % 128, 1) if q else array

        inside = lane < rows
        rho, u1, u2, u3, p = (
            jnp.where(inside, part(surf, q + 1), 1.0) for q in range(5)
        )
        fitted = jnp.where(inside, part(surf, 6), 0.0)
        top_scale = 0.5 * top_inv * inv_height
        s0, s1, s2, s3, s4 = (part(tops, q) * top_scale for q in range(5))
        kinetic, enthalpy = thermo(rho, u1, u2, u3, p)
        fluxes = flux_of(rho, u1, u2, u3, p, enthalpy)
        top_work = (
            fluxes[0] * s0 + fluxes[1] * s1 + fluxes[2] * s2 + fluxes[3] * s3 + fluxes[4] * s4
        )
        dotted = u1 * s1 + u2 * s2 + u3 * s3
        shared = gm * (s3 + u3 * s4)
        common = s0 + dotted + enthalpy * s4
        adjoint = (
            kinetic * s3 - u3 * dotted + u3 * (kinetic - enthalpy) * s4,
            u3 * s1 - u1 * shared,
            u3 * s2 - u2 * shared,
            u3 * s3 - u3 * shared + common,
            gm * s3 + gamma_ratio * u3 * s4,
        )
        heights = facts[1, span, :]
        slopes = facts[2, span, :]
        by_h = sum(adjoint[q] * part(heights, q) for q in range(5))
        by_s = sum(adjoint[q] * part(slopes, q) for q in range(5))
        front = jnp.where(first, 0.0, 1.0)
        metric = -inv_height * (gathered + front * top_work)
        term = jnp.where(inside, metric + front * fitted * by_h, 0.0)
        for d in (1, 2, 4, 8):
            if d < rows:
                term = term + pltpu.roll(term, 128 - d, 1)
        share = term * (1.0 / surface)
        mine = share + jnp.where(inside, front * fitted * by_s, 0.0)
        out = jnp.where(
            (lane >= rows * t) & (lane < rows * t + rows),
            pltpu.roll(mine, rows * t, 1) if t else mine,
            out,
        )
        out = jnp.where(lane == rows * tiles + t, spread_lane(share, 0), out)
    for n in range(fan):
        chunk[n] = out


def final_kernel(
    rows, tiles, depth, total_depth, su_count, sv_count, fan,
    prim, psi, target, normal, su_low, su_high, sv_low, sv_high, chunks,
    result, slope,
    wide, along, across, enth, turn,
):
    su, sv, nrm = lax.axis_index("su"), lax.axis_index("sv"), lax.axis_index("nrm")
    lane = lanes()
    columns = 8 * tiles
    lines = fan // su_count
    ahead = jnp.zeros((8, 128), f32)
    for n in range(fan):
        ahead = ahead + jnp.where(n // lines > su, chunks[n], 0.0)
    packed = chunks[lines * su]
    for n in range(1, lines):
        packed = packed + chunks[lines * su + n]
    upstream = jnp.zeros((8, 128), f32)
    for t in range(tiles):
        upstream = jnp.where(
            (lane >= rows * t) & (lane < rows * t + rows),
            spread_lane(ahead, rows * tiles + t),
            upstream,
        )
    packed = packed + upstream
    turn[...] = jnp.zeros_like(turn)
    for t in range(tiles):
        turn[8 * t : 8 * t + 8, :] = pltpu.roll(packed, 128 - rows * t, 1) if t else packed
    slope[...] = turn[...].T[0:rows, 0:columns]

    low_on, high_on = su > 0, su < su_count - 1
    for r in range(2):
        for ref, on, row in ((su_low, low_on, r), (su_high, high_on, rows + 2 + r)):
            radius = ref[5, r]
            for q in range(5):
                value = jnp.where(on, ref[q, r], 0.0)
                wide[q, row, 8 : 8 + columns, :] = value
                along[q, row] = value * radius
    left_on, right_on = sv > 0, sv < sv_count - 1
    for ref, on, col in ((sv_low, left_on, 6), (sv_high, right_on, 8 + columns)):
        for q in range(5):
            value = jnp.where(on, ref[q], 0.0)
            weighted = value * ref[5]
            for i in range(rows):
                wide[q, i + 2, col : col + 2, :] = value[2 * i : 2 * i + 2]
                across[q, i, col : col + 2, :] = weighted[2 * i : 2 * i + 2]

    @pl.loop(0, rows)
    def _(i):
        for t in range(tiles):
            span = slice(8 * t, 8 * t + 8)
            inner = slice(8 * t + 8, 8 * t + 16)
            rho, u1, u2, u3, p = (prim[q, i, span, :] for q in range(5))
            ratio = p / rho
            sound = jnp.sqrt(gamma_ratio * ratio)
            enth[i, span, :] = (gamma_ratio / gm) * ratio + 0.5 * (u1 * u1 + u2 * u2 + u3 * u3)
            radius_u = jnp.abs(u1) + sound
            radius_v = jnp.abs(u2) + sound
            for q in range(5):
                value = psi[q, i, span, :]
                wide[q, i + 2, inner, :] = value
                along[q, i + 2, span, :] = radius_u * value
                across[q, i, inner, :] = radius_v * value

    fraction = jnp.broadcast_to(
        ((lanes((1, 128)) + nrm * depth).astype(f32) + 0.5) / total_depth, (8, 128)
    )

    @pl.loop(0, rows)
    def _(i):
        turned = pltpu.roll(packed, 128 - i, 1)
        for t in range(tiles):
            span = slice(8 * t, 8 * t + 8)
            at = lambda k: slice(8 * t + 8 + k, 8 * t + 16 + k)
            first, second, damp = [], [], []
            for q in range(5):
                first.append(
                    (8.0 / 12.0) * (wide[q, i + 1, at(0), :] - wide[q, i + 3, at(0), :])
                    - (1.0 / 12.0) * (wide[q, i, at(0), :] - wide[q, i + 4, at(0), :])
                )
                second.append(
                    (8.0 / 12.0) * (wide[q, i + 2, at(-1), :] - wide[q, i + 2, at(1), :])
                    - (1.0 / 12.0) * (wide[q, i + 2, at(-2), :] - wide[q, i + 2, at(2), :])
                )
                far = (
                    along[q, i, span, :] + along[q, i + 4, span, :]
                    + across[q, i, at(-2), :] + across[q, i, at(2), :]
                )
                near = (
                    along[q, i + 1, span, :] + along[q, i + 3, span, :]
                    + across[q, i, at(-1), :] + across[q, i, at(1), :]
                )
                here = along[q, i + 2, span, :] + across[q, i, at(0), :]
                damp.append(
                    damping_coef * far - (4.0 * damping_coef) * near + (6.0 * damping_coef) * here
                )
            third = [normal[q, i, span, :] for q in range(5)]
            rho, u1, u2, u3, p = (prim[q, i, span, :] for q in range(5))
            enthalpy = enth[i, span, :]
            kinetic = (0.5 * gm) * (u1 * u1 + u2 * u2 + u3 * u3)
            fluxes = flux_of(rho, u1, u2, u3, p, enthalpy)
            projected = first[1] + second[2] + third[3]
            energy = u1 * first[4] + u2 * second[4] + u3 * third[4]
            dot = lambda g: u1 * g[1] + u2 * g[2] + u3 * g[3]
            dot1, dot2, dot3 = dot(first), dot(second), dot(third)
            mass_row = (
                kinetic * projected
                - (u1 * dot1 + u2 * dot2 + u3 * dot3)
                + (kinetic - enthalpy) * energy
            )
            shared = gm * (projected + energy)
            moved = lambda b: u1 * first[b] + u2 * second[b] + u3 * third[b]
            rows_out = (
                mass_row,
                moved(1) - u1 * shared + (first[0] + dot1 + enthalpy * first[4]),
                moved(2) - u2 * shared + (second[0] + dot2 + enthalpy * second[4]),
                moved(3) - u3 * shared + (third[0] + dot3 + enthalpy * third[4]),
                gm * projected + gamma_ratio * energy,
            )
            ramp = fraction * spread_lane(turned, rows * t)
            for q in range(5):
                result[q, i, span, :] = (
                    target[q, i, span, :] + rows_out[q] + damp[q] + ramp * fluxes[q]
                )


def call(kernel, outs, operands, scratch, flops, name):
    spec = pl.BlockSpec(memory_space=VMEM)
    many = isinstance(outs, (list, tuple))
    size = sum(4 * a.size for a in operands) + sum(
        4 * o.size for o in (outs if many else [outs])
    )
    return pl.pallas_call(
        kernel,
        out_shape=outs,
        in_specs=[spec] * len(operands),
        out_specs=[spec] * len(outs) if many else spec,
        scratch_shapes=scratch,
        cost_estimate=pl.CostEstimate(flops=flops, transcendentals=0, bytes_accessed=size),
        compiler_params=pltpu.CompilerParams(vmem_limit_bytes=16 << 20),
        name=name,
    )(*operands)


def local(
    primitive, adjoint_state, objective_grad, front_height,
    shock_state, state_by_height, state_by_slope, fitted_flags,
):
    _, rows, columns, depth = adjoint_state.shape
    tiles = columns // 8
    su_count, sv_count, lines = (lax.axis_size(a) for a in ("su", "sv", "nrm"))
    fan = su_count * lines
    shape = lambda *s: jax.ShapeDtypeStruct(s, f32)
    points = 5 * rows * columns * depth

    ends, su_low, su_high, sv_low, sv_high = call(
        functools.partial(edges_kernel, rows, tiles),
        [
            shape(columns, 128),
            shape(6, 2, columns, depth),
            shape(6, 2, columns, depth),
            shape(6, 2 * rows, depth),
            shape(6, 2 * rows, depth),
        ],
        (primitive, adjoint_state),
        [],
        4 * points,
        "edges",
    )

    def ring(count, by):
        return [(i, (i + by) % count) for i in range(count)]

    arrived = lax.ppermute(ends, "nrm", [(0, 1), (1, 0)])
    from_low = lax.ppermute(su_high, "su", ring(su_count, 1))
    from_high = lax.ppermute(su_low, "su", ring(su_count, -1))
    from_left = lax.ppermute(sv_high, "sv", ring(sv_count, 1))
    from_right = lax.ppermute(sv_low, "sv", ring(sv_count, -1))

    chunk, normal = call(
        functools.partial(
            lines_kernel, rows, tiles, depth, depth * lines, rows * su_count, fan
        ),
        [shape(fan, 8, 128), shape(5, rows, columns, depth)],
        (
            primitive, adjoint_state, arrived, front_height,
            shock_state, state_by_height, state_by_slope, fitted_flags,
        ),
        [VMEM((3, 128, 128), f32), VMEM((3, 128, 128), f32)],
        12 * points,
        "lines",
    )
    chunks = lax.all_to_all(chunk, ("su", "nrm"), 0, 0)
    result, slope = call(
        functools.partial(
            final_kernel, rows, tiles, depth, depth * lines, su_count, sv_count, fan
        ),
        [shape(5, rows, columns, depth), shape(rows, columns)],
        (
            primitive, adjoint_state, objective_grad, normal,
            from_low, from_high, from_left, from_right, chunks,
        ),
        [
            VMEM((5, rows + 4, columns + 16, depth), f32),
            VMEM((5, rows + 4, columns, depth), f32),
            VMEM((5, rows, columns + 16, depth), f32),
            VMEM((rows, columns, depth), f32),
            VMEM((128, 128), f32),
        ],
        40 * points,
        "final",
    )
    return result, slope


def solution(mesh):
    wide = P(None, "su", "sv", "nrm")
    flat = P("su", "sv")
    front = P(None, "su", "sv")
    return jax.shard_map(
        local,
        mesh=mesh,
        in_specs=(wide, wide, wide, flat, front, front, front, flat),
        out_specs=(wide, flat),
        check_vma=False,
    )
```

time: 120 us -> 59.6 us (0.50)
  the two profiles are of different devices: /device:TPU:22 before, /device:TPU:30 now
where the time goes in v1:
time: 59.6 us; the launch traced here: 59.3 us
  starting transfers between devices  17.8 us (30%)
  Pallas kernels  16.8 us (28%)
  local copies, waits for them, and re-layouts  14.3 us (24%)
  waiting for transfers between devices  9.63 us (16%)
  between operations  0.73 us (1%)
    pallas_call x3, Pallas kernels, call(): pl.pallas_call(kernel, out_shape=outs, in_specs=[spec] * len(operands), o...  16.8 us
    unnamed x44, local copies, waits for them, and re-layouts  14.3 us
    all_to_all x1, starting transfers between devices, local(): chunks = lax.all_to_all(chunk, ('su', 'nrm'), 0, 0)  11.6 us
    ppermute x1, waiting for transfers between devices, local(): from_left = lax.ppermute(sv_high, 'sv', ring(sv_count, 1))  4.07 us
    ppermute x1, waiting for transfers between devices, local(): arrived = lax.ppermute(ends, 'nrm', [(0, 1), (1, 0)])  4.05 us
    ppermute x1, starting transfers between devices, local(): from_high = lax.ppermute(su_low, 'su', ring(su_count, -1))  2.81 us
    ppermute x1, waiting for transfers between devices, local(): from_right = lax.ppermute(sv_low, 'sv', ring(sv_count, -1))  1.49 us
    ppermute x1, starting transfers between devices, local(): from_right = lax.ppermute(sv_low, 'sv', ring(sv_count, -1))  1.37 us
  transfers between devices with their start and end apart: 6, of which 3 were waited for; matrix products, arithmetic and copies ran while one was open for 0% of the time, Pallas kernels for 0%

profile of v1, /device:TPU:30, one launch (start us, length us, event | category | flops | bytes accessed | tf_op | source)
XLA Modules:
  0.0 59.3 jit_solution(5726346980542363699)
XLA Ops:
  0.6 0.0 copy-start
  0.6 1.4 %copy-done = f32[5,16,40,128]{3,2,1,0:T(8,128)S(1)} copy-done((f32[5,16,40,128]{3,2,1,0:T(8,128)S(1)}, f32[5,16,40,128]{3,2,1,0:T(8,128)}, u32[]{:S(2)}) %copy-start) | copy-done | bytes 1638424
  2.1 1.4 %copy-done.2 = f32[5,16,40,128]{3,2,1,0:T(8,128)S(1)} copy-done((f32[5,16,40,128]{3,2,1,0:T(8,128)S(1)}, f32[5,16,40,128]{3,2,1,0:T(8,128)}, u32[]{:S(2)}) %copy-start.2) | copy-done | bytes 1638424
  3.5 0.6 edges.1
  4.1 0.7 %copy-done.18 = f32[6,2,40,128]{3,2,1,0:T(8,128)} copy-done((f32[6,2,40,128]{3,2,1,0:T(8,128)}, f32[6,2,40,128]{3,2,1,0:T(8,128)S(1)}, u32[]{:S(2)}) %copy-start.18) | copy-done | bytes 245784
  4.8 0.7 %copy-done.19 = f32[6,2,40,128]{3,2,1,0:T(8,128)} copy-done((f32[6,2,40,128]{3,2,1,0:T(8,128)}, f32[6,2,40,128]{3,2,1,0:T(8,128)S(1)}, u32[]{:S(2)}) %copy-start.19) | copy-done | bytes 245784
  5.5 0.6 %copy-done.20 = f32[6,32,128]{2,1,0:T(8,128)} copy-done((f32[6,32,128]{2,1,0:T(8,128)}, f32[6,32,128]{2,1,0:T(8,128)S(1)}, u32[]{:S(2)}) %copy-start.20) | copy-done | bytes 98328
  6.1 0.6 %copy-done.21 = f32[6,32,128]{2,1,0:T(8,128)} copy-done((f32[6,32,128]{2,1,0:T(8,128)}, f32[6,32,128]{2,1,0:T(8,128)S(1)}, u32[]{:S(2)}) %copy-start.21) | copy-done | bytes 98328
  6.7 1.2 %collective-permute-start = (f32[40,128]{1,0:T(8,128)S(1)}, f32[40,128]{1,0:T(8,128)S(1)}, u32[]{:S(2)}, u32[]{:S(2)}) collective-permute-start(f32[40,128]{1,0:T(8,128)S(1)} %get-tuple-element.9), channel_id=1, source_target_pairs={{0,1},{1,0},{2,3},{3,2},{4,5},{5,4},{6,7},{7,6},{8,9},{9,8},{10,11... | collective-permute-start | bytes 61448 | tf_op jit(solution)/shard_map/ppermute | solution.py:355
  8.0 4.1 %collective-permute-done.arrived = f32[40,128]{1,0:T(8,128)S(1)} collective-permute-done((f32[40,128]{1,0:T(8,128)S(1)}, f32[40,128]{1,0:T(8,128)S(1)}, u32[]{:S(2)}, u32[]{:S(2)}) %collective-permute-start) | collective-permute-done | bytes 20512 | tf_op jit(solution)/shard_map/ppermute | solution.py:355
  12.1 10.7 %lines.1 = (f32[32,8,128]{2,1,0:T(8,128)}, f32[5,16,40,128]{3,2,1,0:T(8,128)S(1)}) custom-call(f32[5,16,40,128]{3,2,1,0:T(8,128)S(1)} %copy-done, f32[5,16,40,128]{3,2,1,0:T(8,128)S(1)} %copy-done.2, f32[40,128]{1,0:T(8,128)S(1)} %collective-permute-done.arrived, f32[16,40]{1,0:T(8,128)S(1)} %copy-done.16, f32[5,16,40]{2,1,0:T(8,128)S(1)} %copy-done.13, ...), custom_call_target="tpu_custom_call" | custom-call | flops 4915200 | bytes 5110272 | tf_op jit(solution)/shard_map/lines/pallas_call | solution.py:314
  22.7 1.2 %copy-done.5 = f32[5,16,40,128]{3,2,1,0:T(8,128)} copy-done((f32[5,16,40,128]{3,2,1,0:T(8,128)}, f32[5,16,40,128]{3,2,1,0:T(8,128)S(1)}, u32[]{:S(2)}) %copy-start.5) | copy-done | bytes 1638424
  23.9 11.6 %all-to-all-start = ((f32[32,8,128]{2,1,0:T(8,128)}), f32[32,8,128]{2,1,0:T(8,128)S(1)}, u32[]{:S(2)}, u32[]{:S(2)}) async-start(f32[32,8,128]{2,1,0:T(8,128)} %get-tuple-element.15), calls=%async_computation | async-start | bytes 262144 | tf_op jit(solution)/shard_map/all_to_all | solution.py:374
  35.5 0.2 collective-permute-start.1
  35.7 2.8 %collective-permute-start.2 = (f32[6,2,40,128]{3,2,1,0:T(8,128)}, f32[6,2,40,128]{3,2,1,0:T(8,128)S(1)}, u32[]{:S(2)}, u32[]{:S(2)}) collective-permute-start(f32[6,2,40,128]{3,2,1,0:T(8,128)} %copy-done.18), channel_id=1, source_target_pairs={{0,240},{16,0},{32,16},{48,32},{64,48},{80,64},{96,80},{112,96},{1... | collective-permute-start | bytes 737288 | tf_op jit(solution)/shard_map/ppermute | solution.py:357
  38.5 0.7 %collective-permute-start.3 = (f32[6,32,128]{2,1,0:T(8,128)}, f32[6,32,128]{2,1,0:T(8,128)S(1)}, u32[]{:S(2)}, u32[]{:S(2)}) collective-permute-start(f32[6,32,128]{2,1,0:T(8,128)} %copy-done.21), channel_id=1, source_target_pairs={{0,2},{2,4},{4,6},{6,8},{8,10},{10,12},{12,14},{14,0},{1,3},{3,5},... | collective-permute-start | bytes 294920 | tf_op jit(solution)/shard_map/ppermute | solution.py:358
  39.1 1.4 %collective-permute-start.4 = (f32[6,32,128]{2,1,0:T(8,128)}, f32[6,32,128]{2,1,0:T(8,128)S(1)}, u32[]{:S(2)}, u32[]{:S(2)}) collective-permute-start(f32[6,32,128]{2,1,0:T(8,128)} %copy-done.20), channel_id=1, source_target_pairs={{0,14},{2,0},{4,2},{6,4},{8,6},{10,8},{12,10},{14,12},{1,15},{3,1}... | collective-permute-start | bytes 294920 | tf_op jit(solution)/shard_map/ppermute | solution.py:359
  40.5 4.1 %collective-permute-done.3.sv_low = f32[6,32,128]{2,1,0:T(8,128)S(1)} collective-permute-done((f32[6,32,128]{2,1,0:T(8,128)}, f32[6,32,128]{2,1,0:T(8,128)S(1)}, u32[]{:S(2)}, u32[]{:S(2)}) %collective-permute-start.3) | collective-permute-done | bytes 98336 | tf_op jit(solution)/shard_map/ppermute | solution.py:358
  44.6 1.5 %collective-permute-done.4.sv_high = f32[6,32,128]{2,1,0:T(8,128)S(1)} collective-permute-done((f32[6,32,128]{2,1,0:T(8,128)}, f32[6,32,128]{2,1,0:T(8,128)S(1)}, u32[]{:S(2)}, u32[]{:S(2)}) %collective-permute-start.4) | collective-permute-done | bytes 98336 | tf_op jit(solution)/shard_map/ppermute | solution.py:359
  46.1 0.6 %copy-done.11 = f32[6,32,128]{2,1,0:T(8,128)} copy-done((f32[6,32,128]{2,1,0:T(8,128)}, f32[6,32,128]{2,1,0:T(8,128)S(1)}, u32[]{:S(2)}) %copy-start.11) | copy-done | bytes 98328
  46.7 0.0 collective-permute-done.1.su_low
  46.7 0.7 %copy-done.7 = f32[6,2,40,128]{3,2,1,0:T(8,128)} copy-done((f32[6,2,40,128]{3,2,1,0:T(8,128)}, f32[6,2,40,128]{3,2,1,0:T(8,128)S(1)}, u32[]{:S(2)}) %copy-start.7) | copy-done | bytes 245784
  47.4 0.0 collective-permute-done.2.su_high
  47.4 0.7 %copy-done.9 = f32[6,2,40,128]{3,2,1,0:T(8,128)} copy-done((f32[6,2,40,128]{3,2,1,0:T(8,128)}, f32[6,2,40,128]{3,2,1,0:T(8,128)S(1)}, u32[]{:S(2)}) %copy-start.9) | copy-done | bytes 245784
  48.1 0.0 all-to-all-done.chunks
  48.1 0.0 copy-start.4
  48.1 1.4 %copy-done.4 = f32[5,16,40,128]{3,2,1,0:T(8,128)S(1)} copy-done((f32[5,16,40,128]{3,2,1,0:T(8,128)S(1)}, f32[5,16,40,128]{3,2,1,0:T(8,128)}, u32[]{:S(2)}) %copy-start.4) | copy-done | bytes 1638424
  49.5 1.4 %copy-done.6 = f32[5,16,40,128]{3,2,1,0:T(8,128)S(1)} copy-done((f32[5,16,40,128]{3,2,1,0:T(8,128)S(1)}, f32[5,16,40,128]{3,2,1,0:T(8,128)}, u32[]{:S(2)}) %copy-start.6) | copy-done | bytes 1638424
  51.0 0.9 %copy-done.8 = f32[6,2,40,128]{3,2,1,0:T(8,128)S(1)} copy-done((f32[6,2,40,128]{3,2,1,0:T(8,128)S(1)}, f32[6,2,40,128]{3,2,1,0:T(8,128)}, u32[]{:S(2)}) %copy-start.8) | copy-done | bytes 245784
  51.9 0.9 %copy-done.10 = f32[6,2,40,128]{3,2,1,0:T(8,128)S(1)} copy-done((f32[6,2,40,128]{3,2,1,0:T(8,128)S(1)}, f32[6,2,40,128]{3,2,1,0:T(8,128)}, u32[]{:S(2)}) %copy-start.10) | copy-done | bytes 245784
  52.8 0.9 %copy-done.12 = f32[6,32,128]{2,1,0:T(8,128)S(1)} copy-done((f32[6,32,128]{2,1,0:T(8,128)S(1)}, f32[6,32,128]{2,1,0:T(8,128)}, u32[]{:S(2)}) %copy-start.12) | copy-done | bytes 98328
  53.7 5.5 %final.1 = (f32[5,16,40,128]{3,2,1,0:T(8,128)}, f32[16,40]{1,0:T(8,128)}) custom-call(f32[5,16,40,128]{3,2,1,0:T(8,128)S(1)} %copy-done.1, f32[5,16,40,128]{3,2,1,0:T(8,128)S(1)} %copy-done.3, f32[5,16,40,128]{3,2,1,0:T(8,128)S(1)} %copy-done.4, f32[5,16,40,128]{3,2,1,0:T(8,128)S(1)} %copy-done.6, f32[6,2,40,128]{3,2,1,0:T(8,128)S(1)} %copy-done.8, ...), custom_call_target="tpu_custom_call" | custom-call | flops 16384000 | bytes 9013760 | tf_op jit(solution)/shard_map/final/pallas_call | solution.py:314
  (27 shorter events, 0.0 us)
Async XLA Ops:
  0.6 1.4 %copy-start = (f32[5,16,40,128]{3,2,1,0:T(8,128)S(1)}, f32[5,16,40,128]{3,2,1,0:T(8,128)}, u32[]{:S(2)}) copy-start(f32[5,16,40,128]{3,2,1,0:T(8,128)} %prim.5) | copy-start | bytes 4915204
  2.1 1.4 %copy-start.2 = (f32[5,16,40,128]{3,2,1,0:T(8,128)S(1)}, f32[5,16,40,128]{3,2,1,0:T(8,128)}, u32[]{:S(2)}) copy-start(f32[5,16,40,128]{3,2,1,0:T(8,128)} %psi.5) | copy-start | bytes 4915204
  3.5 8.5 %copy-start.13 = (f32[5,16,40]{2,1,0:T(8,128)S(1)}, f32[5,16,40]{2,1,0:T(8,128)}, u32[]{:S(2)}) copy-start(f32[5,16,40]{2,1,0:T(8,128)} %shock.1) | copy-start | bytes 38404
  3.5 8.5 %copy-start.14 = (f32[5,16,40]{2,1,0:T(8,128)S(1)}, f32[5,16,40]{2,1,0:T(8,128)}, u32[]{:S(2)}) copy-start(f32[5,16,40]{2,1,0:T(8,128)} %by_height.1) | copy-start | bytes 38404
  3.5 8.5 %copy-start.15 = (f32[5,16,40]{2,1,0:T(8,128)S(1)}, f32[5,16,40]{2,1,0:T(8,128)}, u32[]{:S(2)}) copy-start(f32[5,16,40]{2,1,0:T(8,128)} %by_slope.1) | copy-start | bytes 38404
  3.5 8.5 %copy-start.16 = (f32[16,40]{1,0:T(8,128)S(1)}, f32[16,40]{1,0:T(8,128)}, u32[]{:S(2)}) copy-start(f32[16,40]{1,0:T(8,128)} %height.1) | copy-start | bytes 7684
  3.5 8.6 %copy-start.17 = (s32[16,40]{1,0:T(8,128)S(1)}, s32[16,40]{1,0:T(8,128)}, u32[]{:S(2)}) copy-start(s32[16,40]{1,0:T(8,128)} %flags.1) | copy-start | bytes 7684
  4.1 0.7 %copy-start.18 = (f32[6,2,40,128]{3,2,1,0:T(8,128)}, f32[6,2,40,128]{3,2,1,0:T(8,128)S(1)}, u32[]{:S(2)}) copy-start(f32[6,2,40,128]{3,2,1,0:T(8,128)S(1)} %get-tuple-element.12) | copy-start | bytes 737284
  4.8 0.7 %copy-start.19 = (f32[6,2,40,128]{3,2,1,0:T(8,128)}, f32[6,2,40,128]{3,2,1,0:T(8,128)S(1)}, u32[]{:S(2)}) copy-start(f32[6,2,40,128]{3,2,1,0:T(8,128)S(1)} %get-tuple-element.11) | copy-start | bytes 737284
  5.5 0.6 %copy-start.20 = (f32[6,32,128]{2,1,0:T(8,128)}, f32[6,32,128]{2,1,0:T(8,128)S(1)}, u32[]{:S(2)}) copy-start(f32[6,32,128]{2,1,0:T(8,128)S(1)} %get-tuple-element.14) | copy-start | bytes 294916
  6.1 0.7 %copy-start.21 = (f32[6,32,128]{2,1,0:T(8,128)}, f32[6,32,128]{2,1,0:T(8,128)S(1)}, u32[]{:S(2)}) copy-start(f32[6,32,128]{2,1,0:T(8,128)S(1)} %get-tuple-element.13) | copy-start | bytes 294916
  6.7 41.3 %copy-start.1 = (f32[5,16,40,128]{3,2,1,0:T(8,128)S(1)}, f32[5,16,40,128]{3,2,1,0:T(8,128)}, u32[]{:S(2)}) copy-start(f32[5,16,40,128]{3,2,1,0:T(8,128)} %prim.5) | copy-start | bytes 4915204
  6.7 41.3 %copy-start.3 = (f32[5,16,40,128]{3,2,1,0:T(8,128)S(1)}, f32[5,16,40,128]{3,2,1,0:T(8,128)}, u32[]{:S(2)}) copy-start(f32[5,16,40,128]{3,2,1,0:T(8,128)} %psi.5) | copy-start | bytes 4915204
  6.7 5.3 %collective-permute-start = (f32[40,128]{1,0:T(8,128)S(1)}, f32[40,128]{1,0:T(8,128)S(1)}, u32[]{:S(2)}, u32[]{:S(2)}) collective-permute-start(f32[40,128]{1,0:T(8,128)S(1)} %get-tuple-element.9), channel_id=1, source_target_pairs={{0,1},{1,0},{2,3},{3,2},{4,5},{5,4},{6,7},{7,6},{8,9},{9,8},{10,11... | collective-permute-start | bytes 61448 | tf_op jit(solution)/shard_map/ppermute | solution.py:355
  22.7 1.2 %copy-start.5 = (f32[5,16,40,128]{3,2,1,0:T(8,128)}, f32[5,16,40,128]{3,2,1,0:T(8,128)S(1)}, u32[]{:S(2)}) copy-start(f32[5,16,40,128]{3,2,1,0:T(8,128)S(1)} %get-tuple-element.10.normal) | copy-start | bytes 4915204
  23.9 24.2 %all-to-all-start = ((f32[32,8,128]{2,1,0:T(8,128)}), f32[32,8,128]{2,1,0:T(8,128)S(1)}, u32[]{:S(2)}, u32[]{:S(2)}) async-start(f32[32,8,128]{2,1,0:T(8,128)} %get-tuple-element.15), calls=%async_computation | async-start | bytes 262144 | tf_op jit(solution)/shard_map/all_to_all | solution.py:374
  35.5 11.2 %collective-permute-start.1 = (f32[6,2,40,128]{3,2,1,0:T(8,128)}, f32[6,2,40,128]{3,2,1,0:T(8,128)S(1)}, u32[]{:S(2)}, u32[]{:S(2)}) collective-permute-start(f32[6,2,40,128]{3,2,1,0:T(8,128)} %copy-done.19), channel_id=1, source_target_pairs={{0,16},{16,32},{32,48},{48,64},{64,80},{80,96},{96,112},{112,128},... | collective-permute-start | bytes 737288 | tf_op jit(solution)/shard_map/ppermute | solution.py:356
  35.7 11.7 %collective-permute-start.2 = (f32[6,2,40,128]{3,2,1,0:T(8,128)}, f32[6,2,40,128]{3,2,1,0:T(8,128)S(1)}, u32[]{:S(2)}, u32[]{:S(2)}) collective-permute-start(f32[6,2,40,128]{3,2,1,0:T(8,128)} %copy-done.18), channel_id=1, source_target_pairs={{0,240},{16,0},{32,16},{48,32},{64,48},{80,64},{96,80},{112,96},{1... | collective-permute-start | bytes 737288 | tf_op jit(solution)/shard_map/ppermute | solution.py:357
  38.5 6.1 %collective-permute-start.3 = (f32[6,32,128]{2,1,0:T(8,128)}, f32[6,32,128]{2,1,0:T(8,128)S(1)}, u32[]{:S(2)}, u32[]{:S(2)}) collective-permute-start(f32[6,32,128]{2,1,0:T(8,128)} %copy-done.21), channel_id=1, source_target_pairs={{0,2},{2,4},{4,6},{6,8},{8,10},{10,12},{12,14},{14,0},{1,3},{3,5},... | collective-permute-start | bytes 294920 | tf_op jit(solution)/shard_map/ppermute | solution.py:358
  39.1 6.9 %collective-permute-start.4 = (f32[6,32,128]{2,1,0:T(8,128)}, f32[6,32,128]{2,1,0:T(8,128)S(1)}, u32[]{:S(2)}, u32[]{:S(2)}) collective-permute-start(f32[6,32,128]{2,1,0:T(8,128)} %copy-done.20), channel_id=1, source_target_pairs={{0,14},{2,0},{4,2},{6,4},{8,6},{10,8},{12,10},{14,12},{1,15},{3,1}... | collective-permute-start | bytes 294920 | tf_op jit(solution)/shard_map/ppermute | solution.py:359
  46.1 0.6 %copy-start.11 = (f32[6,32,128]{2,1,0:T(8,128)}, f32[6,32,128]{2,1,0:T(8,128)S(1)}, u32[]{:S(2)}) copy-start(f32[6,32,128]{2,1,0:T(8,128)S(1)} %collective-permute-done.4.sv_high) | copy-start | bytes 294916
  46.7 0.7 %copy-start.7 = (f32[6,2,40,128]{3,2,1,0:T(8,128)}, f32[6,2,40,128]{3,2,1,0:T(8,128)S(1)}, u32[]{:S(2)}) copy-start(f32[6,2,40,128]{3,2,1,0:T(8,128)S(1)} %collective-permute-done.1.su_low) | copy-start | bytes 737284
  47.4 0.7 %copy-start.9 = (f32[6,2,40,128]{3,2,1,0:T(8,128)}, f32[6,2,40,128]{3,2,1,0:T(8,128)S(1)}, u32[]{:S(2)}) copy-start(f32[6,2,40,128]{3,2,1,0:T(8,128)S(1)} %collective-permute-done.2.su_high) | copy-start | bytes 737284
  48.1 1.4 %copy-start.4 = (f32[5,16,40,128]{3,2,1,0:T(8,128)S(1)}, f32[5,16,40,128]{3,2,1,0:T(8,128)}, u32[]{:S(2)}) copy-start(f32[5,16,40,128]{3,2,1,0:T(8,128)} %target.1) | copy-start | bytes 4915204
  49.5 1.4 %copy-start.6 = (f32[5,16,40,128]{3,2,1,0:T(8,128)S(1)}, f32[5,16,40,128]{3,2,1,0:T(8,128)}, u32[]{:S(2)}) copy-start(f32[5,16,40,128]{3,2,1,0:T(8,128)} %copy-done.5) | copy-start | bytes 4915204
  50.9 0.9 %copy-start.8 = (f32[6,2,40,128]{3,2,1,0:T(8,128)S(1)}, f32[6,2,40,128]{3,2,1,0:T(8,128)}, u32[]{:S(2)}) copy-start(f32[6,2,40,128]{3,2,1,0:T(8,128)} %copy-done.7) | copy-start | bytes 737284
  51.9 0.9 %copy-start.10 = (f32[6,2,40,128]{3,2,1,0:T(8,128)S(1)}, f32[6,2,40,128]{3,2,1,0:T(8,128)}, u32[]{:S(2)}) copy-start(f32[6,2,40,128]{3,2,1,0:T(8,128)} %copy-done.9) | copy-start | bytes 737284
  52.8 0.9 %copy-start.12 = (f32[6,32,128]{2,1,0:T(8,128)S(1)}, f32[6,32,128]{2,1,0:T(8,128)}, u32[]{:S(2)}) copy-start(f32[6,32,128]{2,1,0:T(8,128)} %copy-done.11) | copy-start | bytes 294916

commit v2 on v1

v2 whole, which is shorter than its diff:
```python
import functools

import jax
import jax.numpy as jnp
from jax import lax
from jax.experimental import pallas as pl
from jax.experimental.pallas import tpu as pltpu
from jax.sharding import PartitionSpec as P

gamma_ratio = 1.4
damping_coef = 0.0625
stretch_rate = 2.2
gm = gamma_ratio - 1.0
f32 = jnp.float32
VMEM = pltpu.VMEM


def lanes(shape=(8, 128)):
    return lax.broadcasted_iota(jnp.int32, shape, 1)


def spread_lane(tile, lane):
    return jnp.broadcast_to(tile[:, lane : lane + 1], tile.shape)


def inv_stretch_at(index, total_depth):
    return 1.0 / jnp.exp(stretch_rate * ((index + 0.5) / total_depth - 1.0))


def even(axis):
    return lax.rem(lax.axis_index(axis), 2) == 0


def flux_of(rho, u1, u2, u3, p, enthalpy):
    mass = rho * u3
    return (mass, mass * u1, mass * u2, mass * u3 + p, mass * enthalpy)


def thermo(rho, u1, u2, u3, p):
    half = 0.5 * (u1 * u1 + u2 * u2 + u3 * u3)
    return gm * half, (gamma_ratio / gm) * (p / rho) + half


def part(array, q, rows):
    return pltpu.roll(array, 128 - rows * q, 1) if q else array


def prepare_kernel(
    rows, tiles, depth, total_depth,
    prim, psi, height, shock, by_height, by_slope, flags,
    packet, su_a, su_b, sv_a, sv_b, normal, flux, enth, tone, inverse,
    turn, facts, tops,
):
    nrm = lax.axis_index("nrm")
    first = nrm == 0
    lane = lanes()
    lane_row = lanes((1, 128))
    columns = 8 * tiles

    turn[...] = jnp.zeros_like(turn)
    tops[...] = jnp.zeros_like(tops)
    for place, array in enumerate(
        [height[...]]
        + [shock[q] for q in range(5)]
        + [flags[...].astype(f32)]
    ):
        turn[0, rows * place : rows * place + rows, 0:columns] = array
    for q in range(5):
        turn[1, rows * q : rows * q + rows, 0:columns] = by_height[q]
        turn[2, rows * q : rows * q + rows, 0:columns] = by_slope[q]
    for n in range(3):
        facts[n] = turn[n].T
    for t in range(tiles):
        span = slice(8 * t, 8 * t + 8)
        inverse[span, :] = jnp.where(
            lane < rows, 1.0 / jnp.where(lane < rows, facts[0, span, :], 1.0), 0.0
        )

    for t in range(tiles):
        span = slice(8 * t, 8 * t + 8)
        for i in range(rows):
            rho, u1, u2, u3, p = (prim[q, i, span, :] for q in range(5))
            ratio = p / rho
            enthalpy = (gamma_ratio / gm) * ratio + 0.5 * (u1 * u1 + u2 * u2 + u3 * u3)
            for q, value in enumerate(flux_of(rho, u1, u2, u3, p, enthalpy)):
                flux[q, i, span, :] = value
            enth[i, span, :] = enthalpy
            tone[i, span, :] = jnp.sqrt(gamma_ratio * ratio)

    extra = jnp.where(first, 1, 0)
    for t in range(tiles):
        span = slice(8 * t, 8 * t + 8)
        for half, ref in ((0, psi), (1, flux)):
            packed = jnp.zeros((8, 128), f32)
            for q in range(5):
                for i in range(rows):
                    spot = rows * q + i
                    moved = pltpu.roll(ref[q, i, span, :], spot + extra, 1)
                    packed = jnp.where(lane == spot, moved, packed)
            packet[span, 128 * half : 128 * half + 128] = packed

    @pl.when(jnp.logical_not(first))
    def _():
        for t in range(tiles):
            span = slice(8 * t, 8 * t + 8)
            packed = jnp.zeros((8, 128), f32)
            for q in range(5):
                for i in range(rows):
                    spot = rows * q + i
                    moved = pltpu.roll(psi[q, i, span, :], spot + 1, 1)
                    packed = jnp.where(lane == spot, moved, packed)
            tops[span, :] = packed

    depth_index = (lane_row + nrm * depth).astype(f32)
    weight = 0.5 * inv_stretch_at(depth_index, total_depth)
    lower = jnp.broadcast_to(jnp.where(lane_row == depth - 1, 0.0, weight), (8, 128))
    upper = jnp.broadcast_to(jnp.where(lane_row == 0, 0.0, weight), (8, 128))
    top_scale = 0.5 * inv_stretch_at(
        jnp.full((1, 128), total_depth - 1, f32), total_depth
    )
    front = jnp.where(first, 0.0, 1.0)
    for t in range(tiles):
        span = slice(8 * t, 8 * t + 8)
        inv_height = inverse[span, :]
        gathered = jnp.zeros((8, 128), f32)
        for i in range(rows):
            inv = spread_lane(inv_height, i)
            low, high = lower * inv, upper * inv
            work = None
            for q in range(5):
                value = psi[q, i, span, :]
                step = pltpu.roll(value * low, 1, 1) - pltpu.roll(value * high, 127, 1)
                normal[q, i, span, :] = step
                term = flux[q, i, span, :] * step
                work = term if work is None else work + term
            summed = jnp.broadcast_to(jnp.sum(work, axis=1, keepdims=True), (8, 128))
            gathered = jnp.where(lane == i, summed, gathered)

        inside = lane < rows
        surf = facts[0, span, :]
        rho, u1, u2, u3, p = (
            jnp.where(inside, part(surf, q + 1, rows), 1.0) for q in range(5)
        )
        fitted = jnp.where(inside, part(surf, 6, rows), 0.0)
        scale = top_scale * inv_height
        last = tops[span, :]
        s0, s1, s2, s3, s4 = (part(last, q, rows) * scale for q in range(5))
        kinetic, enthalpy = thermo(rho, u1, u2, u3, p)
        fluxes = flux_of(rho, u1, u2, u3, p, enthalpy)
        top_work = (
            fluxes[0] * s0 + fluxes[1] * s1 + fluxes[2] * s2 + fluxes[3] * s3 + fluxes[4] * s4
        )
        dotted = u1 * s1 + u2 * s2 + u3 * s3
        shared = gm * (s3 + u3 * s4)
        common = s0 + dotted + enthalpy * s4
        adjoint = (
            kinetic * s3 - u3 * dotted + u3 * (kinetic - enthalpy) * s4,
            u3 * s1 - u1 * shared,
            u3 * s2 - u2 * shared,
            u3 * s3 - u3 * shared + common,
            gm * s3 + gamma_ratio * u3 * s4,
        )
        heights = facts[1, span, :]
        slopes = facts[2, span, :]
        by_h = sum(adjoint[q] * part(heights, q, rows) for q in range(5))
        by_s = sum(adjoint[q] * part(slopes, q, rows) for q in range(5))
        metric = -inv_height * (gathered + front * top_work)
        term = jnp.where(inside, metric + front * fitted * by_h, 0.0)
        tilt = jnp.where(inside, front * fitted * by_s, 0.0)
        packet[span, 0:128] = (
            packet[span, 0:128] + pltpu.roll(term, 5 * rows, 1) + pltpu.roll(tilt, 6 * rows, 1)
        )

    su_even, sv_even = even("su"), even("sv")
    high_row = rows - 2
    row_a = jnp.where(su_even, high_row, 0)
    row_b = high_row - row_a
    for r in range(2):
        for ref, row in ((su_a, row_a + r), (su_b, row_b + r)):
            for q in range(5):
                ref[q, r] = psi[q, row]
            ref[5, r] = jnp.abs(prim[1, row]) + tone[row]
    for i in range(rows):
        pair = slice(2 * i, 2 * i + 2)
        for q in range(6):
            if q < 5:
                low, high = psi[q, i, 0:2, :], psi[q, i, columns - 2 : columns, :]
            else:
                low = jnp.abs(prim[2, i, 0:2, :]) + tone[i, 0:2, :]
                high = (
                    jnp.abs(prim[2, i, columns - 2 : columns, :])
                    + tone[i, columns - 2 : columns, :]
                )
            sv_a[q, pair, :] = jnp.where(sv_even, high, low)
            sv_b[q, pair, :] = jnp.where(sv_even, low, high)


def join_kernel(rows, tiles, depth, total_depth, surface, fan, *refs):
    own, arrived, inverse = refs[:3]
    chunk, mine = refs[-2:]
    first = lax.axis_index("nrm") == 0
    lane = lanes()
    one = jnp.zeros((1, 128), f32)
    before = 0.5 * inv_stretch_at(one + (depth - 1), total_depth)
    after = 0.5 * inv_stretch_at(one + depth, total_depth)
    own_scale = jnp.where(first, before, after)
    far_scale = jnp.where(first, after, before)
    sign = jnp.where(first, 1.0, -1.0)
    sums = jnp.zeros((8, 128), f32)
    kept = jnp.zeros((8, 128), f32)
    for t in range(tiles):
        span = slice(8 * t, 8 * t + 8)
        near, near_flux = own[span, 0:128], own[span, 128:256]
        far, far_flux = arrived[span, 0:128], arrived[span, 128:256]
        cross = near_flux * (far * far_scale) - far_flux * (near * own_scale)
        cross = jnp.where(lane < 5 * rows, cross, 0.0)
        for d in (1, 2, 4):
            cross = cross + pltpu.roll(cross, rows * d, 1)
        inv_height = inverse[span, :]
        total = near + far
        inside = lane < rows
        term = jnp.where(
            inside, part(total, 5, rows) + sign * inv_height * inv_height * cross, 0.0
        )
        for d in (1, 2, 4, 8):
            term = term + pltpu.roll(term, 128 - d, 1)
        share = term * (1.0 / surface)
        slope = jnp.where(inside, share + part(total, 6, rows), 0.0)
        kept = kept + (pltpu.roll(slope, rows * t, 1) if t else slope)
        sums = jnp.where(lane == t, pltpu.roll(share, t, 1) if t else share, sums)
    mine[...] = kept
    for n in range(fan):
        chunk[n] = sums


def final_kernel(
    rows, tiles, depth, total_depth, su_count, sv_count,
    prim, psi, target, normal, flux, enth, tone, inverse, arrived, mine,
    su_a, su_b, sv_a, sv_b, chunks,
    result, slope,
    wide, along, across, turn, done, sems,
):
    su, sv, nrm = lax.axis_index("su"), lax.axis_index("sv"), lax.axis_index("nrm")
    first = nrm == 0
    lane = lanes()
    columns = 8 * tiles
    ahead = jnp.zeros((8, 128), f32)
    for n in range(su_count):
        ahead = ahead + jnp.where(n > su, chunks[n], 0.0)
    upstream = jnp.zeros((8, 128), f32)
    for t in range(tiles):
        upstream = jnp.where(
            (lane >= rows * t) & (lane < rows * t + rows), spread_lane(ahead, t), upstream
        )
    packed = mine[...] + upstream
    turn[...] = jnp.zeros_like(turn)
    for t in range(tiles):
        turn[8 * t : 8 * t + 8, :] = pltpu.roll(packed, 128 - rows * t, 1) if t else packed
    slope[...] = turn[...].T[0:rows, 0:columns]

    su_even, sv_even = even("su"), even("sv")
    low_on, high_on = su > 0, su < su_count - 1
    for r in range(2):
        for swap, on, row in ((su_even, low_on, r), (~su_even, high_on, rows + 2 + r)):
            pick = lambda q: jnp.where(swap, su_b[q, r], su_a[q, r])
            radius = pick(5)
            for q in range(5):
                value = jnp.where(on, pick(q), 0.0)
                wide[q, row, 8 : 8 + columns, :] = value
                along[q, row] = value * radius
    left_on, right_on = sv > 0, sv < sv_count - 1
    for swap, on, col in ((sv_even, left_on, 6), (~sv_even, right_on, 8 + columns)):
        radius = jnp.where(swap, sv_b[5], sv_a[5])
        for q in range(5):
            value = jnp.where(on, jnp.where(swap, sv_b[q], sv_a[q]), 0.0)
            weighted = value * radius
            for i in range(rows):
                wide[q, i + 2, col : col + 2, :] = value[2 * i : 2 * i + 2]
                across[q, i, col : col + 2, :] = weighted[2 * i : 2 * i + 2]

    @pl.loop(0, rows)
    def _(i):
        for t in range(tiles):
            span = slice(8 * t, 8 * t + 8)
            inner = slice(8 * t + 8, 8 * t + 16)
            sound = tone[i, span, :]
            radius_u = jnp.abs(prim[1, i, span, :]) + sound
            radius_v = jnp.abs(prim[2, i, span, :]) + sound
            for q in range(5):
                value = psi[q, i, span, :]
                wide[q, i + 2, inner, :] = value
                along[q, i + 2, span, :] = radius_u * value
                across[q, i, inner, :] = radius_v * value

    fraction = jnp.broadcast_to(
        ((lanes((1, 128)) + nrm * depth).astype(f32) + 0.5) / total_depth, (8, 128)
    )
    one = jnp.zeros((1, 128), f32)
    edge_scale = jnp.where(
        first,
        -0.5 * inv_stretch_at(one + depth, total_depth),
        0.5 * inv_stretch_at(one + (depth - 1), total_depth),
    )
    entry = jnp.where(first, depth - 1, 0)
    at_entry = lane == entry
    for t in range(tiles):
        span = slice(8 * t, 8 * t + 8)
        repeated = inverse[span, :]
        for d in (1, 2, 4):
            repeated = repeated + pltpu.roll(repeated, rows * d, 1)
        turn[span, :] = arrived[span, 0:128] * edge_scale * repeated

    def out_copy(i):
        return pltpu.make_async_copy(done.at[:, i], result.at[:, i], sems.at[i])

    @pl.loop(0, rows)
    def _(i):
        turned = pltpu.roll(packed, 128 - i, 1)
        for t in range(tiles):
            span = slice(8 * t, 8 * t + 8)
            at = lambda k: slice(8 * t + 8 + k, 8 * t + 16 + k)
            ends = turn[span, :]
            first, second, third, damp = [], [], [], []
            for q in range(5):
                first.append(
                    (8.0 / 12.0) * (wide[q, i + 1, at(0), :] - wide[q, i + 3, at(0), :])
                    - (1.0 / 12.0) * (wide[q, i, at(0), :] - wide[q, i + 4, at(0), :])
                )
                second.append(
                    (8.0 / 12.0) * (wide[q, i + 2, at(-1), :] - wide[q, i + 2, at(1), :])
                    - (1.0 / 12.0) * (wide[q, i + 2, at(-2), :] - wide[q, i + 2, at(2), :])
                )
                far = (
                    along[q, i, span, :] + along[q, i + 4, span, :]
                    + across[q, i, at(-2), :] + across[q, i, at(2), :]
                )
                near = (
                    along[q, i + 1, span, :] + along[q, i + 3, span, :]
                    + across[q, i, at(-1), :] + across[q, i, at(1), :]
                )
                here = along[q, i + 2, span, :] + across[q, i, at(0), :]
                damp.append(
                    damping_coef * far - (4.0 * damping_coef) * near + (6.0 * damping_coef) * here
                )
                came = pltpu.roll(ends, entry + (128 - rows * q) - i, 1)
                third.append(normal[q, i, span, :] + jnp.where(at_entry, came, 0.0))
            u1, u2, u3 = (prim[q, i, span, :] for q in (1, 2, 3))
            enthalpy = enth[i, span, :]
            kinetic = (0.5 * gm) * (u1 * u1 + u2 * u2 + u3 * u3)
            projected = first[1] + second[2] + third[3]
            energy = u1 * first[4] + u2 * second[4] + u3 * third[4]
            dot = lambda g: u1 * g[1] + u2 * g[2] + u3 * g[3]
            dot1, dot2, dot3 = dot(first), dot(second), dot(third)
            mass_row = (
                kinetic * projected
                - (u1 * dot1 + u2 * dot2 + u3 * dot3)
                + (kinetic - enthalpy) * energy
            )
            shared = gm * (projected + energy)
            moved = lambda b: u1 * first[b] + u2 * second[b] + u3 * third[b]
            rows_out = (
                mass_row,
                moved(1) - u1 * shared + (first[0] + dot1 + enthalpy * first[4]),
                moved(2) - u2 * shared + (second[0] + dot2 + enthalpy * second[4]),
                moved(3) - u3 * shared + (third[0] + dot3 + enthalpy * third[4]),
                gm * projected + gamma_ratio * energy,
            )
            ramp = fraction * spread_lane(turned, rows * t)
            for q in range(5):
                done[q, i, span, :] = (
                    target[q, i, span, :] + rows_out[q] + damp[q] + ramp * flux[q, i, span, :]
                )
        out_copy(i).start()

    @pl.loop(0, rows)
    def _(i):
        out_copy(i).wait()


def call(kernel, outs, operands, scratch, flops, name, spaces=None):
    spec = pl.BlockSpec(memory_space=VMEM)
    size = sum(4 * a.size for a in operands) + sum(4 * o.size for o in outs)
    return pl.pallas_call(
        kernel,
        out_shape=outs,
        in_specs=[spec] * len(operands),
        out_specs=[pl.BlockSpec(memory_space=s) for s in (spaces or [VMEM] * len(outs))],
        scratch_shapes=scratch,
        cost_estimate=pl.CostEstimate(flops=flops, transcendentals=0, bytes_accessed=size),
        compiler_params=pltpu.CompilerParams(vmem_limit_bytes=16 << 20),
        name=name,
    )(*operands)


def local(
    primitive, adjoint_state, objective_grad, front_height,
    shock_state, state_by_height, state_by_slope, fitted_flags,
):
    _, rows, columns, depth = adjoint_state.shape
    tiles = columns // 8
    su_count, sv_count, lines = (lax.axis_size(a) for a in ("su", "sv", "nrm"))
    total_depth = depth * lines
    shape = lambda *s: jax.ShapeDtypeStruct(s, f32)
    field = shape(5, rows, columns, depth)
    plane = shape(rows, columns, depth)
    points = 5 * rows * columns * depth

    packet, su_a, su_b, sv_a, sv_b, normal, flux, enth, tone, inverse = call(
        functools.partial(prepare_kernel, rows, tiles, depth, total_depth),
        [
            shape(columns, 256),
            shape(6, 2, columns, depth),
            shape(6, 2, columns, depth),
            shape(6, 2 * rows, depth),
            shape(6, 2 * rows, depth),
            field, field, plane, plane,
            shape(columns, 128),
        ],
        (
            primitive, adjoint_state, front_height,
            shock_state, state_by_height, state_by_slope, fitted_flags,
        ),
        [VMEM((3, 128, 128), f32), VMEM((3, 128, 128), f32), VMEM((columns, 128), f32)],
        12 * points,
        "prepare",
    )

    def pairs(count, shift):
        out = []
        for i in range(0, count, 2):
            a, b = (i + shift) % count, (i + shift + 1) % count
            out += [(a, b), (b, a)]
        return out

    arrived = lax.ppermute(packet, "nrm", [(0, 1), (1, 0)])
    su_a = lax.ppermute(su_a, "su", pairs(su_count, 0))
    su_b = lax.ppermute(su_b, "su", pairs(su_count, 1))
    sv_a = lax.ppermute(sv_a, "sv", pairs(sv_count, 0))
    sv_b = lax.ppermute(sv_b, "sv", pairs(sv_count, 1))

    chunk, mine = call(
        functools.partial(
            join_kernel, rows, tiles, depth, total_depth, rows * su_count, su_count
        ),
        [shape(su_count, 8, 128), shape(8, 128)],
        (packet, arrived, inverse, su_a, su_b, sv_a, sv_b),
        [],
        points // 40,
        "join",
    )
    chunks = lax.all_to_all(chunk, "su", 0, 0)
    result, slope = call(
        functools.partial(
            final_kernel, rows, tiles, depth, total_depth, su_count, sv_count
        ),
        [field, shape(rows, columns)],
        (
            primitive, adjoint_state, objective_grad, normal, flux, enth, tone, inverse,
            arrived, mine, su_a, su_b, sv_a, sv_b, chunks,
        ),
        [
            VMEM((5, rows + 4, columns + 16, depth), f32),
            VMEM((5, rows + 4, columns, depth), f32),
            VMEM((5, rows, columns + 16, depth), f32),
            VMEM((128, 128), f32),
            VMEM((5, rows, columns, depth), f32),
            pltpu.SemaphoreType.DMA((rows,)),
        ],
        40 * points,
        "final",
        [pltpu.HBM, VMEM],
    )
    return result, slope


def solution(mesh):
    wide = P(None, "su", "sv", "nrm")
    flat = P("su", "sv")
    front = P(None, "su", "sv")
    return jax.shard_map(
        local,
        mesh=mesh,
        in_specs=(wide, wide, wide, flat, front, front, front, flat),
        out_specs=(wide, flat),
        check_vma=False,
    )
```

time: 59.6 us -> 51.6 us (0.87)
  the two profiles are of different devices: /device:TPU:30 before, /device:TPU:1 now
where the time goes in v2:
time: 51.6 us; the launch traced here: 51.1 us
  blocking collectives  17.8 us (34%)
  Pallas kernels  14.4 us (28%)
  starting transfers between devices  10.3 us (20%)
  local copies, waits for them, and re-layouts  6.59 us (13%)
  waiting for transfers between devices  1.4 us (3%)
  between operations  0.68 us (1%)
    all_to_all x1, blocking collectives, local(): chunks = lax.all_to_all(chunk, 'su', 0, 0)  17.8 us
    pallas_call x3, Pallas kernels, call(): pl.pallas_call(kernel, out_shape=outs, in_specs=[spec] * len(operands), o...  14.4 us
    unnamed x18, local copies, waits for them, and re-layouts  6.59 us
    ppermute x1, starting transfers between devices, local(): arrived = lax.ppermute(packet, 'nrm', [(0, 1), (1, 0)])  3.38 us
    ppermute x1, starting transfers between devices, local(): su_a = lax.ppermute(su_a, 'su', pairs(su_count, 0))  3.33 us
    ppermute x1, starting transfers between devices, local(): sv_b = lax.ppermute(sv_b, 'sv', pairs(sv_count, 1))  2.36 us
    ppermute x1, waiting for transfers between devices, local(): arrived = lax.ppermute(packet, 'nrm', [(0, 1), (1, 0)])  1.39 us
    ppermute x1, starting transfers between devices, local(): sv_a = lax.ppermute(sv_a, 'sv', pairs(sv_count, 0))  1.18 us
  transfers between devices with their start and end apart: 5, of which 1 were waited for; matrix products, arithmetic and copies ran while one was open for 0% of the time, Pallas kernels for 0%

profile of v2, /device:TPU:1, one launch (start us, length us, event | category | flops | bytes accessed | tf_op | source)
XLA Modules:
  0.0 51.1 jit_solution(9738905063310402597)
XLA Ops:
  0.6 0.0 copy-start
  0.6 1.4 %copy-done = f32[5,16,40,128]{3,2,1,0:T(8,128)S(1)} copy-done((f32[5,16,40,128]{3,2,1,0:T(8,128)S(1)}, f32[5,16,40,128]{3,2,1,0:T(8,128)}, u32[]{:S(2)}) %copy-start) | copy-done | bytes 1638424
  2.1 0.0 copy-start.2
  2.1 1.4 %copy-done.2 = f32[5,16,40,128]{3,2,1,0:T(8,128)S(1)} copy-done((f32[5,16,40,128]{3,2,1,0:T(8,128)S(1)}, f32[5,16,40,128]{3,2,1,0:T(8,128)}, u32[]{:S(2)}) %copy-start.2) | copy-done | bytes 1638424
  3.5 0.0 copy-start.4
  3.5 0.8 %copy-done.4 = f32[5,16,40]{2,1,0:T(8,128)S(1)} copy-done((f32[5,16,40]{2,1,0:T(8,128)S(1)}, f32[5,16,40]{2,1,0:T(8,128)}, u32[]{:S(2)}) %copy-start.4) | copy-done | bytes 12824
  4.3 0.0 copy-start.5
  4.3 0.8 %copy-done.5 = f32[5,16,40]{2,1,0:T(8,128)S(1)} copy-done((f32[5,16,40]{2,1,0:T(8,128)S(1)}, f32[5,16,40]{2,1,0:T(8,128)}, u32[]{:S(2)}) %copy-start.5) | copy-done | bytes 12824
  5.1 0.0 copy-start.6
  5.1 0.8 %copy-done.6 = f32[5,16,40]{2,1,0:T(8,128)S(1)} copy-done((f32[5,16,40]{2,1,0:T(8,128)S(1)}, f32[5,16,40]{2,1,0:T(8,128)}, u32[]{:S(2)}) %copy-start.6) | copy-done | bytes 12824
  5.8 0.0 copy-start.7
  5.8 0.7 %copy-done.7 = f32[16,40]{1,0:T(8,128)S(1)} copy-done((f32[16,40]{1,0:T(8,128)S(1)}, f32[16,40]{1,0:T(8,128)}, u32[]{:S(2)}) %copy-start.7) | copy-done | bytes 2584
  6.5 0.0 copy-start.8
  6.5 0.7 %copy-done.8 = s32[16,40]{1,0:T(8,128)S(1)} copy-done((s32[16,40]{1,0:T(8,128)S(1)}, s32[16,40]{1,0:T(8,128)}, u32[]{:S(2)}) %copy-start.8) | copy-done | bytes 2584
  7.2 0.0 copy-start.1
  7.2 0.0 copy-start.3
  7.2 8.4 %prepare.1 = (f32[40,256]{1,0:T(8,128)S(1)}, f32[6,2,40,128]{3,2,1,0:T(8,128)S(1)}, f32[6,2,40,128]{3,2,1,0:T(8,128)S(1)}, f32[6,32,128]{2,1,0:T(8,128)S(1)}, f3...) custom-call(f32[5,16,40,128]{3,2,1,0:T(8,128)S(1)} %copy-done, ...), custom_call_target="tpu_custom_call" | custom-call | flops 4915200 | bytes 8002048 | tf_op jit(solution)/shard_map/prepare/pallas_call | solution.py:383
  15.7 3.3 %collective-permute-start.1 = (f32[6,2,40,128]{3,2,1,0:T(8,128)S(1)}, f32[6,2,40,128]{3,2,1,0:T(8,128)S(1)}, u32[]{:S(2)}, u32[]{:S(2)}) collective-permute-start(f32[6,2,40,128]{3,2,1,0:T(8,128)S(1)} %get-tuple-element.20), channel_id=1, source_target_pairs={{0,16},{16,0},{32,48},{48,32},{64,80},{80,64},{96,112},{112,96},{1... | collective-permute-start | bytes 737288 | tf_op jit(solution)/shard_map/ppermute | solution.py:436
  19.0 0.0 collective-permute-start.2
  19.0 1.2 %collective-permute-start.3 = (f32[6,32,128]{2,1,0:T(8,128)S(1)}, f32[6,32,128]{2,1,0:T(8,128)S(1)}, u32[]{:S(2)}, u32[]{:S(2)}) collective-permute-start(f32[6,32,128]{2,1,0:T(8,128)S(1)} %get-tuple-element.22), channel_id=1, source_target_pairs={{0,2},{2,0},{4,6},{6,4},{8,10},{10,8},{12,14},{14,12},{1,3},{3,1},... | collective-permute-start | bytes 294920 | tf_op jit(solution)/shard_map/ppermute | solution.py:438
  20.2 2.4 %collective-permute-start.4 = (f32[6,32,128]{2,1,0:T(8,128)S(1)}, f32[6,32,128]{2,1,0:T(8,128)S(1)}, u32[]{:S(2)}, u32[]{:S(2)}) collective-permute-start(f32[6,32,128]{2,1,0:T(8,128)S(1)} %get-tuple-element.23), channel_id=1, source_target_pairs={{2,4},{4,2},{6,8},{8,6},{10,12},{12,10},{14,0},{0,14},{3,5},{5,3},... | collective-permute-start | bytes 294920 | tf_op jit(solution)/shard_map/ppermute | solution.py:439
  22.5 3.4 %collective-permute-start = (f32[40,256]{1,0:T(8,128)S(1)}, f32[40,256]{1,0:T(8,128)S(1)}, u32[]{:S(2)}, u32[]{:S(2)}) collective-permute-start(f32[40,256]{1,0:T(8,128)S(1)} %get-tuple-element.19.refs_0_), channel_id=1, source_target_pairs={{0,1},{1,0},{2,3},{3,2},{4,5},{5,4},{6,7},{7,6},{8,9},{9,8},{10,11... | collective-permute-start | bytes 122888 | tf_op jit(solution)/shard_map/ppermute | solution.py:435
  25.9 1.4 %collective-permute-done.refs_1_.arrived = f32[40,256]{1,0:T(8,128)S(1)} collective-permute-done((f32[40,256]{1,0:T(8,128)S(1)}, f32[40,256]{1,0:T(8,128)S(1)}, u32[]{:S(2)}, u32[]{:S(2)}) %collective-permute-start) | collective-permute-done | bytes 40992 | tf_op jit(solution)/shard_map/ppermute | solution.py:435
  27.3 0.0 collective-permute-done.3.refs_5_.sv_a
  27.3 0.0 collective-permute-done.4.refs_6_.sv_b
  27.3 0.0 collective-permute-done.1.refs_3_.su_a
  27.3 0.0 collective-permute-done.2.refs_4_.su_b
  27.3 0.6 %join.1 = (f32[16,8,128]{2,1,0:T(8,128)S(1)}, f32[8,128]{1,0:T(8,128)S(1)}) custom-call(f32[40,256]{1,0:T(8,128)S(1)} %get-tuple-element.19.refs_0_, f32[40,256]{1,0:T(8,128)S(1)} %collective-permute-done.refs_1_.arrived, f32[40,128]{1,0:T(8,128)S(1)} %get-tuple-element.18.refs_2_.inverse, f32[6,2,40,128]{3,2,1,0:T(8,128)S(1)} %collective-permute-done.1.refs_3_.su_a, ...), custom_call_target="tpu_custom_call" | custom-call | flops 10240 | bytes 860160 | tf_op jit(solution)/shard_map/join/pallas_call | solution.py:383
  27.9 17.8 %all_to_all.5.chunks = f32[16,8,128]{2,1,0:T(8,128)S(1)} all-to-all(f32[16,8,128]{2,1,0:T(8,128)S(1)} %get-tuple-element.25), channel_id=1, replica_groups=mesh['su'=16,'sv'=8,'nrm'=2] {'su'}, dimensions={0} | all-to-all | bytes 131072 | tf_op jit(solution)/shard_map/all_to_all | solution.py:451
  45.7 0.0 copy-done.1
  45.7 0.0 copy-done.3
  45.7 5.4 %final.1 = (f32[5,16,40,128]{3,2,1,0:T(8,128)}, f32[16,40]{1,0:T(8,128)}) custom-call(f32[5,16,40,128]{3,2,1,0:T(8,128)S(1)} %copy-done.1, f32[5,16,40,128]{3,2,1,0:T(8,128)S(1)} %copy-done.2, f32[5,16,40,128]{3,2,1,0:T(8,128)S(1)} %copy-done.3, f32[5,16,40,128]{3,2,1,0:T(8,128)S(1)} %get-tuple-element.14.normal, ...), custom_call_target="tpu_custom_call" | custom-call | flops 16384000 | bytes 11307520 | tf_op jit(solution)/shard_map/final/pallas_call | solution.py:383
Async XLA Ops:
  0.6 1.4 %copy-start = (f32[5,16,40,128]{3,2,1,0:T(8,128)S(1)}, f32[5,16,40,128]{3,2,1,0:T(8,128)}, u32[]{:S(2)}) copy-start(f32[5,16,40,128]{3,2,1,0:T(8,128)} %prim.3) | copy-start | bytes 4915204
  2.1 1.4 %copy-start.2 = (f32[5,16,40,128]{3,2,1,0:T(8,128)S(1)}, f32[5,16,40,128]{3,2,1,0:T(8,128)}, u32[]{:S(2)}) copy-start(f32[5,16,40,128]{3,2,1,0:T(8,128)} %psi.3) | copy-start | bytes 4915204
  3.5 0.8 %copy-start.4 = (f32[5,16,40]{2,1,0:T(8,128)S(1)}, f32[5,16,40]{2,1,0:T(8,128)}, u32[]{:S(2)}) copy-start(f32[5,16,40]{2,1,0:T(8,128)} %shock.1) | copy-start | bytes 38404
  4.3 0.8 %copy-start.5 = (f32[5,16,40]{2,1,0:T(8,128)S(1)}, f32[5,16,40]{2,1,0:T(8,128)}, u32[]{:S(2)}) copy-start(f32[5,16,40]{2,1,0:T(8,128)} %by_height.1) | copy-start | bytes 38404
  5.1 0.8 %copy-start.6 = (f32[5,16,40]{2,1,0:T(8,128)S(1)}, f32[5,16,40]{2,1,0:T(8,128)}, u32[]{:S(2)}) copy-start(f32[5,16,40]{2,1,0:T(8,128)} %by_slope.1) | copy-start | bytes 38404
  5.8 0.7 %copy-start.7 = (f32[16,40]{1,0:T(8,128)S(1)}, f32[16,40]{1,0:T(8,128)}, u32[]{:S(2)}) copy-start(f32[16,40]{1,0:T(8,128)} %height.1) | copy-start | bytes 7684
  6.5 0.7 %copy-start.8 = (s32[16,40]{1,0:T(8,128)S(1)}, s32[16,40]{1,0:T(8,128)}, u32[]{:S(2)}) copy-start(s32[16,40]{1,0:T(8,128)} %flags.1) | copy-start | bytes 7684
  7.2 38.5 %copy-start.1 = (f32[5,16,40,128]{3,2,1,0:T(8,128)S(1)}, f32[5,16,40,128]{3,2,1,0:T(8,128)}, u32[]{:S(2)}) copy-start(f32[5,16,40,128]{3,2,1,0:T(8,128)} %prim.3) | copy-start | bytes 4915204
  7.2 38.5 %copy-start.3 = (f32[5,16,40,128]{3,2,1,0:T(8,128)S(1)}, f32[5,16,40,128]{3,2,1,0:T(8,128)}, u32[]{:S(2)}) copy-start(f32[5,16,40,128]{3,2,1,0:T(8,128)} %target.1) | copy-start | bytes 4915204
  15.7 11.7 %collective-permute-start.1 = (f32[6,2,40,128]{3,2,1,0:T(8,128)S(1)}, f32[6,2,40,128]{3,2,1,0:T(8,128)S(1)}, u32[]{:S(2)}, u32[]{:S(2)}) collective-permute-start(f32[6,2,40,128]{3,2,1,0:T(8,128)S(1)} %get-tuple-element.20), channel_id=1, source_target_pairs={{0,16},{16,0},{32,48},{48,32},{64,80},{80,64},{96,112},{112,96},{1... | collective-permute-start | bytes 737288 | tf_op jit(solution)/shard_map/ppermute | solution.py:436
  19.0 8.3 %collective-permute-start.2 = (f32[6,2,40,128]{3,2,1,0:T(8,128)S(1)}, f32[6,2,40,128]{3,2,1,0:T(8,128)S(1)}, u32[]{:S(2)}, u32[]{:S(2)}) collective-permute-start(f32[6,2,40,128]{3,2,1,0:T(8,128)S(1)} %get-tuple-element.21), channel_id=1, source_target_pairs={{16,32},{32,16},{48,64},{64,48},{80,96},{96,80},{112,128},{128,112... | collective-permute-start | bytes 737288 | tf_op jit(solution)/shard_map/ppermute | solution.py:437
  19.0 8.3 %collective-permute-start.3 = (f32[6,32,128]{2,1,0:T(8,128)S(1)}, f32[6,32,128]{2,1,0:T(8,128)S(1)}, u32[]{:S(2)}, u32[]{:S(2)}) collective-permute-start(f32[6,32,128]{2,1,0:T(8,128)S(1)} %get-tuple-element.22), channel_id=1, source_target_pairs={{0,2},{2,0},{4,6},{6,4},{8,10},{10,8},{12,14},{14,12},{1,3},{3,1},... | collective-permute-start | bytes 294920 | tf_op jit(solution)/shard_map/ppermute | solution.py:438
  20.2 7.1 %collective-permute-start.4 = (f32[6,32,128]{2,1,0:T(8,128)S(1)}, f32[6,32,128]{2,1,0:T(8,128)S(1)}, u32[]{:S(2)}, u32[]{:S(2)}) collective-permute-start(f32[6,32,128]{2,1,0:T(8,128)S(1)} %get-tuple-element.23), channel_id=1, source_target_pairs={{2,4},{4,2},{6,8},{8,6},{10,12},{12,10},{14,0},{0,14},{3,5},{5,3},... | collective-permute-start | bytes 294920 | tf_op jit(solution)/shard_map/ppermute | solution.py:439
  22.5 4.8 %collective-permute-start = (f32[40,256]{1,0:T(8,128)S(1)}, f32[40,256]{1,0:T(8,128)S(1)}, u32[]{:S(2)}, u32[]{:S(2)}) collective-permute-start(f32[40,256]{1,0:T(8,128)S(1)} %get-tuple-element.19.refs_0_), channel_id=1, source_target_pairs={{0,1},{1,0},{2,3},{3,2},{4,5},{5,4},{6,7},{7,6},{8,9},{9,8},{10,11... | collective-permute-start | bytes 122888 | tf_op jit(solution)/shard_map/ppermute | solution.py:435

commit v3 on v2

--- a/solution.py
+++ b/solution.py
@@ -46,19 +46,60 @@
 
 
 def prepare_kernel(
-    rows, tiles, depth, total_depth,
-    prim, psi, height, shock, by_height, by_slope, flags,
-    packet, su_a, su_b, sv_a, sv_b, normal, flux, enth, tone, inverse,
-    turn, facts, tops,
+    rows, tiles, depth, total_depth, step_rows,
+    prim_far, psi_far, height_far, shock_far, by_height_far, by_slope_far, flags_far,
+    packet, su_a, su_b, sv_a, sv_b, normal, flux, enth, tone, inverse, prim, psi,
+    turn, facts, tops, spread, work, height, shock, by_height, by_slope, flags, small, large,
 ):
+    surfaces = [
+        pltpu.make_async_copy(far, near, small.at[n])
+        for n, (far, near) in enumerate(
+            (
+                (height_far, height),
+                (shock_far, shock),
+                (by_height_far, by_height),
+                (by_slope_far, by_slope),
+                (flags_far, flags),
+            )
+        )
+    ]
+    chunks = rows // step_rows
+    loads = []
+    for c in range(chunks):
+        part_rows = pl.ds(c * step_rows, step_rows)
+        loads.append(
+            [
+                pltpu.make_async_copy(far.at[:, part_rows], near.at[:, part_rows], large.at[n, c])
+                for n, (far, near) in enumerate(((prim_far, prim), (psi_far, psi)))
+            ]
+        )
+    for copy in surfaces:
+        copy.start()
+    for pair in loads:
+        for copy in pair:
+            copy.start()
+
     nrm = lax.axis_index("nrm")
     first = nrm == 0
     lane = lanes()
     lane_row = lanes((1, 128))
     columns = 8 * tiles
+    spans = [slice(8 * t, 8 * t + 8) for t in range(tiles)]
+    depth_index = (lane_row + nrm * depth).astype(f32)
+    weight = 0.5 * inv_stretch_at(depth_index, total_depth)
+    lower = jnp.broadcast_to(jnp.where(lane_row == depth - 1, 0.0, weight), (8, 128))
+    upper = jnp.broadcast_to(jnp.where(lane_row == 0, 0.0, weight), (8, 128))
+    top_scale = 0.5 * inv_stretch_at(
+        jnp.full((1, 128), total_depth - 1, f32), total_depth
+    )
+    front = jnp.where(first, 0.0, 1.0)
+    extra = jnp.where(first, 1, 0)
 
     turn[...] = jnp.zeros_like(turn)
     tops[...] = jnp.zeros_like(tops)
+    packet[...] = jnp.zeros_like(packet)
+    for copy in surfaces:
+        copy.wait()
     for place, array in enumerate(
         [height[...]]
         + [shock[q] for q in range(5)]
@@ -70,39 +111,53 @@
         turn[2, rows * q : rows * q + rows, 0:columns] = by_slope[q]
     for n in range(3):
         facts[n] = turn[n].T
-    for t in range(tiles):
-        span = slice(8 * t, 8 * t + 8)
+    for span in spans:
         inverse[span, :] = jnp.where(
             lane < rows, 1.0 / jnp.where(lane < rows, facts[0, span, :], 1.0), 0.0
         )
-
-    for t in range(tiles):
-        span = slice(8 * t, 8 * t + 8)
+    for span in spans:
+        inv_height = inverse[span, :]
         for i in range(rows):
-            rho, u1, u2, u3, p = (prim[q, i, span, :] for q in range(5))
-            ratio = p / rho
-            enthalpy = (gamma_ratio / gm) * ratio + 0.5 * (u1 * u1 + u2 * u2 + u3 * u3)
-            for q, value in enumerate(flux_of(rho, u1, u2, u3, p, enthalpy)):
-                flux[q, i, span, :] = value
-            enth[i, span, :] = enthalpy
-            tone[i, span, :] = jnp.sqrt(gamma_ratio * ratio)
-
-    extra = jnp.where(first, 1, 0)
-    for t in range(tiles):
-        span = slice(8 * t, 8 * t + 8)
-        for half, ref in ((0, psi), (1, flux)):
-            packed = jnp.zeros((8, 128), f32)
-            for q in range(5):
-                for i in range(rows):
-                    spot = rows * q + i
-                    moved = pltpu.roll(ref[q, i, span, :], spot + extra, 1)
-                    packed = jnp.where(lane == spot, moved, packed)
-            packet[span, 128 * half : 128 * half + 128] = packed
+            spread[i, span, :] = spread_lane(inv_height, i)
+
+    for c in range(chunks):
+        for copy in loads[c]:
+            copy.wait()
+        mine = range(c * step_rows, (c + 1) * step_rows)
+        for i in mine:
+            for span in spans:
+                rho, u1, u2, u3, p = (prim[q, i, span, :] for q in range(5))
+                ratio = p / rho
+                enthalpy = (gamma_ratio / gm) * ratio + 0.5 * (u1 * u1 + u2 * u2 + u3 * u3)
+                for q, value in enumerate(flux_of(rho, u1, u2, u3, p, enthalpy)):
+                    flux[q, i, span, :] = value
+                enth[i, span, :] = enthalpy
+                tone[i, span, :] = jnp.sqrt(gamma_ratio * ratio)
+        for i in mine:
+            for span in spans:
+                inv = spread[i, span, :]
+                low, high = lower * inv, upper * inv
+                total = None
+                for q in range(5):
+                    value = psi[q, i, span, :]
+                    step = pltpu.roll(value * low, 1, 1) - pltpu.roll(value * high, 127, 1)
+                    normal[q, i, span, :] = step
+                    term = flux[q, i, span, :] * step
+                    total = term if total is None else total + term
+                work[i, span, :] = total
+        for span in spans:
+            for half, ref in ((0, psi), (1, flux)):
+                packed = packet[span, 128 * half : 128 * half + 128]
+                for q in range(5):
+                    for i in mine:
+                        spot = rows * q + i
+                        moved = pltpu.roll(ref[q, i, span, :], spot + extra, 1)
+                        packed = jnp.where(lane == spot, moved, packed)
+                packet[span, 128 * half : 128 * half + 128] = packed
 
     @pl.when(jnp.logical_not(first))
     def _():
-        for t in range(tiles):
-            span = slice(8 * t, 8 * t + 8)
+        for span in spans:
             packed = jnp.zeros((8, 128), f32)
             for q in range(5):
                 for i in range(rows):
@@ -111,31 +166,16 @@
                     packed = jnp.where(lane == spot, moved, packed)
             tops[span, :] = packed
 
-    depth_index = (lane_row + nrm * depth).astype(f32)
-    weight = 0.5 * inv_stretch_at(depth_index, total_depth)
-    lower = jnp.broadcast_to(jnp.where(lane_row == depth - 1, 0.0, weight), (8, 128))
-    upper = jnp.broadcast_to(jnp.where(lane_row == 0, 0.0, weight), (8, 128))
-    top_scale = 0.5 * inv_stretch_at(
-        jnp.full((1, 128), total_depth - 1, f32), total_depth
-    )
-    front = jnp.where(first, 0.0, 1.0)
-    for t in range(tiles):
-        span = slice(8 * t, 8 * t + 8)
-        inv_height = inverse[span, :]
+    for span in spans:
         gathered = jnp.zeros((8, 128), f32)
         for i in range(rows):
-            inv = spread_lane(inv_height, i)
-            low, high = lower * inv, upper * inv
-            work = None
-            for q in range(5):
-                value = psi[q, i, span, :]
-                step = pltpu.roll(value * low, 1, 1) - pltpu.roll(value * high, 127, 1)
-                normal[q, i, span, :] = step
-                term = flux[q, i, span, :] * step
-                work = term if work is None else work + term
-            summed = jnp.broadcast_to(jnp.sum(work, axis=1, keepdims=True), (8, 128))
-            gathered = jnp.where(lane == i, summed, gathered)
-
+            total = jnp.sum(work[i, span, :], axis=1, keepdims=True)
+            gathered = jnp.where(lane == i, jnp.broadcast_to(total, (8, 128)), gathered)
+        turn[0, span, :] = gathered
+
+    for span in spans:
+        inv_height = inverse[span, :]
+        gathered = turn[0, span, :]
         inside = lane < rows
         surf = facts[0, span, :]
         rho, u1, u2, u3, p = (
@@ -235,11 +275,21 @@
 
 def final_kernel(
     rows, tiles, depth, total_depth, su_count, sv_count,
-    prim, psi, target, normal, flux, enth, tone, inverse, arrived, mine,
+    prim, psi, target_far, normal, flux, enth, tone, inverse, arrived, mine,
     su_a, su_b, sv_a, sv_b, chunks,
     result, slope,
-    wide, along, across, turn, done, sems,
+    wide, along, across, turn, done, target, sems, large,
 ):
+    step_rows = 4
+    loads = [
+        pltpu.make_async_copy(
+            target_far.at[:, pl.ds(r, step_rows)], target.at[:, pl.ds(r, step_rows)],
+            large.at[r // step_rows],
+        )
+        for r in range(0, rows, step_rows)
+    ]
+    for copy in loads:
+        copy.start()
     su, sv, nrm = lax.axis_index("su"), lax.axis_index("sv"), lax.axis_index("nrm")
     first = nrm == 0
     lane = lanes()
@@ -313,8 +363,7 @@
     def out_copy(i):
         return pltpu.make_async_copy(done.at[:, i], result.at[:, i], sems.at[i])
 
-    @pl.loop(0, rows)
-    def _(i):
+    def finish(i):
         turned = pltpu.roll(packed, 128 - i, 1)
         for t in range(tiles):
             span = slice(8 * t, 8 * t + 8)
@@ -372,18 +421,26 @@
                 )
         out_copy(i).start()
 
+    for c, copy in enumerate(loads):
+        copy.wait()
+        pl.loop(c * step_rows, (c + 1) * step_rows)(finish)
+
     @pl.loop(0, rows)
     def _(i):
         out_copy(i).wait()
 
 
-def call(kernel, outs, operands, scratch, flops, name, spaces=None):
-    spec = pl.BlockSpec(memory_space=VMEM)
+def call(kernel, outs, operands, scratch, flops, name, spaces=None, far=()):
+    spec = lambda n: pl.BlockSpec(memory_space=pltpu.HBM if n in far else VMEM)
     size = sum(4 * a.size for a in operands) + sum(4 * o.size for o in outs)
+    operands = [
+        pltpu.with_memory_space_constraint(a, pltpu.HBM) if n in far else a
+        for n, a in enumerate(operands)
+    ]
     return pl.pallas_call(
         kernel,
         out_shape=outs,
-        in_specs=[spec] * len(operands),
+        in_specs=[spec(n) for n in range(len(operands))],
         out_specs=[pl.BlockSpec(memory_space=s) for s in (spaces or [VMEM] * len(outs))],
         scratch_shapes=scratch,
         cost_estimate=pl.CostEstimate(flops=flops, transcendentals=0, bytes_accessed=size),
@@ -405,8 +462,8 @@
     plane = shape(rows, columns, depth)
     points = 5 * rows * columns * depth
 
-    packet, su_a, su_b, sv_a, sv_b, normal, flux, enth, tone, inverse = call(
-        functools.partial(prepare_kernel, rows, tiles, depth, total_depth),
+    packet, su_a, su_b, sv_a, sv_b, normal, flux, enth, tone, inverse, prim, psi = call(
+        functools.partial(prepare_kernel, rows, tiles, depth, total_depth, rows // 4),
         [
             shape(columns, 256),
             shape(6, 2, columns, depth),
@@ -415,14 +472,29 @@
             shape(6, 2 * rows, depth),
             field, field, plane, plane,
             shape(columns, 128),
+            field, field,
         ],
         (
             primitive, adjoint_state, front_height,
             shock_state, state_by_height, state_by_slope, fitted_flags,
         ),
-        [VMEM((3, 128, 128), f32), VMEM((3, 128, 128), f32), VMEM((columns, 128), f32)],
+        [
+            VMEM((3, 128, 128), f32),
+            VMEM((3, 128, 128), f32),
+            VMEM((columns, 128), f32),
+            VMEM((rows, columns, depth), f32),
+            VMEM((rows, columns, depth), f32),
+            VMEM((rows, columns), f32),
+            VMEM((5, rows, columns), f32),
+            VMEM((5, rows, columns), f32),
+            VMEM((5, rows, columns), f32),
+            VMEM((rows, columns), jnp.int32),
+            pltpu.SemaphoreType.DMA((5,)),
+            pltpu.SemaphoreType.DMA((2, 4)),
+        ],
         12 * points,
         "prepare",
+        far=range(7),
     )
 
     def pairs(count, shift):
@@ -455,7 +527,7 @@
         ),
         [field, shape(rows, columns)],
         (
-            primitive, adjoint_state, objective_grad, normal, flux, enth, tone, inverse,
+            prim, psi, objective_grad, normal, flux, enth, tone, inverse,
             arrived, mine, su_a, su_b, sv_a, sv_b, chunks,
         ),
         [
@@ -464,11 +536,14 @@
             VMEM((5, rows, columns + 16, depth), f32),
             VMEM((128, 128), f32),
             VMEM((5, rows, columns, depth), f32),
+            VMEM((5, rows, columns, depth), f32),
             pltpu.SemaphoreType.DMA((rows,)),
+            pltpu.SemaphoreType.DMA((4,)),
         ],
         40 * points,
         "final",
         [pltpu.HBM, VMEM],
+        far=(2,),
     )
     return result, slope
 

time: 51.6 us -> 40.8 us (0.79)
  local copies, waits for them, and re-layouts: 6.59 us -> 0 us
  Pallas kernels: 14.4 us -> 10.6 us
    unnamed x18 -> x0, local copies, waits for them, and re-layouts: 6.59 us -> none
    pallas_call x3, Pallas kernels: 14.4 us -> 10.6 us  [call(): pl.pallas_call(kernel, out_shape=outs, in_specs=[spec(n) for n in range(l...]
where the time goes in v3:
time: 40.8 us; the launch traced here: 40.7 us
  blocking collectives  17.8 us (44%)
  Pallas kernels  10.6 us (26%)
  starting transfers between devices  10.3 us (25%)
  waiting for transfers between devices  1.4 us (3%)
  between operations  0.66 us (2%)
    all_to_all x1, blocking collectives, local(): chunks = lax.all_to_all(chunk, 'su', 0, 0)  17.8 us
    pallas_call x3, Pallas kernels, call(): pl.pallas_call(kernel, out_shape=outs, in_specs=[spec(n) for n in range(l...  10.6 us
    ppermute x1, starting transfers between devices, local(): arrived = lax.ppermute(packet, 'nrm', [(0, 1), (1, 0)])  3.38 us
    ppermute x1, starting transfers between devices, local(): su_a = lax.ppermute(su_a, 'su', pairs(su_count, 0))  3.33 us
    ppermute x1, starting transfers between devices, local(): sv_b = lax.ppermute(sv_b, 'sv', pairs(sv_count, 1))  2.36 us
    ppermute x1, waiting for transfers between devices, local(): arrived = lax.ppermute(packet, 'nrm', [(0, 1), (1, 0)])  1.39 us
    ppermute x1, starting transfers between devices, local(): sv_a = lax.ppermute(sv_a, 'sv', pairs(sv_count, 0))  1.18 us
  transfers between devices with their start and end apart: 5, of which 1 were waited for; matrix products, arithmetic and copies ran while one was open for 0% of the time, Pallas kernels for 0%

profile of v3, /device:TPU:1, one launch (start us, length us, event | category | flops | bytes accessed | tf_op | source)
XLA Modules:
  0.0 40.7 jit_solution(4579427734739996591)
XLA Ops:
  0.6 4.3 %prepare.1 = (f32[40,256]{1,0:T(8,128)S(1)}, f32[6,2,40,128]{3,2,1,0:T(8,128)S(1)}, f32[6,2,40,128]{3,2,1,0:T(8,128)S(1)}, f32[6,32,128]{2,1,0:T(8,128)S(1)}, f3...) custom-call(f32[5,16,40,128]{3,2,1,0:T(8,128)} %prim_far.1, ...), custom_call_target="tpu_custom_call" | custom-call | flops 4915200 | bytes 11278848 | tf_op jit(solution)/shard_map/prepare/pallas_call | solution.py:440
  5.0 3.3 %collective-permute-start.1 = (f32[6,2,40,128]{3,2,1,0:T(8,128)S(1)}, f32[6,2,40,128]{3,2,1,0:T(8,128)S(1)}, u32[]{:S(2)}, u32[]{:S(2)}) collective-permute-start(f32[6,2,40,128]{3,2,1,0:T(8,128)S(1)} %get-tuple-element.24), channel_id=1, source_target_pairs={{0,16},{16,0},{32,48},{48,32},{64,80},{80,64},{96,112},{112,96},{1... | collective-permute-start | bytes 737288 | tf_op jit(solution)/shard_map/ppermute | solution.py:508
  8.3 0.0 collective-permute-start.2
  8.3 1.2 %collective-permute-start.3 = (f32[6,32,128]{2,1,0:T(8,128)S(1)}, f32[6,32,128]{2,1,0:T(8,128)S(1)}, u32[]{:S(2)}, u32[]{:S(2)}) collective-permute-start(f32[6,32,128]{2,1,0:T(8,128)S(1)} %get-tuple-element.26), channel_id=1, source_target_pairs={{0,2},{2,0},{4,6},{6,4},{8,10},{10,8},{12,14},{14,12},{1,3},{3,1},... | collective-permute-start | bytes 294920 | tf_op jit(solution)/shard_map/ppermute | solution.py:510
  9.5 2.4 %collective-permute-start.4 = (f32[6,32,128]{2,1,0:T(8,128)S(1)}, f32[6,32,128]{2,1,0:T(8,128)S(1)}, u32[]{:S(2)}, u32[]{:S(2)}) collective-permute-start(f32[6,32,128]{2,1,0:T(8,128)S(1)} %get-tuple-element.27), channel_id=1, source_target_pairs={{2,4},{4,2},{6,8},{8,6},{10,12},{12,10},{14,0},{0,14},{3,5},{5,3},... | collective-permute-start | bytes 294920 | tf_op jit(solution)/shard_map/ppermute | solution.py:511
  11.8 3.4 %collective-permute-start = (f32[40,256]{1,0:T(8,128)S(1)}, f32[40,256]{1,0:T(8,128)S(1)}, u32[]{:S(2)}, u32[]{:S(2)}) collective-permute-start(f32[40,256]{1,0:T(8,128)S(1)} %get-tuple-element.23.refs_0_), channel_id=1, source_target_pairs={{0,1},{1,0},{2,3},{3,2},{4,5},{5,4},{6,7},{7,6},{8,9},{9,8},{10,11... | collective-permute-start | bytes 122888 | tf_op jit(solution)/shard_map/ppermute | solution.py:507
  15.2 1.4 %collective-permute-done.refs_1_.arrived = f32[40,256]{1,0:T(8,128)S(1)} collective-permute-done((f32[40,256]{1,0:T(8,128)S(1)}, f32[40,256]{1,0:T(8,128)S(1)}, u32[]{:S(2)}, u32[]{:S(2)}) %collective-permute-start) | collective-permute-done | bytes 40992 | tf_op jit(solution)/shard_map/ppermute | solution.py:507
  16.6 0.0 collective-permute-done.3.refs_5_.sv_a
  16.6 0.0 collective-permute-done.4.refs_6_.sv_b
  16.6 0.0 collective-permute-done.1.refs_3_.su_a
  16.6 0.0 collective-permute-done.2.refs_4_.su_b
  16.6 0.6 %join.1 = (f32[16,8,128]{2,1,0:T(8,128)S(1)}, f32[8,128]{1,0:T(8,128)S(1)}) custom-call(f32[40,256]{1,0:T(8,128)S(1)} %get-tuple-element.23.refs_0_, f32[40,256]{1,0:T(8,128)S(1)} %collective-permute-done.refs_1_.arrived, f32[40,128]{1,0:T(8,128)S(1)} %get-tuple-element.22.refs_2_.inverse, f32[6,2,40,128]{3,2,1,0:T(8,128)S(1)} %collective-permute-done.1.refs_3_.su_a, ...), custom_call_target="tpu_custom_call" | custom-call | flops 10240 | bytes 860160 | tf_op jit(solution)/shard_map/join/pallas_call | solution.py:440
  17.2 17.8 %all_to_all.5.chunks = f32[16,8,128]{2,1,0:T(8,128)S(1)} all-to-all(f32[16,8,128]{2,1,0:T(8,128)S(1)} %get-tuple-element.29), channel_id=1, replica_groups=mesh['su'=16,'sv'=8,'nrm'=2] {'su'}, dimensions={0} | all-to-all | bytes 131072 | tf_op jit(solution)/shard_map/all_to_all | solution.py:523
  35.0 5.7 %final.1 = (f32[5,16,40,128]{3,2,1,0:T(8,128)}, f32[16,40]{1,0:T(8,128)}) custom-call(f32[5,16,40,128]{3,2,1,0:T(8,128)S(1)} %get-tuple-element.16.prim, f32[5,16,40,128]{3,2,1,0:T(8,128)S(1)} %get-tuple-element.17.psi, f32[5,16,40,128]{3,2,1,0:T(8,128)} %target_far.1, f32[5,16,40,128]{3,2,1,0:T(8,128)S(1)} %get-tuple-element.18.normal, ...), custom_call_target="tpu_custom_call" | custom-call | flops 16384000 | bytes 11307520 | tf_op jit(solution)/shard_map/final/pallas_call | solution.py:440
Async XLA Ops:
  5.0 11.7 %collective-permute-start.1 = (f32[6,2,40,128]{3,2,1,0:T(8,128)S(1)}, f32[6,2,40,128]{3,2,1,0:T(8,128)S(1)}, u32[]{:S(2)}, u32[]{:S(2)}) collective-permute-start(f32[6,2,40,128]{3,2,1,0:T(8,128)S(1)} %get-tuple-element.24), channel_id=1, source_target_pairs={{0,16},{16,0},{32,48},{48,32},{64,80},{80,64},{96,112},{112,96},{1... | collective-permute-start | bytes 737288 | tf_op jit(solution)/shard_map/ppermute | solution.py:508
  8.3 8.3 %collective-permute-start.2 = (f32[6,2,40,128]{3,2,1,0:T(8,128)S(1)}, f32[6,2,40,128]{3,2,1,0:T(8,128)S(1)}, u32[]{:S(2)}, u32[]{:S(2)}) collective-permute-start(f32[6,2,40,128]{3,2,1,0:T(8,128)S(1)} %get-tuple-element.25), channel_id=1, source_target_pairs={{16,32},{32,16},{48,64},{64,48},{80,96},{96,80},{112,128},{128,112... | collective-permute-start | bytes 737288 | tf_op jit(solution)/shard_map/ppermute | solution.py:509
  8.3 8.3 %collective-permute-start.3 = (f32[6,32,128]{2,1,0:T(8,128)S(1)}, f32[6,32,128]{2,1,0:T(8,128)S(1)}, u32[]{:S(2)}, u32[]{:S(2)}) collective-permute-start(f32[6,32,128]{2,1,0:T(8,128)S(1)} %get-tuple-element.26), channel_id=1, source_target_pairs={{0,2},{2,0},{4,6},{6,4},{8,10},{10,8},{12,14},{14,12},{1,3},{3,1},... | collective-permute-start | bytes 294920 | tf_op jit(solution)/shard_map/ppermute | solution.py:510
  9.5 7.1 %collective-permute-start.4 = (f32[6,32,128]{2,1,0:T(8,128)S(1)}, f32[6,32,128]{2,1,0:T(8,128)S(1)}, u32[]{:S(2)}, u32[]{:S(2)}) collective-permute-start(f32[6,32,128]{2,1,0:T(8,128)S(1)} %get-tuple-element.27), channel_id=1, source_target_pairs={{2,4},{4,2},{6,8},{8,6},{10,12},{12,10},{14,0},{0,14},{3,5},{5,3},... | collective-permute-start | bytes 294920 | tf_op jit(solution)/shard_map/ppermute | solution.py:511
  11.8 4.8 %collective-permute-start = (f32[40,256]{1,0:T(8,128)S(1)}, f32[40,256]{1,0:T(8,128)S(1)}, u32[]{:S(2)}, u32[]{:S(2)}) collective-permute-start(f32[40,256]{1,0:T(8,128)S(1)} %get-tuple-element.23.refs_0_), channel_id=1, source_target_pairs={{0,1},{1,0},{2,3},{3,2},{4,5},{5,4},{6,7},{7,6},{8,9},{9,8},{10,11... | collective-permute-start | bytes 122888 | tf_op jit(solution)/shard_map/ppermute | solution.py:507

commit v4 on v3

--- a/solution.py
+++ b/solution.py
@@ -235,9 +235,9 @@
             sv_b[q, pair, :] = jnp.where(sv_even, low, high)
 
 
-def join_kernel(rows, tiles, depth, total_depth, surface, fan, *refs):
-    own, arrived, inverse = refs[:3]
-    chunk, mine = refs[-2:]
+def join_kernel(
+    rows, tiles, depth, total_depth, surface, fan, own, arrived, inverse, chunk, mine
+):
     first = lax.axis_index("nrm") == 0
     lane = lanes()
     one = jnp.zeros((1, 128), f32)
@@ -328,7 +328,7 @@
                 wide[q, i + 2, col : col + 2, :] = value[2 * i : 2 * i + 2]
                 across[q, i, col : col + 2, :] = weighted[2 * i : 2 * i + 2]
 
-    @pl.loop(0, rows)
+    @pl.loop(0, rows, unroll=4)
     def _(i):
         for t in range(tiles):
             span = slice(8 * t, 8 * t + 8)
@@ -423,7 +423,7 @@
 
     for c, copy in enumerate(loads):
         copy.wait()
-        pl.loop(c * step_rows, (c + 1) * step_rows)(finish)
+        pl.loop(c * step_rows, (c + 1) * step_rows, unroll=step_rows)(finish)
 
     @pl.loop(0, rows)
     def _(i):
@@ -515,11 +515,12 @@
             join_kernel, rows, tiles, depth, total_depth, rows * su_count, su_count
         ),
         [shape(su_count, 8, 128), shape(8, 128)],
-        (packet, arrived, inverse, su_a, su_b, sv_a, sv_b),
+        (packet, arrived, inverse),
         [],
-        points // 40,
+        100_000 * points,
         "join",
     )
+    chunk, su_a, su_b, sv_a, sv_b = lax.optimization_barrier((chunk, su_a, su_b, sv_a, sv_b))
     chunks = lax.all_to_all(chunk, "su", 0, 0)
     result, slope = call(
         functools.partial(

time: 40.8 us -> 42.7 us (1.047)
  waiting for transfers between devices: 1.4 us -> 3.49 us
  starting transfers between devices: 10.3 us -> 11 us
  Pallas kernels: 10.6 us -> 10.1 us
  blocking collectives: 17.8 us -> 17.3 us
    ppermute x1, waiting for transfers between devices: 0.01 us -> 3.48 us  [local(): su_b = lax.ppermute(su_b, 'su', pairs(su_count, 1))]
    ppermute x1, starting transfers between devices: 3.33 us -> 1.51 us  [local(): su_a = lax.ppermute(su_a, 'su', pairs(su_count, 0))]
    ppermute x1, starting transfers between devices: 0.01 us -> 1.53 us  [local(): su_b = lax.ppermute(su_b, 'su', pairs(su_count, 1))]
    ppermute x1, waiting for transfers between devices: 1.39 us -> 0.01 us  [local(): arrived = lax.ppermute(packet, 'nrm', [(0, 1), (1, 0)])]
    ppermute x1, starting transfers between devices: 3.38 us -> 4.3 us  [local(): arrived = lax.ppermute(packet, 'nrm', [(0, 1), (1, 0)])]
    ppermute x1, starting transfers between devices: 2.36 us -> 3.26 us  [local(): sv_b = lax.ppermute(sv_b, 'sv', pairs(sv_count, 1))]
    ppermute x1, starting transfers between devices: 1.18 us -> 0.4 us  [local(): sv_a = lax.ppermute(sv_a, 'sv', pairs(sv_count, 0))]
    all_to_all x1, blocking collectives: 17.8 us -> 17.3 us  [local(): chunks = lax.all_to_all(chunk, 'su', 0, 0)]
  transfers between devices with their start and end apart: 5 -> 5, of which waited for: 1 -> 1; matrix products, arithmetic and copies ran while one was open for 0% -> 0% of each run, Pallas kernels for 0% -> 1%
where the time goes in v4:
time: 42.7 us; the launch traced here: 42.6 us
  blocking collectives  17.3 us (41%)
  starting transfers between devices  11 us (26%)
  Pallas kernels  10.1 us (24%)
  waiting for transfers between devices  3.49 us (8%)
  between operations  0.68 us (2%)
    all_to_all x1, blocking collectives, local(): chunks = lax.all_to_all(chunk, 'su', 0, 0)  17.3 us
    pallas_call x3, Pallas kernels, call(): pl.pallas_call(kernel, out_shape=outs, in_specs=[spec(n) for n in range(l...  10.1 us
    ppermute x1, starting transfers between devices, local(): arrived = lax.ppermute(packet, 'nrm', [(0, 1), (1, 0)])  4.3 us
    ppermute x1, waiting for transfers between devices, local(): su_b = lax.ppermute(su_b, 'su', pairs(su_count, 1))  3.48 us
    ppermute x1, starting transfers between devices, local(): sv_b = lax.ppermute(sv_b, 'sv', pairs(sv_count, 1))  3.26 us
    ppermute x1, starting transfers between devices, local(): su_b = lax.ppermute(su_b, 'su', pairs(su_count, 1))  1.53 us
    ppermute x1, starting transfers between devices, local(): su_a = lax.ppermute(su_a, 'su', pairs(su_count, 0))  1.51 us
  transfers between devices with their start and end apart: 5, of which 1 were waited for; matrix products, arithmetic and copies ran while one was open for 0% of the time, Pallas kernels for 1%

profile of v4, /device:TPU:1, one launch (start us, length us, event | category | flops | bytes accessed | tf_op | source)
XLA Modules:
  0.0 42.6 jit_solution(1548077985292689458)
XLA Ops:
  0.6 4.3 %prepare.1 = (f32[40,256]{1,0:T(8,128)S(1)}, f32[6,2,40,128]{3,2,1,0:T(8,128)S(1)}, f32[6,2,40,128]{3,2,1,0:T(8,128)S(1)}, f32[6,32,128]{2,1,0:T(8,128)S(1)}, f3...) custom-call(f32[5,16,40,128]{3,2,1,0:T(8,128)} %prim_far.1, ...), custom_call_target="tpu_custom_call" | custom-call | flops 4915200 | bytes 11278848 | tf_op jit(solution)/shard_map/prepare/pallas_call | solution.py:440
  5.0 4.3 %collective-permute-start = (f32[40,256]{1,0:T(8,128)S(1)}, f32[40,256]{1,0:T(8,128)S(1)}, u32[]{:S(2)}, u32[]{:S(2)}) collective-permute-start(f32[40,256]{1,0:T(8,128)S(1)} %get-tuple-element.28.own), channel_id=1, source_target_pairs={{0,1},{1,0},{2,3},{3,2},{4,5},{5,4},{6,7},{7,6},{8,9},{9,8},{10,11... | collective-permute-start | bytes 122888 | tf_op jit(solution)/shard_map/ppermute | solution.py:507
  9.3 0.4 collective-permute-start.3
  9.7 3.3 %collective-permute-start.4 = (f32[6,32,128]{2,1,0:T(8,128)S(1)}, f32[6,32,128]{2,1,0:T(8,128)S(1)}, u32[]{:S(2)}, u32[]{:S(2)}) collective-permute-start(f32[6,32,128]{2,1,0:T(8,128)S(1)} %get-tuple-element.34), channel_id=1, source_target_pairs={{2,4},{4,2},{6,8},{8,6},{10,12},{12,10},{14,0},{0,14},{3,5},{5,3},... | collective-permute-start | bytes 294920 | tf_op jit(solution)/shard_map/ppermute | solution.py:511
  12.9 1.5 %collective-permute-start.1 = (f32[6,2,40,128]{3,2,1,0:T(8,128)S(1)}, f32[6,2,40,128]{3,2,1,0:T(8,128)S(1)}, u32[]{:S(2)}, u32[]{:S(2)}) collective-permute-start(f32[6,2,40,128]{3,2,1,0:T(8,128)S(1)} %get-tuple-element.31), channel_id=1, source_target_pairs={{0,16},{16,0},{32,48},{48,32},{64,80},{80,64},{96,112},{112,96},{1... | collective-permute-start | bytes 737288 | tf_op jit(solution)/shard_map/ppermute | solution.py:508
  14.5 1.5 %collective-permute-start.2 = (f32[6,2,40,128]{3,2,1,0:T(8,128)S(1)}, f32[6,2,40,128]{3,2,1,0:T(8,128)S(1)}, u32[]{:S(2)}, u32[]{:S(2)}) collective-permute-start(f32[6,2,40,128]{3,2,1,0:T(8,128)S(1)} %get-tuple-element.32), channel_id=1, source_target_pairs={{16,32},{32,16},{48,64},{64,48},{80,96},{96,80},{112,128},{128,112... | collective-permute-start | bytes 737288 | tf_op jit(solution)/shard_map/ppermute | solution.py:509
  16.0 0.0 collective-permute-done.arrived
  16.0 0.6 %join.1 = (f32[16,8,128]{2,1,0:T(8,128)S(1)}, f32[8,128]{1,0:T(8,128)S(1)}) custom-call(f32[40,256]{1,0:T(8,128)S(1)} %get-tuple-element.28.own, f32[40,256]{1,0:T(8,128)S(1)} %collective-permute-done.arrived, f32[40,128]{1,0:T(8,128)S(1)} %get-tuple-element.27.inverse), custom_call_target="tpu_custom_call" | custom-call | flops 40960000000 | bytes 172032 | tf_op jit(solution)/shard_map/join/pallas_call | solution.py:440
  16.6 0.0 collective-permute-done.3.sv_a
  16.6 0.0 collective-permute-done.4.sv_b
  16.6 0.0 collective-permute-done.1.su_a
  16.6 3.5 %collective-permute-done.2.su_b = f32[6,2,40,128]{3,2,1,0:T(8,128)S(1)} collective-permute-done((f32[6,2,40,128]{3,2,1,0:T(8,128)S(1)}, f32[6,2,40,128]{3,2,1,0:T(8,128)S(1)}, u32[]{:S(2)}, u32[]{:S(2)}) %collective-permute-start.2) | collective-permute-done | bytes 245792 | tf_op jit(solution)/shard_map/ppermute | solution.py:509
  20.1 17.3 %all_to_all.5.chunks = f32[16,8,128]{2,1,0:T(8,128)S(1)} all-to-all(f32[16,8,128]{2,1,0:T(8,128)S(1)} %get-tuple-element.39), channel_id=1, replica_groups=mesh['su'=16,'sv'=8,'nrm'=2] {'su'}, dimensions={0} | all-to-all | bytes 131072 | tf_op jit(solution)/shard_map/all_to_all | solution.py:524
  37.4 5.2 %final.1 = (f32[5,16,40,128]{3,2,1,0:T(8,128)}, f32[16,40]{1,0:T(8,128)}) custom-call(f32[5,16,40,128]{3,2,1,0:T(8,128)S(1)} %get-tuple-element.21.prim, f32[5,16,40,128]{3,2,1,0:T(8,128)S(1)} %get-tuple-element.22.psi, f32[5,16,40,128]{3,2,1,0:T(8,128)} %target_far.1, f32[5,16,40,128]{3,2,1,0:T(8,128)S(1)} %get-tuple-element.23.normal, ...), custom_call_target="tpu_custom_call" | custom-call | flops 16384000 | bytes 11307520 | tf_op jit(solution)/shard_map/final/pallas_call | solution.py:440
Async XLA Ops:
  5.0 11.0 %collective-permute-start = (f32[40,256]{1,0:T(8,128)S(1)}, f32[40,256]{1,0:T(8,128)S(1)}, u32[]{:S(2)}, u32[]{:S(2)}) collective-permute-start(f32[40,256]{1,0:T(8,128)S(1)} %get-tuple-element.28.own), channel_id=1, source_target_pairs={{0,1},{1,0},{2,3},{3,2},{4,5},{5,4},{6,7},{7,6},{8,9},{9,8},{10,11... | collective-permute-start | bytes 122888 | tf_op jit(solution)/shard_map/ppermute | solution.py:507
  9.3 7.3 %collective-permute-start.3 = (f32[6,32,128]{2,1,0:T(8,128)S(1)}, f32[6,32,128]{2,1,0:T(8,128)S(1)}, u32[]{:S(2)}, u32[]{:S(2)}) collective-permute-start(f32[6,32,128]{2,1,0:T(8,128)S(1)} %get-tuple-element.33), channel_id=1, source_target_pairs={{0,2},{2,0},{4,6},{6,4},{8,10},{10,8},{12,14},{14,12},{1,3},{3,1},... | collective-permute-start | bytes 294920 | tf_op jit(solution)/shard_map/ppermute | solution.py:510
  9.7 6.9 %collective-permute-start.4 = (f32[6,32,128]{2,1,0:T(8,128)S(1)}, f32[6,32,128]{2,1,0:T(8,128)S(1)}, u32[]{:S(2)}, u32[]{:S(2)}) collective-permute-start(f32[6,32,128]{2,1,0:T(8,128)S(1)} %get-tuple-element.34), channel_id=1, source_target_pairs={{2,4},{4,2},{6,8},{8,6},{10,12},{12,10},{14,0},{0,14},{3,5},{5,3},... | collective-permute-start | bytes 294920 | tf_op jit(solution)/shard_map/ppermute | solution.py:511
  12.9 3.6 %collective-permute-start.1 = (f32[6,2,40,128]{3,2,1,0:T(8,128)S(1)}, f32[6,2,40,128]{3,2,1,0:T(8,128)S(1)}, u32[]{:S(2)}, u32[]{:S(2)}) collective-permute-start(f32[6,2,40,128]{3,2,1,0:T(8,128)S(1)} %get-tuple-element.31), channel_id=1, source_target_pairs={{0,16},{16,0},{32,48},{48,32},{64,80},{80,64},{96,112},{112,96},{1... | collective-permute-start | bytes 737288 | tf_op jit(solution)/shard_map/ppermute | solution.py:508
  14.5 5.6 %collective-permute-start.2 = (f32[6,2,40,128]{3,2,1,0:T(8,128)S(1)}, f32[6,2,40,128]{3,2,1,0:T(8,128)S(1)}, u32[]{:S(2)}, u32[]{:S(2)}) collective-permute-start(f32[6,2,40,128]{3,2,1,0:T(8,128)S(1)} %get-tuple-element.32), channel_id=1, source_target_pairs={{16,32},{32,16},{48,64},{64,48},{80,96},{96,80},{112,128},{128,112... | collective-permute-start | bytes 737288 | tf_op jit(solution)/shard_map/ppermute | solution.py:509

commit v5 on v4

--- a/solution.py
+++ b/solution.py
@@ -13,6 +13,8 @@
 gm = gamma_ratio - 1.0
 f32 = jnp.float32
 VMEM = pltpu.VMEM
+JOIN_COST = 5_000
+INTERIOR_COST = 5_000
 
 
 def lanes(shape=(8, 128)):
@@ -273,14 +275,40 @@
         chunk[n] = sums
 
 
-def final_kernel(
-    rows, tiles, depth, total_depth, su_count, sv_count,
-    prim, psi, target_far, normal, flux, enth, tone, inverse, arrived, mine,
-    su_a, su_b, sv_a, sv_b, chunks,
-    result, slope,
-    wide, along, across, turn, done, target, sems, large,
+def transposed(speeds, kinetic, enthalpy, first, second, third):
+    given = [(d, g) for d, g in ((0, first), (1, second), (2, third)) if g is not None]
+    add = lambda parts: functools.reduce(lambda x, y: x + y, parts)
+    projected = add([g[d + 1] for d, g in given])
+    energy = add([speeds[d] * g[4] for d, g in given])
+    dots = {
+        d: speeds[0] * g[1] + speeds[1] * g[2] + speeds[2] * g[3] for d, g in given
+    }
+    shared = gm * (projected + energy)
+    out = [
+        kinetic * projected
+        - add([speeds[d] * dots[d] for d, _ in given])
+        + (kinetic - enthalpy) * energy
+    ]
+    for c in range(3):
+        value = add([speeds[d] * g[c + 1] for d, g in given]) - speeds[c] * shared
+        for d, g in given:
+            if d == c:
+                value = value + (g[0] + dots[d] + enthalpy * g[4])
+        out.append(value)
+    out.append(gm * projected + gamma_ratio * energy)
+    return out
+
+
+near_weight, far_weight = 8.0 / 12.0, 1.0 / 12.0
+
+
+def interior_kernel(
+    rows, tiles, prim, psi, target_far, normal, enth, tone,
+    base,
+    wide, along, across, target, large,
 ):
     step_rows = 4
+    columns = 8 * tiles
     loads = [
         pltpu.make_async_copy(
             target_far.at[:, pl.ds(r, step_rows)], target.at[:, pl.ds(r, step_rows)],
@@ -290,43 +318,14 @@
     ]
     for copy in loads:
         copy.start()
-    su, sv, nrm = lax.axis_index("su"), lax.axis_index("sv"), lax.axis_index("nrm")
-    first = nrm == 0
-    lane = lanes()
-    columns = 8 * tiles
-    ahead = jnp.zeros((8, 128), f32)
-    for n in range(su_count):
-        ahead = ahead + jnp.where(n > su, chunks[n], 0.0)
-    upstream = jnp.zeros((8, 128), f32)
-    for t in range(tiles):
-        upstream = jnp.where(
-            (lane >= rows * t) & (lane < rows * t + rows), spread_lane(ahead, t), upstream
-        )
-    packed = mine[...] + upstream
-    turn[...] = jnp.zeros_like(turn)
-    for t in range(tiles):
-        turn[8 * t : 8 * t + 8, :] = pltpu.roll(packed, 128 - rows * t, 1) if t else packed
-    slope[...] = turn[...].T[0:rows, 0:columns]
-
-    su_even, sv_even = even("su"), even("sv")
-    low_on, high_on = su > 0, su < su_count - 1
-    for r in range(2):
-        for swap, on, row in ((su_even, low_on, r), (~su_even, high_on, rows + 2 + r)):
-            pick = lambda q: jnp.where(swap, su_b[q, r], su_a[q, r])
-            radius = pick(5)
-            for q in range(5):
-                value = jnp.where(on, pick(q), 0.0)
-                wide[q, row, 8 : 8 + columns, :] = value
-                along[q, row] = value * radius
-    left_on, right_on = sv > 0, sv < sv_count - 1
-    for swap, on, col in ((sv_even, left_on, 6), (~sv_even, right_on, 8 + columns)):
-        radius = jnp.where(swap, sv_b[5], sv_a[5])
-        for q in range(5):
-            value = jnp.where(on, jnp.where(swap, sv_b[q], sv_a[q]), 0.0)
-            weighted = value * radius
-            for i in range(rows):
-                wide[q, i + 2, col : col + 2, :] = value[2 * i : 2 * i + 2]
-                across[q, i, col : col + 2, :] = weighted[2 * i : 2 * i + 2]
+    for q in range(5):
+        for row in (0, 1, rows + 2, rows + 3):
+            wide[q, row] = jnp.zeros_like(wide[q, row])
+            along[q, row] = jnp.zeros_like(along[q, row])
+        for i in range(rows):
+            for low in (0, 8 + columns):
+                wide[q, i + 2, low : low + 8, :] = jnp.zeros((8, 128), f32)
+                across[q, i, low : low + 8, :] = jnp.zeros((8, 128), f32)
 
     @pl.loop(0, rows, unroll=4)
     def _(i):
@@ -342,42 +341,19 @@
                 along[q, i + 2, span, :] = radius_u * value
                 across[q, i, inner, :] = radius_v * value
 
-    fraction = jnp.broadcast_to(
-        ((lanes((1, 128)) + nrm * depth).astype(f32) + 0.5) / total_depth, (8, 128)
-    )
-    one = jnp.zeros((1, 128), f32)
-    edge_scale = jnp.where(
-        first,
-        -0.5 * inv_stretch_at(one + depth, total_depth),
-        0.5 * inv_stretch_at(one + (depth - 1), total_depth),
-    )
-    entry = jnp.where(first, depth - 1, 0)
-    at_entry = lane == entry
-    for t in range(tiles):
-        span = slice(8 * t, 8 * t + 8)
-        repeated = inverse[span, :]
-        for d in (1, 2, 4):
-            repeated = repeated + pltpu.roll(repeated, rows * d, 1)
-        turn[span, :] = arrived[span, 0:128] * edge_scale * repeated
-
-    def out_copy(i):
-        return pltpu.make_async_copy(done.at[:, i], result.at[:, i], sems.at[i])
-
-    def finish(i):
-        turned = pltpu.roll(packed, 128 - i, 1)
+    def fill(i):
         for t in range(tiles):
             span = slice(8 * t, 8 * t + 8)
             at = lambda k: slice(8 * t + 8 + k, 8 * t + 16 + k)
-            ends = turn[span, :]
             first, second, third, damp = [], [], [], []
             for q in range(5):
                 first.append(
-                    (8.0 / 12.0) * (wide[q, i + 1, at(0), :] - wide[q, i + 3, at(0), :])
-                    - (1.0 / 12.0) * (wide[q, i, at(0), :] - wide[q, i + 4, at(0), :])
+                    near_weight * (wide[q, i + 1, at(0), :] - wide[q, i + 3, at(0), :])
+                    - far_weight * (wide[q, i, at(0), :] - wide[q, i + 4, at(0), :])
                 )
                 second.append(
-                    (8.0 / 12.0) * (wide[q, i + 2, at(-1), :] - wide[q, i + 2, at(1), :])
-                    - (1.0 / 12.0) * (wide[q, i + 2, at(-2), :] - wide[q, i + 2, at(2), :])
+                    near_weight * (wide[q, i + 2, at(-1), :] - wide[q, i + 2, at(1), :])
+                    - far_weight * (wide[q, i + 2, at(-2), :] - wide[q, i + 2, at(2), :])
                 )
                 far = (
                     along[q, i, span, :] + along[q, i + 4, span, :]
@@ -391,39 +367,157 @@
                 damp.append(
                     damping_coef * far - (4.0 * damping_coef) * near + (6.0 * damping_coef) * here
                 )
-                came = pltpu.roll(ends, entry + (128 - rows * q) - i, 1)
-                third.append(normal[q, i, span, :] + jnp.where(at_entry, came, 0.0))
-            u1, u2, u3 = (prim[q, i, span, :] for q in (1, 2, 3))
-            enthalpy = enth[i, span, :]
+                third.append(normal[q, i, span, :])
+            speeds = tuple(prim[q, i, span, :] for q in (1, 2, 3))
+            u1, u2, u3 = speeds
             kinetic = (0.5 * gm) * (u1 * u1 + u2 * u2 + u3 * u3)
-            projected = first[1] + second[2] + third[3]
-            energy = u1 * first[4] + u2 * second[4] + u3 * third[4]
-            dot = lambda g: u1 * g[1] + u2 * g[2] + u3 * g[3]
-            dot1, dot2, dot3 = dot(first), dot(second), dot(third)
-            mass_row = (
-                kinetic * projected
-                - (u1 * dot1 + u2 * dot2 + u3 * dot3)
-                + (kinetic - enthalpy) * energy
-            )
-            shared = gm * (projected + energy)
-            moved = lambda b: u1 * first[b] + u2 * second[b] + u3 * third[b]
-            rows_out = (
-                mass_row,
-                moved(1) - u1 * shared + (first[0] + dot1 + enthalpy * first[4]),
-                moved(2) - u2 * shared + (second[0] + dot2 + enthalpy * second[4]),
-                moved(3) - u3 * shared + (third[0] + dot3 + enthalpy * third[4]),
-                gm * projected + gamma_ratio * energy,
-            )
-            ramp = fraction * spread_lane(turned, rows * t)
-            for q in range(5):
-                done[q, i, span, :] = (
-                    target[q, i, span, :] + rows_out[q] + damp[q] + ramp * flux[q, i, span, :]
-                )
-        out_copy(i).start()
+            terms = transposed(speeds, kinetic, enth[i, span, :], first, second, third)
+            for q in range(5):
+                base[q, i, span, :] = target[q, i, span, :] + terms[q] + damp[q]
 
     for c, copy in enumerate(loads):
         copy.wait()
-        pl.loop(c * step_rows, (c + 1) * step_rows, unroll=step_rows)(finish)
+        pl.loop(c * step_rows, (c + 1) * step_rows, unroll=step_rows)(fill)
+
+
+def final_kernel(
+    rows, tiles, depth, total_depth, su_count, sv_count,
+    prim, base, flux, enth, inverse, arrived, mine,
+    su_a, su_b, sv_a, sv_b, chunks,
+    result, slope,
+    left, right, turn, done, sems,
+):
+    su, sv, nrm = lax.axis_index("su"), lax.axis_index("sv"), lax.axis_index("nrm")
+    before = nrm == 0
+    lane = lanes()
+    line = lax.broadcasted_iota(jnp.int32, (8, 128), 0)
+    columns = 8 * tiles
+    ahead = jnp.zeros((8, 128), f32)
+    for n in range(su_count):
+        ahead = ahead + jnp.where(n > su, chunks[n], 0.0)
+    upstream = jnp.zeros((8, 128), f32)
+    for t in range(tiles):
+        upstream = jnp.where(
+            (lane >= rows * t) & (lane < rows * t + rows), spread_lane(ahead, t), upstream
+        )
+    packed = mine[...] + upstream
+    turn[...] = jnp.zeros_like(turn)
+    for t in range(tiles):
+        turn[8 * t : 8 * t + 8, :] = pltpu.roll(packed, 128 - rows * t, 1) if t else packed
+    slope[...] = turn[...].T[0:rows, 0:columns]
+
+    one = jnp.zeros((1, 128), f32)
+    edge_scale = jnp.where(
+        before,
+        -0.5 * inv_stretch_at(one + depth, total_depth),
+        0.5 * inv_stretch_at(one + (depth - 1), total_depth),
+    )
+    entry = jnp.where(before, depth - 1, 0)
+    at_entry = lane == entry
+    for t in range(tiles):
+        span = slice(8 * t, 8 * t + 8)
+        repeated = inverse[span, :]
+        for d in (1, 2, 4):
+            repeated = repeated + pltpu.roll(repeated, rows * d, 1)
+        turn[span, :] = arrived[span, 0:128] * edge_scale * repeated
+
+    su_even, sv_even = even("su"), even("sv")
+    for piece in range(2 * rows // 8):
+        at = slice(8 * piece, 8 * piece + 8)
+        outer = lax.rem(line, 2) == 0
+        for swap, on, ref, offset, sign in (
+            (sv_even, sv > 0, left, 0, 1.0),
+            (~sv_even, sv < sv_count - 1, right, 8, -1.0),
+        ):
+            into = slice(8 * piece + offset, 8 * piece + offset + 8)
+            pick = lambda q: jnp.where(swap, sv_b[q, at, :], sv_a[q, at, :])
+            radius = pick(5)
+            for q in range(5):
+                value = jnp.where(on, pick(q), 0.0)
+                weighted = value * radius
+                grads, damps = [], []
+                for array, close, away, kept in (
+                    (value, sign * near_weight, -sign * far_weight, grads),
+                    (weighted, -4.0 * damping_coef, damping_coef, damps),
+                ):
+                    if offset == 0:
+                        even_part = close * pltpu.roll(array, 7, 0) + away * array
+                        odd_part = away * array
+                    else:
+                        even_part = away * array
+                        odd_part = close * pltpu.roll(array, 1, 0) + away * array
+                    kept.append(jnp.where(outer, even_part, odd_part))
+                ref[q, into, :] = grads[0]
+                ref[5 + q, into, :] = damps[0]
+
+    def out_copy(i):
+        return pltpu.make_async_copy(done.at[:, i], result.at[:, i], sems.at[i])
+
+    fraction = jnp.broadcast_to(
+        ((lanes((1, 128)) + nrm * depth).astype(f32) + 0.5) / total_depth, (8, 128)
+    )
+
+    def finish(i, beside):
+        turned = pltpu.roll(packed, 128 - i, 1)
+        for t in range(tiles):
+            span = slice(8 * t, 8 * t + 8)
+            ends = turn[span, :]
+            third = [
+                jnp.where(at_entry, pltpu.roll(ends, entry + (128 - rows * q) - i, 1), 0.0)
+                for q in range(5)
+            ]
+            first = second = None
+            damp = [None] * 5
+            if beside is not None:
+                first, damp = beside(span)
+            if t in (0, tiles - 1):
+                ref, start = (left, 2 * i) if t == 0 else (right, 2 * i + 2)
+                here = line < 2 if t == 0 else line >= 6
+                load = lambda q: jnp.where(here, ref[q, pl.ds(start, 8), :], 0.0)
+                second = [load(q) for q in range(5)]
+                damp = [
+                    load(5 + q) if damp[q] is None else damp[q] + load(5 + q) for q in range(5)
+                ]
+            speeds = tuple(prim[q, i, span, :] for q in (1, 2, 3))
+            u1, u2, u3 = speeds
+            kinetic = (0.5 * gm) * (u1 * u1 + u2 * u2 + u3 * u3)
+            terms = transposed(speeds, kinetic, enth[i, span, :], first, second, third)
+            ramp = fraction * spread_lane(turned, rows * t)
+            for q in range(5):
+                value = base[q, i, span, :] + terms[q] + ramp * flux[q, i, span, :]
+                done[q, i, span, :] = value if damp[q] is None else value + damp[q]
+        out_copy(i).start()
+
+    def edge_row(low, inner):
+        swap, on, sign = (
+            (su_even, su > 0, 1.0) if low else (~su_even, su < su_count - 1, -1.0)
+        )
+
+        def beside(span):
+            pick = lambda q, r: jnp.where(swap, su_b[q, r, span, :], su_a[q, r, span, :])
+            close, away = (1, 0) if low else (0, 1)
+            grads, damps = [], []
+            for q in range(5):
+                value = jnp.where(on, pick(q, close), 0.0)
+                weighted = value * pick(5, close)
+                if inner:
+                    grads.append((-sign * far_weight) * value)
+                    damps.append(damping_coef * weighted)
+                else:
+                    other = jnp.where(on, pick(q, away), 0.0)
+                    grads.append((sign * near_weight) * value - (sign * far_weight) * other)
+                    damps.append(
+                        damping_coef * (other * pick(5, away)) - (4.0 * damping_coef) * weighted
+                    )
+            return grads, damps
+
+        return beside
+
+    finish(0, edge_row(True, False))
+    finish(1, edge_row(True, True))
+    pl.loop(2, rows - 2, unroll=4)(lambda i: finish(i, None))
+    finish(rows - 2, edge_row(False, True))
+    finish(rows - 1, edge_row(False, False))
 
     @pl.loop(0, rows)
     def _(i):
@@ -517,10 +611,27 @@
         [shape(su_count, 8, 128), shape(8, 128)],
         (packet, arrived, inverse),
         [],
-        100_000 * points,
+        JOIN_COST * points,
         "join",
     )
-    chunk, su_a, su_b, sv_a, sv_b = lax.optimization_barrier((chunk, su_a, su_b, sv_a, sv_b))
+    (base,) = call(
+        functools.partial(interior_kernel, rows, tiles),
+        [field],
+        (prim, psi, objective_grad, normal, enth, tone),
+        [
+            VMEM((5, rows + 4, columns + 16, depth), f32),
+            VMEM((5, rows + 4, columns, depth), f32),
+            VMEM((5, rows, columns + 16, depth), f32),
+            VMEM((5, rows, columns, depth), f32),
+            pltpu.SemaphoreType.DMA((4,)),
+        ],
+        INTERIOR_COST * points,
+        "interior",
+        far=(2,),
+    )
+    chunk, su_a, su_b, sv_a, sv_b, base = lax.optimization_barrier(
+        (chunk, su_a, su_b, sv_a, sv_b, base)
+    )
     chunks = lax.all_to_all(chunk, "su", 0, 0)
     result, slope = call(
         functools.partial(
@@ -528,23 +639,19 @@
         ),
         [field, shape(rows, columns)],
         (
-            prim, psi, objective_grad, normal, flux, enth, tone, inverse,
+            prim, base, flux, enth, inverse,
             arrived, mine, su_a, su_b, sv_a, sv_b, chunks,
         ),
         [
-            VMEM((5, rows + 4, columns + 16, depth), f32),
-            VMEM((5, rows + 4, columns, depth), f32),
-            VMEM((5, rows, columns + 16, depth), f32),
+            VMEM((10, 2 * rows + 8, depth), f32),
+            VMEM((10, 2 * rows + 16, depth), f32),
             VMEM((128, 128), f32),
             VMEM((5, rows, columns, depth), f32),
-            VMEM((5, rows, columns, depth), f32),
             pltpu.SemaphoreType.DMA((rows,)),
-            pltpu.SemaphoreType.DMA((4,)),
         ],
-        40 * points,
+        20 * points,
         "final",
         [pltpu.HBM, VMEM],
-        far=(2,),
     )
     return result, slope
 

time: 42.7 us -> 38.3 us (0.90)
  waiting for transfers between devices: 3.49 us -> 0.01 us
  blocking collectives: 17.3 us -> 15.8 us
  Pallas kernels: 10.1 us -> 11.2 us
  starting transfers between devices: 11 us -> 10.4 us
    ppermute x1, waiting for transfers between devices: 3.48 us -> 0.01 us  [local(): su_b = lax.ppermute(su_b, 'su', pairs(su_count, 1))]
    all_to_all x1, blocking collectives: 17.3 us -> 15.8 us  [local(): chunks = lax.all_to_all(chunk, 'su', 0, 0)]
    pallas_call x3 -> x4, Pallas kernels: 10.1 us -> 11.2 us  [call(): pl.pallas_call(kernel, out_shape=outs, in_specs=[spec(n) for n in range(l...]
    ppermute x1, starting transfers between devices: 1.51 us -> 0.95 us  [local(): su_a = lax.ppermute(su_a, 'su', pairs(su_count, 0))]
  transfers between devices with their start and end apart: 5 -> 5, of which waited for: 1 -> 0; matrix products, arithmetic and copies ran while one was open for 0% -> 0% of each run, Pallas kernels for 1% -> 10%
where the time goes in v5:
time: 38.3 us; the launch traced here: 38.2 us
  blocking collectives  15.8 us (41%)
  Pallas kernels  11.2 us (29%)
  starting transfers between devices  10.4 us (27%)
  between operations  0.7 us (2%)
    all_to_all x1, blocking collectives, local(): chunks = lax.all_to_all(chunk, 'su', 0, 0)  15.8 us
    pallas_call x4, Pallas kernels, call(): pl.pallas_call(kernel, out_shape=outs, in_specs=[spec(n) for n in range(l...  11.2 us
    ppermute x1, starting transfers between devices, local(): arrived = lax.ppermute(packet, 'nrm', [(0, 1), (1, 0)])  4.3 us
    ppermute x1, starting transfers between devices, local(): sv_b = lax.ppermute(sv_b, 'sv', pairs(sv_count, 1))  3.26 us
    ppermute x1, starting transfers between devices, local(): su_b = lax.ppermute(su_b, 'su', pairs(su_count, 1))  1.53 us
    ppermute x1, starting transfers between devices, local(): su_a = lax.ppermute(su_a, 'su', pairs(su_count, 0))  0.95 us
  transfers between devices with their start and end apart: 5, of which 0 were waited for; matrix products, arithmetic and copies ran while one was open for 0% of the time, Pallas kernels for 10%

profile of v5, /device:TPU:1, one launch (start us, length us, event | category | flops | bytes accessed | tf_op | source)
XLA Modules:
  0.0 38.2 jit_solution(15913626859563169736)
XLA Ops:
  0.6 4.3 %prepare.1 = (f32[40,256]{1,0:T(8,128)S(1)}, f32[6,2,40,128]{3,2,1,0:T(8,128)S(1)}, f32[6,2,40,128]{3,2,1,0:T(8,128)S(1)}, f32[6,32,128]{2,1,0:T(8,128)S(1)}, f3...) custom-call(f32[5,16,40,128]{3,2,1,0:T(8,128)} %prim_far.1, ...), custom_call_target="tpu_custom_call" | custom-call | flops 4915200 | bytes 11278848 | tf_op jit(solution)/shard_map/prepare/pallas_call | solution.py:534
  4.9 4.3 %collective-permute-start = (f32[40,256]{1,0:T(8,128)S(1)}, f32[40,256]{1,0:T(8,128)S(1)}, u32[]{:S(2)}, u32[]{:S(2)}) collective-permute-start(f32[40,256]{1,0:T(8,128)S(1)} %get-tuple-element.23.own), channel_id=1, source_target_pairs={{0,1},{1,0},{2,3},{3,2},{4,5},{5,4},{6,7},{7,6},{8,9},{9,8},{10,11... | collective-permute-start | bytes 122888 | tf_op jit(solution)/shard_map/ppermute | solution.py:601
  9.2 1.0 %collective-permute-start.1 = (f32[6,2,40,128]{3,2,1,0:T(8,128)S(1)}, f32[6,2,40,128]{3,2,1,0:T(8,128)S(1)}, u32[]{:S(2)}, u32[]{:S(2)}) collective-permute-start(f32[6,2,40,128]{3,2,1,0:T(8,128)S(1)} %get-tuple-element.26), channel_id=1, source_target_pairs={{0,16},{16,0},{32,48},{48,32},{64,80},{80,64},{96,112},{112,96},{1... | collective-permute-start | bytes 737288 | tf_op jit(solution)/shard_map/ppermute | solution.py:602
  10.2 1.5 %collective-permute-start.2 = (f32[6,2,40,128]{3,2,1,0:T(8,128)S(1)}, f32[6,2,40,128]{3,2,1,0:T(8,128)S(1)}, u32[]{:S(2)}, u32[]{:S(2)}) collective-permute-start(f32[6,2,40,128]{3,2,1,0:T(8,128)S(1)} %get-tuple-element.27), channel_id=1, source_target_pairs={{16,32},{32,16},{48,64},{64,48},{80,96},{96,80},{112,128},{128,112... | collective-permute-start | bytes 737288 | tf_op jit(solution)/shard_map/ppermute | solution.py:603
  11.7 0.4 %collective-permute-start.3 = (f32[6,32,128]{2,1,0:T(8,128)S(1)}, f32[6,32,128]{2,1,0:T(8,128)S(1)}, u32[]{:S(2)}, u32[]{:S(2)}) collective-permute-start(f32[6,32,128]{2,1,0:T(8,128)S(1)} %get-tuple-element.28), channel_id=1, source_target_pairs={{0,2},{2,0},{4,6},{6,4},{8,10},{10,8},{12,14},{14,12},{1,3},{3,1},... | collective-permute-start | bytes 294920 | tf_op jit(solution)/shard_map/ppermute | solution.py:604
  12.1 3.3 %collective-permute-start.4 = (f32[6,32,128]{2,1,0:T(8,128)S(1)}, f32[6,32,128]{2,1,0:T(8,128)S(1)}, u32[]{:S(2)}, u32[]{:S(2)}) collective-permute-start(f32[6,32,128]{2,1,0:T(8,128)S(1)} %get-tuple-element.29), channel_id=1, source_target_pairs={{2,4},{4,2},{6,8},{8,6},{10,12},{12,10},{14,0},{0,14},{3,5},{5,3},... | collective-permute-start | bytes 294920 | tf_op jit(solution)/shard_map/ppermute | solution.py:605
  15.4 3.3 %interior.1.base = f32[5,16,40,128]{3,2,1,0:T(8,128)S(1)} custom-call(f32[5,16,40,128]{3,2,1,0:T(8,128)S(1)} %get-tuple-element.22.prim, f32[5,16,40,128]{3,2,1,0:T(8,128)S(1)} %get-tuple-element.30.psi, f32[5,16,40,128]{3,2,1,0:T(8,128)} %target_far.1, f32[5,16,40,128]{3,2,1,0:T(8,128)S(1)} %get-tuple-element.31.normal, ...), custom_call_target="tpu_custom_call" | custom-call | flops 2048000000 | bytes 8847360 | tf_op jit(solution)/shard_map/interior/pallas_call | solution.py:534
  18.7 0.0 collective-permute-done.arrived
  18.7 0.6 %join.1 = (f32[16,8,128]{2,1,0:T(8,128)S(1)}, f32[8,128]{1,0:T(8,128)S(1)}) custom-call(f32[40,256]{1,0:T(8,128)S(1)} %get-tuple-element.23.own, f32[40,256]{1,0:T(8,128)S(1)} %collective-permute-done.arrived, f32[40,128]{1,0:T(8,128)S(1)} %get-tuple-element.24.inverse), custom_call_target="tpu_custom_call" | custom-call | flops 2048000000 | bytes 172032 | tf_op jit(solution)/shard_map/join/pallas_call | solution.py:534
  19.3 0.0 collective-permute-done.3.sv_a
  19.3 0.0 collective-permute-done.4.sv_b
  19.3 0.0 collective-permute-done.1.su_a
  19.3 0.0 collective-permute-done.2.su_b
  19.3 15.8 %all_to_all.5.chunks = f32[16,8,128]{2,1,0:T(8,128)S(1)} all-to-all(f32[16,8,128]{2,1,0:T(8,128)S(1)} %get-tuple-element.41), channel_id=1, replica_groups=mesh['su'=16,'sv'=8,'nrm'=2] {'su'}, dimensions={0} | all-to-all | bytes 131072 | tf_op jit(solution)/shard_map/all_to_all | solution.py:635
  35.1 3.1 %final.1 = (f32[5,16,40,128]{3,2,1,0:T(8,128)}, f32[16,40]{1,0:T(8,128)}) custom-call(f32[5,16,40,128]{3,2,1,0:T(8,128)S(1)} %get-tuple-element.22.prim, f32[5,16,40,128]{3,2,1,0:T(8,128)S(1)} %interior.1.base, f32[5,16,40,128]{3,2,1,0:T(8,128)S(1)} %get-tuple-element.35.flux, f32[16,40,128]{2,1,0:T(8,128)S(1)} %get-tuple-element.32.enth, ...), custom_call_target="tpu_custom_call" | custom-call | flops 8192000 | bytes 7703040 | tf_op jit(solution)/shard_map/final/pallas_call | solution.py:534
Async XLA Ops:
  4.9 13.7 %collective-permute-start = (f32[40,256]{1,0:T(8,128)S(1)}, f32[40,256]{1,0:T(8,128)S(1)}, u32[]{:S(2)}, u32[]{:S(2)}) collective-permute-start(f32[40,256]{1,0:T(8,128)S(1)} %get-tuple-element.23.own), channel_id=1, source_target_pairs={{0,1},{1,0},{2,3},{3,2},{4,5},{5,4},{6,7},{7,6},{8,9},{9,8},{10,11... | collective-permute-start | bytes 122888 | tf_op jit(solution)/shard_map/ppermute | solution.py:601
  9.2 10.1 %collective-permute-start.1 = (f32[6,2,40,128]{3,2,1,0:T(8,128)S(1)}, f32[6,2,40,128]{3,2,1,0:T(8,128)S(1)}, u32[]{:S(2)}, u32[]{:S(2)}) collective-permute-start(f32[6,2,40,128]{3,2,1,0:T(8,128)S(1)} %get-tuple-element.26), channel_id=1, source_target_pairs={{0,16},{16,0},{32,48},{48,32},{64,80},{80,64},{96,112},{112,96},{1... | collective-permute-start | bytes 737288 | tf_op jit(solution)/shard_map/ppermute | solution.py:602
  10.2 9.1 %collective-permute-start.2 = (f32[6,2,40,128]{3,2,1,0:T(8,128)S(1)}, f32[6,2,40,128]{3,2,1,0:T(8,128)S(1)}, u32[]{:S(2)}, u32[]{:S(2)}) collective-permute-start(f32[6,2,40,128]{3,2,1,0:T(8,128)S(1)} %get-tuple-element.27), channel_id=1, source_target_pairs={{16,32},{32,16},{48,64},{64,48},{80,96},{96,80},{112,128},{128,112... | collective-permute-start | bytes 737288 | tf_op jit(solution)/shard_map/ppermute | solution.py:603
  11.7 7.6 %collective-permute-start.3 = (f32[6,32,128]{2,1,0:T(8,128)S(1)}, f32[6,32,128]{2,1,0:T(8,128)S(1)}, u32[]{:S(2)}, u32[]{:S(2)}) collective-permute-start(f32[6,32,128]{2,1,0:T(8,128)S(1)} %get-tuple-element.28), channel_id=1, source_target_pairs={{0,2},{2,0},{4,6},{6,4},{8,10},{10,8},{12,14},{14,12},{1,3},{3,1},... | collective-permute-start | bytes 294920 | tf_op jit(solution)/shard_map/ppermute | solution.py:604
  12.1 7.2 %collective-permute-start.4 = (f32[6,32,128]{2,1,0:T(8,128)S(1)}, f32[6,32,128]{2,1,0:T(8,128)S(1)}, u32[]{:S(2)}, u32[]{:S(2)}) collective-permute-start(f32[6,32,128]{2,1,0:T(8,128)S(1)} %get-tuple-element.29), channel_id=1, source_target_pairs={{2,4},{4,2},{6,8},{8,6},{10,12},{12,10},{14,0},{0,14},{3,5},{5,3},... | collective-permute-start | bytes 294920 | tf_op jit(solution)/shard_map/ppermute | solution.py:605

commit v6 on v5

--- a/solution.py
+++ b/solution.py
@@ -51,7 +51,7 @@
     rows, tiles, depth, total_depth, step_rows,
     prim_far, psi_far, height_far, shock_far, by_height_far, by_slope_far, flags_far,
     packet, su_a, su_b, sv_a, sv_b, normal, flux, enth, tone, inverse, prim, psi,
-    turn, facts, tops, spread, work, height, shock, by_height, by_slope, flags, small, large,
+    turn, facts, tops, feet, spread, work, height, shock, by_height, by_slope, flags, small, large,
 ):
     surfaces = [
         pltpu.make_async_copy(far, near, small.at[n])
@@ -99,29 +99,8 @@
 
     turn[...] = jnp.zeros_like(turn)
     tops[...] = jnp.zeros_like(tops)
+    feet[...] = jnp.zeros_like(feet)
     packet[...] = jnp.zeros_like(packet)
-    for copy in surfaces:
-        copy.wait()
-    for place, array in enumerate(
-        [height[...]]
-        + [shock[q] for q in range(5)]
-        + [flags[...].astype(f32)]
-    ):
-        turn[0, rows * place : rows * place + rows, 0:columns] = array
-    for q in range(5):
-        turn[1, rows * q : rows * q + rows, 0:columns] = by_height[q]
-        turn[2, rows * q : rows * q + rows, 0:columns] = by_slope[q]
-    for n in range(3):
-        facts[n] = turn[n].T
-    for span in spans:
-        inverse[span, :] = jnp.where(
-            lane < rows, 1.0 / jnp.where(lane < rows, facts[0, span, :], 1.0), 0.0
-        )
-    for span in spans:
-        inv_height = inverse[span, :]
-        for i in range(rows):
-            spread[i, span, :] = spread_lane(inv_height, i)
-
     for c in range(chunks):
         for copy in loads[c]:
             copy.wait()
@@ -135,6 +114,28 @@
                     flux[q, i, span, :] = value
                 enth[i, span, :] = enthalpy
                 tone[i, span, :] = jnp.sqrt(gamma_ratio * ratio)
+        if c == 0:
+            for copy in surfaces:
+                copy.wait()
+            for place, array in enumerate(
+                [height[...]]
+                + [shock[q] for q in range(5)]
+                + [flags[...].astype(f32)]
+            ):
+                turn[0, rows * place : rows * place + rows, 0:columns] = array
+            for q in range(5):
+                turn[1, rows * q : rows * q + rows, 0:columns] = by_height[q]
+                turn[2, rows * q : rows * q + rows, 0:columns] = by_slope[q]
+            for n in range(3):
+                facts[n] = turn[n].T
+            for span in spans:
+                inverse[span, :] = jnp.where(
+                    lane < rows, 1.0 / jnp.where(lane < rows, facts[0, span, :], 1.0), 0.0
+                )
+            for span in spans:
+                inv_height = inverse[span, :]
+                for i in range(rows):
+                    spread[i, span, :] = spread_lane(inv_height, i)
         for i in mine:
             for span in spans:
                 inv = spread[i, span, :]
@@ -148,25 +149,24 @@
                     total = term if total is None else total + term
                 work[i, span, :] = total
         for span in spans:
-            for half, ref in ((0, psi), (1, flux)):
-                packed = packet[span, 128 * half : 128 * half + 128]
-                for q in range(5):
-                    for i in mine:
-                        spot = rows * q + i
-                        moved = pltpu.roll(ref[q, i, span, :], spot + extra, 1)
-                        packed = jnp.where(lane == spot, moved, packed)
-                packet[span, 128 * half : 128 * half + 128] = packed
-
-    @pl.when(jnp.logical_not(first))
-    def _():
-        for span in spans:
-            packed = jnp.zeros((8, 128), f32)
-            for q in range(5):
-                for i in range(rows):
+            high, low = tops[span, :], feet[span, :]
+            packed = packet[span, 128:256]
+            for q in range(5):
+                for i in mine:
                     spot = rows * q + i
                     moved = pltpu.roll(psi[q, i, span, :], spot + 1, 1)
+                    high = jnp.where(lane == spot, moved, high)
+                    low = jnp.where(lane == spot + 1, moved, low)
+                    moved = pltpu.roll(flux[q, i, span, :], spot + extra, 1)
                     packed = jnp.where(lane == spot, moved, packed)
-            tops[span, :] = packed
+            tops[span, :] = high
+            feet[span, :] = low
+            packet[span, 128:256] = packed
+
+    for span in spans:
+        packet[span, 0:128] = jnp.where(
+            first, tops[span, :], pltpu.roll(feet[span, :], 127, 1)
+        )
 
     for span in spans:
         gathered = jnp.zeros((8, 128), f32)
@@ -576,6 +576,7 @@
             VMEM((3, 128, 128), f32),
             VMEM((3, 128, 128), f32),
             VMEM((columns, 128), f32),
+            VMEM((columns, 128), f32),
             VMEM((rows, columns, depth), f32),
             VMEM((rows, columns, depth), f32),
             VMEM((rows, columns), f32),

time: 38.3 us -> 38 us (level)
  starting transfers between devices: 10.4 us -> 9.98 us
    ppermute x1, starting transfers between devices: 4.3 us -> 3.83 us  [local(): arrived = lax.ppermute(packet, 'nrm', [(0, 1), (1, 0)])]
where the time goes in v6:
time: 38 us; the launch traced here: 37.9 us
  blocking collectives  15.8 us (42%)
  Pallas kernels  11.4 us (30%)
  starting transfers between devices  9.98 us (26%)
  between operations  0.7 us (2%)
    all_to_all x1, blocking collectives, local(): chunks = lax.all_to_all(chunk, 'su', 0, 0)  15.8 us
    pallas_call x4, Pallas kernels, call(): pl.pallas_call(kernel, out_shape=outs, in_specs=[spec(n) for n in range(l...  11.4 us
    ppermute x1, starting transfers between devices, local(): arrived = lax.ppermute(packet, 'nrm', [(0, 1), (1, 0)])  3.83 us
    ppermute x1, starting transfers between devices, local(): sv_b = lax.ppermute(sv_b, 'sv', pairs(sv_count, 1))  3.26 us
    ppermute x1, starting transfers between devices, local(): su_b = lax.ppermute(su_b, 'su', pairs(su_count, 1))  1.53 us
    ppermute x1, starting transfers between devices, local(): su_a = lax.ppermute(su_a, 'su', pairs(su_count, 0))  0.96 us
  transfers between devices with their start and end apart: 5, of which 0 were waited for; matrix products, arithmetic and copies ran while one was open for 0% of the time, Pallas kernels for 10%

profile of v6, /device:TPU:1, one launch (start us, length us, event | category | flops | bytes accessed | tf_op | source)
XLA Modules:
  0.0 37.9 jit_solution(16126931060231660228)
XLA Ops:
  0.6 4.5 %prepare.1 = (f32[40,256]{1,0:T(8,128)S(1)}, f32[6,2,40,128]{3,2,1,0:T(8,128)S(1)}, f32[6,2,40,128]{3,2,1,0:T(8,128)S(1)}, f32[6,32,128]{2,1,0:T(8,128)S(1)}, f3...) custom-call(f32[5,16,40,128]{3,2,1,0:T(8,128)} %prim_far.1, ...), custom_call_target="tpu_custom_call" | custom-call | flops 4915200 | bytes 11278848 | tf_op jit(solution)/shard_map/prepare/pallas_call | solution.py:534
  5.1 3.8 %collective-permute-start = (f32[40,256]{1,0:T(8,128)S(1)}, f32[40,256]{1,0:T(8,128)S(1)}, u32[]{:S(2)}, u32[]{:S(2)}) collective-permute-start(f32[40,256]{1,0:T(8,128)S(1)} %get-tuple-element.23.own), channel_id=1, source_target_pairs={{0,1},{1,0},{2,3},{3,2},{4,5},{5,4},{6,7},{7,6},{8,9},{9,8},{10,11... | collective-permute-start | bytes 122888 | tf_op jit(solution)/shard_map/ppermute | solution.py:602
  8.9 1.0 %collective-permute-start.1 = (f32[6,2,40,128]{3,2,1,0:T(8,128)S(1)}, f32[6,2,40,128]{3,2,1,0:T(8,128)S(1)}, u32[]{:S(2)}, u32[]{:S(2)}) collective-permute-start(f32[6,2,40,128]{3,2,1,0:T(8,128)S(1)} %get-tuple-element.26), channel_id=1, source_target_pairs={{0,16},{16,0},{32,48},{48,32},{64,80},{80,64},{96,112},{112,96},{1... | collective-permute-start | bytes 737288 | tf_op jit(solution)/shard_map/ppermute | solution.py:603
  9.9 1.5 %collective-permute-start.2 = (f32[6,2,40,128]{3,2,1,0:T(8,128)S(1)}, f32[6,2,40,128]{3,2,1,0:T(8,128)S(1)}, u32[]{:S(2)}, u32[]{:S(2)}) collective-permute-start(f32[6,2,40,128]{3,2,1,0:T(8,128)S(1)} %get-tuple-element.27), channel_id=1, source_target_pairs={{16,32},{32,16},{48,64},{64,48},{80,96},{96,80},{112,128},{128,112... | collective-permute-start | bytes 737288 | tf_op jit(solution)/shard_map/ppermute | solution.py:604
  11.4 0.4 %collective-permute-start.3 = (f32[6,32,128]{2,1,0:T(8,128)S(1)}, f32[6,32,128]{2,1,0:T(8,128)S(1)}, u32[]{:S(2)}, u32[]{:S(2)}) collective-permute-start(f32[6,32,128]{2,1,0:T(8,128)S(1)} %get-tuple-element.28), channel_id=1, source_target_pairs={{0,2},{2,0},{4,6},{6,4},{8,10},{10,8},{12,14},{14,12},{1,3},{3,1},... | collective-permute-start | bytes 294920 | tf_op jit(solution)/shard_map/ppermute | solution.py:605
  11.8 3.3 %collective-permute-start.4 = (f32[6,32,128]{2,1,0:T(8,128)S(1)}, f32[6,32,128]{2,1,0:T(8,128)S(1)}, u32[]{:S(2)}, u32[]{:S(2)}) collective-permute-start(f32[6,32,128]{2,1,0:T(8,128)S(1)} %get-tuple-element.29), channel_id=1, source_target_pairs={{2,4},{4,2},{6,8},{8,6},{10,12},{12,10},{14,0},{0,14},{3,5},{5,3},... | collective-permute-start | bytes 294920 | tf_op jit(solution)/shard_map/ppermute | solution.py:606
  15.1 3.3 %interior.1.base = f32[5,16,40,128]{3,2,1,0:T(8,128)S(1)} custom-call(f32[5,16,40,128]{3,2,1,0:T(8,128)S(1)} %get-tuple-element.22.prim, f32[5,16,40,128]{3,2,1,0:T(8,128)S(1)} %get-tuple-element.30.psi, f32[5,16,40,128]{3,2,1,0:T(8,128)} %target_far.1, f32[5,16,40,128]{3,2,1,0:T(8,128)S(1)} %get-tuple-element.31.normal, ...), custom_call_target="tpu_custom_call" | custom-call | flops 2048000000 | bytes 8847360 | tf_op jit(solution)/shard_map/interior/pallas_call | solution.py:534
  18.4 0.0 collective-permute-done.arrived
  18.4 0.6 %join.1 = (f32[16,8,128]{2,1,0:T(8,128)S(1)}, f32[8,128]{1,0:T(8,128)S(1)}) custom-call(f32[40,256]{1,0:T(8,128)S(1)} %get-tuple-element.23.own, f32[40,256]{1,0:T(8,128)S(1)} %collective-permute-done.arrived, f32[40,128]{1,0:T(8,128)S(1)} %get-tuple-element.24.inverse), custom_call_target="tpu_custom_call" | custom-call | flops 2048000000 | bytes 172032 | tf_op jit(solution)/shard_map/join/pallas_call | solution.py:534
  19.0 0.0 collective-permute-done.3.sv_a
  19.0 0.0 collective-permute-done.4.sv_b
  19.0 0.0 collective-permute-done.1.su_a
  19.0 0.0 collective-permute-done.2.su_b
  19.0 15.8 %all_to_all.5.chunks = f32[16,8,128]{2,1,0:T(8,128)S(1)} all-to-all(f32[16,8,128]{2,1,0:T(8,128)S(1)} %get-tuple-element.41), channel_id=1, replica_groups=mesh['su'=16,'sv'=8,'nrm'=2] {'su'}, dimensions={0} | all-to-all | bytes 131072 | tf_op jit(solution)/shard_map/all_to_all | solution.py:636
  34.8 3.1 %final.1 = (f32[5,16,40,128]{3,2,1,0:T(8,128)}, f32[16,40]{1,0:T(8,128)}) custom-call(f32[5,16,40,128]{3,2,1,0:T(8,128)S(1)} %get-tuple-element.22.prim, f32[5,16,40,128]{3,2,1,0:T(8,128)S(1)} %interior.1.base, f32[5,16,40,128]{3,2,1,0:T(8,128)S(1)} %get-tuple-element.35.flux, f32[16,40,128]{2,1,0:T(8,128)S(1)} %get-tuple-element.32.enth, ...), custom_call_target="tpu_custom_call" | custom-call | flops 8192000 | bytes 7703040 | tf_op jit(solution)/shard_map/final/pallas_call | solution.py:534
Async XLA Ops:
  5.1 13.3 %collective-permute-start = (f32[40,256]{1,0:T(8,128)S(1)}, f32[40,256]{1,0:T(8,128)S(1)}, u32[]{:S(2)}, u32[]{:S(2)}) collective-permute-start(f32[40,256]{1,0:T(8,128)S(1)} %get-tuple-element.23.own), channel_id=1, source_target_pairs={{0,1},{1,0},{2,3},{3,2},{4,5},{5,4},{6,7},{7,6},{8,9},{9,8},{10,11... | collective-permute-start | bytes 122888 | tf_op jit(solution)/shard_map/ppermute | solution.py:602
  8.9 10.1 %collective-permute-start.1 = (f32[6,2,40,128]{3,2,1,0:T(8,128)S(1)}, f32[6,2,40,128]{3,2,1,0:T(8,128)S(1)}, u32[]{:S(2)}, u32[]{:S(2)}) collective-permute-start(f32[6,2,40,128]{3,2,1,0:T(8,128)S(1)} %get-tuple-element.26), channel_id=1, source_target_pairs={{0,16},{16,0},{32,48},{48,32},{64,80},{80,64},{96,112},{112,96},{1... | collective-permute-start | bytes 737288 | tf_op jit(solution)/shard_map/ppermute | solution.py:603
  9.9 9.1 %collective-permute-start.2 = (f32[6,2,40,128]{3,2,1,0:T(8,128)S(1)}, f32[6,2,40,128]{3,2,1,0:T(8,128)S(1)}, u32[]{:S(2)}, u32[]{:S(2)}) collective-permute-start(f32[6,2,40,128]{3,2,1,0:T(8,128)S(1)} %get-tuple-element.27), channel_id=1, source_target_pairs={{16,32},{32,16},{48,64},{64,48},{80,96},{96,80},{112,128},{128,112... | collective-permute-start | bytes 737288 | tf_op jit(solution)/shard_map/ppermute | solution.py:604
  11.4 7.6 %collective-permute-start.3 = (f32[6,32,128]{2,1,0:T(8,128)S(1)}, f32[6,32,128]{2,1,0:T(8,128)S(1)}, u32[]{:S(2)}, u32[]{:S(2)}) collective-permute-start(f32[6,32,128]{2,1,0:T(8,128)S(1)} %get-tuple-element.28), channel_id=1, source_target_pairs={{0,2},{2,0},{4,6},{6,4},{8,10},{10,8},{12,14},{14,12},{1,3},{3,1},... | collective-permute-start | bytes 294920 | tf_op jit(solution)/shard_map/ppermute | solution.py:605
  11.8 7.2 %collective-permute-start.4 = (f32[6,32,128]{2,1,0:T(8,128)S(1)}, f32[6,32,128]{2,1,0:T(8,128)S(1)}, u32[]{:S(2)}, u32[]{:S(2)}) collective-permute-start(f32[6,32,128]{2,1,0:T(8,128)S(1)} %get-tuple-element.29), channel_id=1, source_target_pairs={{2,4},{4,2},{6,8},{8,6},{10,12},{12,10},{14,0},{0,14},{3,5},{5,3},... | collective-permute-start | bytes 294920 | tf_op jit(solution)/shard_map/ppermute | solution.py:606

commit v7 on v6

--- a/solution.py
+++ b/solution.py
@@ -13,7 +13,7 @@
 gm = gamma_ratio - 1.0
 f32 = jnp.float32
 VMEM = pltpu.VMEM
-JOIN_COST = 5_000
+JOIN_COST = 100
 INTERIOR_COST = 5_000
 
 
@@ -319,9 +319,6 @@
     for copy in loads:
         copy.start()
     for q in range(5):
-        for row in (0, 1, rows + 2, rows + 3):
-            wide[q, row] = jnp.zeros_like(wide[q, row])
-            along[q, row] = jnp.zeros_like(along[q, row])
         for i in range(rows):
             for low in (0, 8 + columns):
                 wide[q, i + 2, low : low + 8, :] = jnp.zeros((8, 128), f32)
@@ -338,8 +335,15 @@
             for q in range(5):
                 value = psi[q, i, span, :]
                 wide[q, i + 2, inner, :] = value
-                along[q, i + 2, span, :] = radius_u * value
+                along[q, i, span, :] = radius_u * value
                 across[q, i, inner, :] = radius_v * value
+
+    def pair(i, tap, k, sign):
+        if i < k:
+            return sign * tap(k)
+        if i + k >= rows:
+            return tap(-k)
+        return tap(-k) + tap(k) if sign > 0 else tap(-k) - tap(k)
 
     def fill(i):
         for t in range(tiles):
@@ -347,23 +351,18 @@
             at = lambda k: slice(8 * t + 8 + k, 8 * t + 16 + k)
             first, second, third, damp = [], [], [], []
             for q in range(5):
+                tap = lambda k: wide[q, i + 2 + k, at(0), :]
                 first.append(
-                    near_weight * (wide[q, i + 1, at(0), :] - wide[q, i + 3, at(0), :])
-                    - far_weight * (wide[q, i, at(0), :] - wide[q, i + 4, at(0), :])
+                    near_weight * pair(i, tap, 1, -1.0) - far_weight * pair(i, tap, 2, -1.0)
                 )
                 second.append(
                     near_weight * (wide[q, i + 2, at(-1), :] - wide[q, i + 2, at(1), :])
                     - far_weight * (wide[q, i + 2, at(-2), :] - wide[q, i + 2, at(2), :])
                 )
-                far = (
-                    along[q, i, span, :] + along[q, i + 4, span, :]
-                    + across[q, i, at(-2), :] + across[q, i, at(2), :]
-                )
-                near = (
-                    along[q, i + 1, span, :] + along[q, i + 3, span, :]
-                    + across[q, i, at(-1), :] + across[q, i, at(1), :]
-                )
-                here = along[q, i + 2, span, :] + across[q, i, at(0), :]
+                tap = lambda k: along[q, i + k, span, :]
+                far = pair(i, tap, 2, 1.0) + (across[q, i, at(-2), :] + across[q, i, at(2), :])
+                near = pair(i, tap, 1, 1.0) + (across[q, i, at(-1), :] + across[q, i, at(1), :])
+                here = along[q, i, span, :] + across[q, i, at(0), :]
                 damp.append(
                     damping_coef * far - (4.0 * damping_coef) * near + (6.0 * damping_coef) * here
                 )
@@ -377,7 +376,8 @@
 
     for c, copy in enumerate(loads):
         copy.wait()
-        pl.loop(c * step_rows, (c + 1) * step_rows, unroll=step_rows)(fill)
+        for i in range(c * step_rows, (c + 1) * step_rows):
+            fill(i)
 
 
 def final_kernel(
@@ -621,7 +621,7 @@
         (prim, psi, objective_grad, normal, enth, tone),
         [
             VMEM((5, rows + 4, columns + 16, depth), f32),
-            VMEM((5, rows + 4, columns, depth), f32),
+            VMEM((5, rows, columns, depth), f32),
             VMEM((5, rows, columns + 16, depth), f32),
             VMEM((5, rows, columns, depth), f32),
             pltpu.SemaphoreType.DMA((4,)),

time: 38 us -> 38 us (level)
    ppermute x1, starting transfers between devices: 0.96 us -> 3.33 us  [local(): su_a = lax.ppermute(su_a, 'su', pairs(su_count, 0))]
    ppermute x1, starting transfers between devices: 1.53 us -> 0.01 us  [local(): su_b = lax.ppermute(su_b, 'su', pairs(su_count, 1))]
    ppermute x1, starting transfers between devices: 3.83 us -> 2.8 us  [local(): arrived = lax.ppermute(packet, 'nrm', [(0, 1), (1, 0)])]
where the time goes in v7:
time: 38 us; the launch traced here: 37.8 us
  blocking collectives  16 us (42%)
  Pallas kernels  11.4 us (30%)
  starting transfers between devices  9.79 us (26%)
  between operations  0.7 us (2%)
    all_to_all x1, blocking collectives, local(): chunks = lax.all_to_all(chunk, 'su', 0, 0)  16 us
    pallas_call x4, Pallas kernels, call(): pl.pallas_call(kernel, out_shape=outs, in_specs=[spec(n) for n in range(l...  11.4 us
    ppermute x1, starting transfers between devices, local(): su_a = lax.ppermute(su_a, 'su', pairs(su_count, 0))  3.33 us
    ppermute x1, starting transfers between devices, local(): sv_b = lax.ppermute(sv_b, 'sv', pairs(sv_count, 1))  3.26 us
    ppermute x1, starting transfers between devices, local(): arrived = lax.ppermute(packet, 'nrm', [(0, 1), (1, 0)])  2.8 us
  transfers between devices with their start and end apart: 5, of which 0 were waited for; matrix products, arithmetic and copies ran while one was open for 0% of the time, Pallas kernels for 10%

profile of v7, /device:TPU:1, one launch (start us, length us, event | category | flops | bytes accessed | tf_op | source)
XLA Modules:
  0.0 37.8 jit_solution(1533051062005945939)
XLA Ops:
  0.6 4.5 %prepare.1 = (f32[40,256]{1,0:T(8,128)S(1)}, f32[6,2,40,128]{3,2,1,0:T(8,128)S(1)}, f32[6,2,40,128]{3,2,1,0:T(8,128)S(1)}, f32[6,32,128]{2,1,0:T(8,128)S(1)}, f3...) custom-call(f32[5,16,40,128]{3,2,1,0:T(8,128)} %prim_far.1, ...), custom_call_target="tpu_custom_call" | custom-call | flops 4915200 | bytes 11278848 | tf_op jit(solution)/shard_map/prepare/pallas_call | solution.py:534
  5.1 3.3 %collective-permute-start.1 = (f32[6,2,40,128]{3,2,1,0:T(8,128)S(1)}, f32[6,2,40,128]{3,2,1,0:T(8,128)S(1)}, u32[]{:S(2)}, u32[]{:S(2)}) collective-permute-start(f32[6,2,40,128]{3,2,1,0:T(8,128)S(1)} %get-tuple-element.26), channel_id=1, source_target_pairs={{0,16},{16,0},{32,48},{48,32},{64,80},{80,64},{96,112},{112,96},{1... | collective-permute-start | bytes 737288 | tf_op jit(solution)/shard_map/ppermute | solution.py:603
  8.4 0.0 collective-permute-start.2
  8.4 2.8 %collective-permute-start = (f32[40,256]{1,0:T(8,128)S(1)}, f32[40,256]{1,0:T(8,128)S(1)}, u32[]{:S(2)}, u32[]{:S(2)}) collective-permute-start(f32[40,256]{1,0:T(8,128)S(1)} %get-tuple-element.23.own), channel_id=1, source_target_pairs={{0,1},{1,0},{2,3},{3,2},{4,5},{5,4},{6,7},{7,6},{8,9},{9,8},{10,11... | collective-permute-start | bytes 122888 | tf_op jit(solution)/shard_map/ppermute | solution.py:602
  11.2 0.4 %collective-permute-start.3 = (f32[6,32,128]{2,1,0:T(8,128)S(1)}, f32[6,32,128]{2,1,0:T(8,128)S(1)}, u32[]{:S(2)}, u32[]{:S(2)}) collective-permute-start(f32[6,32,128]{2,1,0:T(8,128)S(1)} %get-tuple-element.28), channel_id=1, source_target_pairs={{0,2},{2,0},{4,6},{6,4},{8,10},{10,8},{12,14},{14,12},{1,3},{3,1},... | collective-permute-start | bytes 294920 | tf_op jit(solution)/shard_map/ppermute | solution.py:605
  11.6 3.3 %collective-permute-start.4 = (f32[6,32,128]{2,1,0:T(8,128)S(1)}, f32[6,32,128]{2,1,0:T(8,128)S(1)}, u32[]{:S(2)}, u32[]{:S(2)}) collective-permute-start(f32[6,32,128]{2,1,0:T(8,128)S(1)} %get-tuple-element.29), channel_id=1, source_target_pairs={{2,4},{4,2},{6,8},{8,6},{10,12},{12,10},{14,0},{0,14},{3,5},{5,3},... | collective-permute-start | bytes 294920 | tf_op jit(solution)/shard_map/ppermute | solution.py:606
  14.9 3.3 %interior.1.base = f32[5,16,40,128]{3,2,1,0:T(8,128)S(1)} custom-call(f32[5,16,40,128]{3,2,1,0:T(8,128)S(1)} %get-tuple-element.22.prim, f32[5,16,40,128]{3,2,1,0:T(8,128)S(1)} %get-tuple-element.30.psi, f32[5,16,40,128]{3,2,1,0:T(8,128)} %target_far.1, f32[5,16,40,128]{3,2,1,0:T(8,128)S(1)} %get-tuple-element.31.normal, ...), custom_call_target="tpu_custom_call" | custom-call | flops 2048000000 | bytes 8847360 | tf_op jit(solution)/shard_map/interior/pallas_call | solution.py:534
  18.2 0.0 collective-permute-done.arrived
  18.2 0.6 %join.1 = (f32[16,8,128]{2,1,0:T(8,128)S(1)}, f32[8,128]{1,0:T(8,128)S(1)}) custom-call(f32[40,256]{1,0:T(8,128)S(1)} %get-tuple-element.23.own, f32[40,256]{1,0:T(8,128)S(1)} %collective-permute-done.arrived, f32[40,128]{1,0:T(8,128)S(1)} %get-tuple-element.24.inverse), custom_call_target="tpu_custom_call" | custom-call | flops 40960000 | bytes 172032 | tf_op jit(solution)/shard_map/join/pallas_call | solution.py:534
  18.8 0.0 collective-permute-done.3.sv_a
  18.8 0.0 collective-permute-done.4.sv_b
  18.8 0.0 collective-permute-done.1.su_a
  18.8 0.0 collective-permute-done.2.su_b
  18.8 16.0 %all_to_all.5.chunks = f32[16,8,128]{2,1,0:T(8,128)S(1)} all-to-all(f32[16,8,128]{2,1,0:T(8,128)S(1)} %get-tuple-element.41), channel_id=1, replica_groups=mesh['su'=16,'sv'=8,'nrm'=2] {'su'}, dimensions={0} | all-to-all | bytes 131072 | tf_op jit(solution)/shard_map/all_to_all | solution.py:636
  34.8 3.1 %final.1 = (f32[5,16,40,128]{3,2,1,0:T(8,128)}, f32[16,40]{1,0:T(8,128)}) custom-call(f32[5,16,40,128]{3,2,1,0:T(8,128)S(1)} %get-tuple-element.22.prim, f32[5,16,40,128]{3,2,1,0:T(8,128)S(1)} %interior.1.base, f32[5,16,40,128]{3,2,1,0:T(8,128)S(1)} %get-tuple-element.35.flux, f32[16,40,128]{2,1,0:T(8,128)S(1)} %get-tuple-element.32.enth, ...), custom_call_target="tpu_custom_call" | custom-call | flops 8192000 | bytes 7703040 | tf_op jit(solution)/shard_map/final/pallas_call | solution.py:534
Async XLA Ops:
  5.1 13.7 %collective-permute-start.1 = (f32[6,2,40,128]{3,2,1,0:T(8,128)S(1)}, f32[6,2,40,128]{3,2,1,0:T(8,128)S(1)}, u32[]{:S(2)}, u32[]{:S(2)}) collective-permute-start(f32[6,2,40,128]{3,2,1,0:T(8,128)S(1)} %get-tuple-element.26), channel_id=1, source_target_pairs={{0,16},{16,0},{32,48},{48,32},{64,80},{80,64},{96,112},{112,96},{1... | collective-permute-start | bytes 737288 | tf_op jit(solution)/shard_map/ppermute | solution.py:603
  8.4 10.4 %collective-permute-start.2 = (f32[6,2,40,128]{3,2,1,0:T(8,128)S(1)}, f32[6,2,40,128]{3,2,1,0:T(8,128)S(1)}, u32[]{:S(2)}, u32[]{:S(2)}) collective-permute-start(f32[6,2,40,128]{3,2,1,0:T(8,128)S(1)} %get-tuple-element.27), channel_id=1, source_target_pairs={{16,32},{32,16},{48,64},{64,48},{80,96},{96,80},{112,128},{128,112... | collective-permute-start | bytes 737288 | tf_op jit(solution)/shard_map/ppermute | solution.py:604
  8.4 9.7 %collective-permute-start = (f32[40,256]{1,0:T(8,128)S(1)}, f32[40,256]{1,0:T(8,128)S(1)}, u32[]{:S(2)}, u32[]{:S(2)}) collective-permute-start(f32[40,256]{1,0:T(8,128)S(1)} %get-tuple-element.23.own), channel_id=1, source_target_pairs={{0,1},{1,0},{2,3},{3,2},{4,5},{5,4},{6,7},{7,6},{8,9},{9,8},{10,11... | collective-permute-start | bytes 122888 | tf_op jit(solution)/shard_map/ppermute | solution.py:602
  11.2 7.5 %collective-permute-start.3 = (f32[6,32,128]{2,1,0:T(8,128)S(1)}, f32[6,32,128]{2,1,0:T(8,128)S(1)}, u32[]{:S(2)}, u32[]{:S(2)}) collective-permute-start(f32[6,32,128]{2,1,0:T(8,128)S(1)} %get-tuple-element.28), channel_id=1, source_target_pairs={{0,2},{2,0},{4,6},{6,4},{8,10},{10,8},{12,14},{14,12},{1,3},{3,1},... | collective-permute-start | bytes 294920 | tf_op jit(solution)/shard_map/ppermute | solution.py:605
  11.6 7.1 %collective-permute-start.4 = (f32[6,32,128]{2,1,0:T(8,128)S(1)}, f32[6,32,128]{2,1,0:T(8,128)S(1)}, u32[]{:S(2)}, u32[]{:S(2)}) collective-permute-start(f32[6,32,128]{2,1,0:T(8,128)S(1)} %get-tuple-element.29), channel_id=1, source_target_pairs={{2,4},{4,2},{6,8},{8,6},{10,12},{12,10},{14,0},{0,14},{3,5},{5,3},... | collective-permute-start | bytes 294920 | tf_op jit(solution)/shard_map/ppermute | solution.py:606

commit v8 on v7

--- a/solution.py
+++ b/solution.py
@@ -557,7 +557,7 @@
     points = 5 * rows * columns * depth
 
     packet, su_a, su_b, sv_a, sv_b, normal, flux, enth, tone, inverse, prim, psi = call(
-        functools.partial(prepare_kernel, rows, tiles, depth, total_depth, rows // 4),
+        functools.partial(prepare_kernel, rows, tiles, depth, total_depth, rows // 8),
         [
             shape(columns, 256),
             shape(6, 2, columns, depth),
@@ -585,7 +585,7 @@
             VMEM((5, rows, columns), f32),
             VMEM((rows, columns), jnp.int32),
             pltpu.SemaphoreType.DMA((5,)),
-            pltpu.SemaphoreType.DMA((2, 4)),
+            pltpu.SemaphoreType.DMA((2, 8)),
         ],
         12 * points,
         "prepare",

time: 38 us -> 38.4 us (1.011)
  Pallas kernels: 11.4 us -> 11.8 us
    pallas_call x4, Pallas kernels: 11.4 us -> 11.8 us  [call(): pl.pallas_call(kernel, out_shape=outs, in_specs=[spec(n) for n in range(l...]
where the time goes in v8:
time: 38.4 us; the launch traced here: 38.3 us
  blocking collectives  16 us (42%)
  Pallas kernels  11.8 us (31%)
  starting transfers between devices  9.78 us (25%)
  between operations  0.7 us (2%)
    all_to_all x1, blocking collectives, local(): chunks = lax.all_to_all(chunk, 'su', 0, 0)  16 us
    pallas_call x4, Pallas kernels, call(): pl.pallas_call(kernel, out_shape=outs, in_specs=[spec(n) for n in range(l...  11.8 us
    ppermute x1, starting transfers between devices, local(): su_a = lax.ppermute(su_a, 'su', pairs(su_count, 0))  3.32 us
    ppermute x1, starting transfers between devices, local(): sv_b = lax.ppermute(sv_b, 'sv', pairs(sv_count, 1))  3.26 us
    ppermute x1, starting transfers between devices, local(): arrived = lax.ppermute(packet, 'nrm', [(0, 1), (1, 0)])  2.8 us
  transfers between devices with their start and end apart: 5, of which 0 were waited for; matrix products, arithmetic and copies ran while one was open for 0% of the time, Pallas kernels for 10%

profile of v8, /device:TPU:1, one launch (start us, length us, event | category | flops | bytes accessed | tf_op | source)
XLA Modules:
  0.0 38.3 jit_solution(1359505818015525048)
XLA Ops:
  0.6 4.9 %prepare.1 = (f32[40,256]{1,0:T(8,128)S(1)}, f32[6,2,40,128]{3,2,1,0:T(8,128)S(1)}, f32[6,2,40,128]{3,2,1,0:T(8,128)S(1)}, f32[6,32,128]{2,1,0:T(8,128)S(1)}, f3...) custom-call(f32[5,16,40,128]{3,2,1,0:T(8,128)} %prim_far.1, ...), custom_call_target="tpu_custom_call" | custom-call | flops 4915200 | bytes 11278848 | tf_op jit(solution)/shard_map/prepare/pallas_call | solution.py:534
  5.6 3.3 %collective-permute-start.1 = (f32[6,2,40,128]{3,2,1,0:T(8,128)S(1)}, f32[6,2,40,128]{3,2,1,0:T(8,128)S(1)}, u32[]{:S(2)}, u32[]{:S(2)}) collective-permute-start(f32[6,2,40,128]{3,2,1,0:T(8,128)S(1)} %get-tuple-element.26), channel_id=1, source_target_pairs={{0,16},{16,0},{32,48},{48,32},{64,80},{80,64},{96,112},{112,96},{1... | collective-permute-start | bytes 737288 | tf_op jit(solution)/shard_map/ppermute | solution.py:603
  8.9 0.0 collective-permute-start.2
  8.9 2.8 %collective-permute-start = (f32[40,256]{1,0:T(8,128)S(1)}, f32[40,256]{1,0:T(8,128)S(1)}, u32[]{:S(2)}, u32[]{:S(2)}) collective-permute-start(f32[40,256]{1,0:T(8,128)S(1)} %get-tuple-element.23.own), channel_id=1, source_target_pairs={{0,1},{1,0},{2,3},{3,2},{4,5},{5,4},{6,7},{7,6},{8,9},{9,8},{10,11... | collective-permute-start | bytes 122888 | tf_op jit(solution)/shard_map/ppermute | solution.py:602
  11.7 0.4 %collective-permute-start.3 = (f32[6,32,128]{2,1,0:T(8,128)S(1)}, f32[6,32,128]{2,1,0:T(8,128)S(1)}, u32[]{:S(2)}, u32[]{:S(2)}) collective-permute-start(f32[6,32,128]{2,1,0:T(8,128)S(1)} %get-tuple-element.28), channel_id=1, source_target_pairs={{0,2},{2,0},{4,6},{6,4},{8,10},{10,8},{12,14},{14,12},{1,3},{3,1},... | collective-permute-start | bytes 294920 | tf_op jit(solution)/shard_map/ppermute | solution.py:605
  12.1 3.3 %collective-permute-start.4 = (f32[6,32,128]{2,1,0:T(8,128)S(1)}, f32[6,32,128]{2,1,0:T(8,128)S(1)}, u32[]{:S(2)}, u32[]{:S(2)}) collective-permute-start(f32[6,32,128]{2,1,0:T(8,128)S(1)} %get-tuple-element.29), channel_id=1, source_target_pairs={{2,4},{4,2},{6,8},{8,6},{10,12},{12,10},{14,0},{0,14},{3,5},{5,3},... | collective-permute-start | bytes 294920 | tf_op jit(solution)/shard_map/ppermute | solution.py:606
  15.3 3.3 %interior.1.base = f32[5,16,40,128]{3,2,1,0:T(8,128)S(1)} custom-call(f32[5,16,40,128]{3,2,1,0:T(8,128)S(1)} %get-tuple-element.22.prim, f32[5,16,40,128]{3,2,1,0:T(8,128)S(1)} %get-tuple-element.30.psi, f32[5,16,40,128]{3,2,1,0:T(8,128)} %target_far.1, f32[5,16,40,128]{3,2,1,0:T(8,128)S(1)} %get-tuple-element.31.normal, ...), custom_call_target="tpu_custom_call" | custom-call | flops 2048000000 | bytes 8847360 | tf_op jit(solution)/shard_map/interior/pallas_call | solution.py:534
  18.6 0.0 collective-permute-done.arrived
  18.6 0.6 %join.1 = (f32[16,8,128]{2,1,0:T(8,128)S(1)}, f32[8,128]{1,0:T(8,128)S(1)}) custom-call(f32[40,256]{1,0:T(8,128)S(1)} %get-tuple-element.23.own, f32[40,256]{1,0:T(8,128)S(1)} %collective-permute-done.arrived, f32[40,128]{1,0:T(8,128)S(1)} %get-tuple-element.24.inverse), custom_call_target="tpu_custom_call" | custom-call | flops 40960000 | bytes 172032 | tf_op jit(solution)/shard_map/join/pallas_call | solution.py:534
  19.2 0.0 collective-permute-done.3.sv_a
  19.2 0.0 collective-permute-done.4.sv_b
  19.2 0.0 collective-permute-done.1.su_a
  19.2 0.0 collective-permute-done.2.su_b
  19.2 16.0 %all_to_all.5.chunks = f32[16,8,128]{2,1,0:T(8,128)S(1)} all-to-all(f32[16,8,128]{2,1,0:T(8,128)S(1)} %get-tuple-element.41), channel_id=1, replica_groups=mesh['su'=16,'sv'=8,'nrm'=2] {'su'}, dimensions={0} | all-to-all | bytes 131072 | tf_op jit(solution)/shard_map/all_to_all | solution.py:636
  35.2 3.1 %final.1 = (f32[5,16,40,128]{3,2,1,0:T(8,128)}, f32[16,40]{1,0:T(8,128)}) custom-call(f32[5,16,40,128]{3,2,1,0:T(8,128)S(1)} %get-tuple-element.22.prim, f32[5,16,40,128]{3,2,1,0:T(8,128)S(1)} %interior.1.base, f32[5,16,40,128]{3,2,1,0:T(8,128)S(1)} %get-tuple-element.35.flux, f32[16,40,128]{2,1,0:T(8,128)S(1)} %get-tuple-element.32.enth, ...), custom_call_target="tpu_custom_call" | custom-call | flops 8192000 | bytes 7703040 | tf_op jit(solution)/shard_map/final/pallas_call | solution.py:534
Async XLA Ops:
  5.6 13.7 %collective-permute-start.1 = (f32[6,2,40,128]{3,2,1,0:T(8,128)S(1)}, f32[6,2,40,128]{3,2,1,0:T(8,128)S(1)}, u32[]{:S(2)}, u32[]{:S(2)}) collective-permute-start(f32[6,2,40,128]{3,2,1,0:T(8,128)S(1)} %get-tuple-element.26), channel_id=1, source_target_pairs={{0,16},{16,0},{32,48},{48,32},{64,80},{80,64},{96,112},{112,96},{1... | collective-permute-start | bytes 737288 | tf_op jit(solution)/shard_map/ppermute | solution.py:603
  8.9 10.4 %collective-permute-start.2 = (f32[6,2,40,128]{3,2,1,0:T(8,128)S(1)}, f32[6,2,40,128]{3,2,1,0:T(8,128)S(1)}, u32[]{:S(2)}, u32[]{:S(2)}) collective-permute-start(f32[6,2,40,128]{3,2,1,0:T(8,128)S(1)} %get-tuple-element.27), channel_id=1, source_target_pairs={{16,32},{32,16},{48,64},{64,48},{80,96},{96,80},{112,128},{128,112... | collective-permute-start | bytes 737288 | tf_op jit(solution)/shard_map/ppermute | solution.py:604
  8.9 9.7 %collective-permute-start = (f32[40,256]{1,0:T(8,128)S(1)}, f32[40,256]{1,0:T(8,128)S(1)}, u32[]{:S(2)}, u32[]{:S(2)}) collective-permute-start(f32[40,256]{1,0:T(8,128)S(1)} %get-tuple-element.23.own), channel_id=1, source_target_pairs={{0,1},{1,0},{2,3},{3,2},{4,5},{5,4},{6,7},{7,6},{8,9},{9,8},{10,11... | collective-permute-start | bytes 122888 | tf_op jit(solution)/shard_map/ppermute | solution.py:602
  11.7 7.5 %collective-permute-start.3 = (f32[6,32,128]{2,1,0:T(8,128)S(1)}, f32[6,32,128]{2,1,0:T(8,128)S(1)}, u32[]{:S(2)}, u32[]{:S(2)}) collective-permute-start(f32[6,32,128]{2,1,0:T(8,128)S(1)} %get-tuple-element.28), channel_id=1, source_target_pairs={{0,2},{2,0},{4,6},{6,4},{8,10},{10,8},{12,14},{14,12},{1,3},{3,1},... | collective-permute-start | bytes 294920 | tf_op jit(solution)/shard_map/ppermute | solution.py:605
  12.1 7.1 %collective-permute-start.4 = (f32[6,32,128]{2,1,0:T(8,128)S(1)}, f32[6,32,128]{2,1,0:T(8,128)S(1)}, u32[]{:S(2)}, u32[]{:S(2)}) collective-permute-start(f32[6,32,128]{2,1,0:T(8,128)S(1)} %get-tuple-element.29), channel_id=1, source_target_pairs={{2,4},{4,2},{6,8},{8,6},{10,12},{12,10},{14,0},{0,14},{3,5},{5,3},... | collective-permute-start | bytes 294920 | tf_op jit(solution)/shard_map/ppermute | solution.py:606
